TPU v7x, 256 devices: a whole 4x4x8 slice. The times are simulated.
256 devices in a mesh: dp: 16 (over x, y), ctx: 16 (over z, core).
Axes of the slice: x: 4, y: 4, z: 8, core: 2. Of those that a mesh axis runs over, the one named last changes fastest.
Arguments:
- queries: bfloat16 [16, 4096, 1024], P('dp', 'ctx'), may hold values from -12 to 12
- keyvals: bfloat16 [16, 4096, 256], P('dp', 'ctx'), may hold values from -6 to 6
- dest_bin: int32 [16, 4096], P('dp', 'ctx'), may hold values from 0 to 15, as said below
- source_owner: int32 [16, 4096], P('dp', 'ctx'), may hold values from 0 to 15, as said below
- seq_lengths: int32 [16, 4], P('dp'), may hold values from 1 to 3072, 4096 in all within a row
Outputs:
- attended: bfloat16 [16, 4096, 1024], P('dp', 'ctx')
Inputs may be any that keep to these rules, and one draw needn't show every extreme that they name: In every block c and for every owner o and bin b, the positions of block c of owner o with dest_bin b are as many as the positions of block c of bin b with source_owner o, and at most 32; in every block some owner sends exactly 32 to some bin. `source_owner`: matches dest_bin as stated there.
All inputs are finite; a program needn't handle non-finite values.
Results may differ from a plain program's by a relative error of at most 0.0065.
Values may be sent and summed in bfloat16 or wider, within the bound.
No kernel may reach another device: no remote copies, remote signals or barrier semaphores. Data moves between devices by JAX's collectives and lax.ppermute only.
A program may use at most 128 MiB of HBM per device.

v0:
```python
import functools

import jax
import jax.numpy as jnp
from jax import lax
from jax.experimental import pallas as pl
from jax.experimental.pallas import tpu as pltpu
from jax.sharding import PartitionSpec as P


LOG2E = 1.4426950408889634
LOW = -1e30


def slots_of(labels, owners, capacity):
    n = labels.shape[1]
    hot = lax.broadcasted_iota(jnp.int32, (owners, n), 0) == labels
    hot16 = jnp.where(hot, 1.0, 0.0).astype(jnp.bfloat16)
    earlier = lax.broadcasted_iota(jnp.int32, (n, n), 0) < lax.broadcasted_iota(
        jnp.int32, (n, n), 1
    )
    earlier16 = jnp.where(earlier, 1.0, 0.0).astype(jnp.bfloat16)
    before = jnp.dot(hot16, earlier16, preferred_element_type=jnp.float32)
    rank = jnp.sum(jnp.where(hot, before, 0.0), axis=0, keepdims=True)
    return labels * capacity + rank.astype(jnp.int32)


def pack_kernel(owners, capacity, dest_ref, rows_ref, out_ref):
    slots = slots_of(dest_ref[...], owners, capacity)
    n = slots.shape[1]
    hot = lax.broadcasted_iota(jnp.int32, (owners * capacity, n), 0) == slots
    picks = jnp.where(hot, 1.0, 0.0).astype(jnp.bfloat16)
    out_ref[...] = jnp.dot(
        picks, rows_ref[...], preferred_element_type=jnp.float32
    ).astype(out_ref.dtype)


def picks_of(source_ref, owners, capacity):
    slots = slots_of(source_ref[...], owners, capacity)
    n = slots.shape[1]
    wide = jnp.broadcast_to(slots.astype(jnp.float32), (128, n))
    tall = jnp.transpose(wide).astype(jnp.int32)
    lane = lax.broadcasted_iota(jnp.int32, (n, 128), 1)
    parts = [
        jnp.where(tall == lane + 128 * i, 1.0, 0.0).astype(jnp.bfloat16)
        for i in range(owners * capacity // 128)
    ]
    return jnp.concatenate(parts, axis=1)


def picks_kernel(owners, capacity, source_ref, out_ref):
    out_ref[...] = picks_of(source_ref, owners, capacity)


def unpack_kernel(picks_ref, rows_ref, out_ref):
    out_ref[...] = jnp.dot(
        picks_ref[...], rows_ref[...], preferred_element_type=jnp.float32
    ).astype(out_ref.dtype)


def join_kernel(own_ref, other_ref, out_ref):
    n = own_ref.shape[0]
    core = lax.rem(lax.axis_index("ctx"), 2)
    out_ref[pl.ds(pl.multiple_of(core * n, n), n), :] = own_ref[...]
    out_ref[pl.ds(pl.multiple_of((1 - core) * n, n), n), :] = other_ref[...]


def attend_kernel(head, far, *refs):
    lengths_ref, picks_ref, got_ref = refs[:3]
    near = refs[3 : 3 + len(far)]
    out_ref, kv, q_all, acc, top, over = refs[3 + len(far) :]
    n = picks_ref.shape[0]
    groups = out_ref.shape[1] // head
    chunk = 2 * n
    me = lax.axis_index("ctx")
    chip = me // 2
    core = me - 2 * chip

    picks = picks_ref[...]
    for h in range(groups):
        exact = jnp.dot(
            picks, got_ref[:, h * head : (h + 1) * head], preferred_element_type=jnp.float32
        ) * (LOG2E * head ** (-0.5))
        high = exact.astype(jnp.bfloat16)
        q_all[:, 2 * h * head : (2 * h + 1) * head] = high
        rest = exact - high.astype(jnp.float32)
        q_all[:, (2 * h + 1) * head : (2 * h + 2) * head] = rest.astype(jnp.bfloat16)

    starts = [jnp.int32(0)]
    for i in range(lengths_ref.shape[1] - 1):
        starts.append(starts[-1] + lengths_ref[0, i])

    def start_of(position):
        found = jnp.zeros_like(position)
        for s in starts[1:]:
            found = jnp.where(position >= s, jnp.maximum(found, s), found)
        return found

    q_first = me * n
    q_pos = q_first + lax.broadcasted_iota(jnp.int32, (1, n), 1)
    q_start = start_of(q_pos)
    low = start_of(q_first)
    high = start_of(q_first + n - 1)

    def distance(i):
        d = jnp.int32(0)
        for j, (a, b) in enumerate(far):
            d = jnp.where(i == j, jnp.where(core == 0, a, b), d)
        return d

    for i, (ref, (a, b)) in enumerate(zip(near, far)):
        at = (chip - jnp.where(core == 0, a, b)) * chunk

        @pl.when((at >= 0) & (at + chunk > low))
        def _():
            kv[i, :, :head] = ref[:, :head]
            kv[i, :, head:] = ref[:, head:]

    def tree_max(s):
        while s.shape[0] > 8:
            half = s.shape[0] // 2
            s = jnp.maximum(s[:half], s[half:])
        return jnp.max(s, axis=0, keepdims=True)

    def step(i, at, masked, mode):
        keys = jnp.concatenate([kv[i, :, :head]] * 2, axis=1)
        values = jnp.concatenate(
            [jnp.transpose(kv[i, :, head:]), jnp.ones((16, chunk), jnp.bfloat16)], axis=0
        )
        if masked:
            k_pos = at + lax.broadcasted_iota(jnp.int32, (chunk, n), 0)
            visible = (k_pos <= q_pos) & (k_pos >= q_start)

        def qk(h):
            s = lax.dot_general(
                keys,
                q_all[:, 2 * h * head : 2 * (h + 1) * head],
                (((1,), (1,)), ((), ())),
                preferred_element_type=jnp.float32,
            )
            return jnp.where(visible, s, LOW) if masked else s

        def soft(h, s):
            if mode == "fast":
                e = s - top[h]
                over[...] = jnp.maximum(over[...], tree_max(e))
                return jnp.exp2(e).astype(jnp.bfloat16), None
            if mode == "first":
                m = tree_max(s)
                top[h] = m
                return jnp.exp2(s - m).astype(jnp.bfloat16), None
            old = top[h]
            m = jnp.maximum(old, tree_max(s))
            top[h] = m
            return jnp.exp2(s - m).astype(jnp.bfloat16), jnp.exp2(old - m)

        def pv(h, w, fade):
            part = jnp.dot(values, w, preferred_element_type=jnp.float32)
            if mode == "fast":
                acc[h] += part
            elif mode == "first":
                acc[h] = part
            else:
                acc[h] = acc[h] * fade + part

        lag = 2
        s_of, w_of = {}, {}
        for t in range(groups + 1 + lag):
            if t < groups:
                s_of[t] = qk(t)
            if 0 <= t - 1 < groups:
                w_of[t - 1] = soft(t - 1, s_of.pop(t - 1))
            if 0 <= t - 1 - lag < groups:
                pv(t - 1 - lag, *w_of.pop(t - 1 - lag))

    def here(at):
        return (at >= 0) & (at + chunk > low)

    over[...] = jnp.full((1, n), LOW, jnp.float32)
    step(0, chip * chunk, True, "first")

    @pl.loop(1, len(far))
    def _(i):
        at = (chip - distance(i)) * chunk
        clear = (at >= high) & (at + chunk <= q_first)

        @pl.when(here(at) & clear)
        def _():
            step(i, at, False, "fast")

        @pl.when(here(at) & jnp.logical_not(clear))
        def _():
            step(i, at, True, "fast")

    @pl.when(jnp.max(over[...]) > 64.0)
    def _():
        for h in range(groups):
            top[h] = jnp.full((1, n), LOW, jnp.float32)
            acc[h] = jnp.zeros(acc.shape[1:], jnp.float32)

        @pl.loop(0, len(far))
        def _(i):
            at = (chip - distance(i)) * chunk

            @pl.when(here(at))
            def _():
                step(i, at, True, "slow")

    for h in range(groups):
        done = (acc[h, :head] * (1.0 / acc[h, head : head + 1])).astype(out_ref.dtype)
        out_ref[:, h * head : (h + 1) * head] = jnp.transpose(done)


def vmem(count):
    return [pl.BlockSpec(memory_space=pltpu.VMEM)] * count


def body(queries, keyvals, dest_bin, source_owner, seq_lengths):
    owners = lax.axis_size("dp")
    n_ctx = lax.axis_size("ctx")
    n = queries.shape[1]
    width = queries.shape[2]
    kv_width = keyvals.shape[2]
    head = kv_width // 2
    capacity = 2 * n // owners
    slots = owners * capacity

    def pack(rows):
        return pl.pallas_call(
            functools.partial(pack_kernel, owners, capacity),
            out_shape=jax.ShapeDtypeStruct((slots, rows.shape[1]), rows.dtype),
            in_specs=vmem(2),
            out_specs=vmem(1)[0],
            cost_estimate=pl.CostEstimate(
                flops=2 * slots * n * rows.shape[1],
                bytes_accessed=6 * n * rows.shape[1],
                transcendentals=0,
            ),
        )(dest_bin, rows)

    def exchange(rows):
        return lax.all_to_all(
            rows.reshape(owners, capacity, rows.shape[1]),
            "dp",
            split_axis=0,
            concat_axis=0,
            tiled=True,
        ).reshape(slots, rows.shape[1])

    got_kv = exchange(pack(keyvals[0]))
    got_q = exchange(pack(queries[0]))
    picks = pl.pallas_call(
        functools.partial(picks_kernel, owners, capacity),
        out_shape=jax.ShapeDtypeStruct((n, slots), keyvals.dtype),
        in_specs=vmem(1),
        out_specs=vmem(1)[0],
        compiler_params=pltpu.CompilerParams(vmem_limit_bytes=4 << 20),
        cost_estimate=pl.CostEstimate(
            flops=2 * n * n * owners, bytes_accessed=2 * n * slots, transcendentals=0
        ),
    )(source_owner)
    own = pl.pallas_call(
        unpack_kernel,
        out_shape=jax.ShapeDtypeStruct((n, kv_width), keyvals.dtype),
        in_specs=vmem(2),
        out_specs=vmem(1)[0],
        compiler_params=pltpu.CompilerParams(vmem_limit_bytes=12 << 20),
        cost_estimate=pl.CostEstimate(
            flops=2 * slots * n * kv_width, bytes_accessed=6 * n * kv_width, transcendentals=0
        ),
    )(picks, got_kv)

    def hop(x, up, down):
        return lax.ppermute(
            x,
            "ctx",
            [(c, (c + (2 * up if c % 2 == 0 else -2 * down)) % n_ctx) for c in range(n_ctx)],
        )

    def swap(x):
        return lax.ppermute(x, "ctx", [(c, c ^ 1) for c in range(n_ctx)])

    pair = pl.pallas_call(
        join_kernel,
        out_shape=jax.ShapeDtypeStruct((2 * n, kv_width), keyvals.dtype),
        in_specs=vmem(2),
        out_specs=vmem(1)[0],
        compiler_params=pltpu.CompilerParams(vmem_limit_bytes=4 << 20),
        cost_estimate=pl.CostEstimate(
            flops=0, bytes_accessed=8 * n * kv_width, transcendentals=0
        ),
    )(own, swap(own))
    hop1 = hop(pair, 1, 2)
    hop2 = hop(hop1, 1, 1)
    hop3 = hop(hop1, 2, 2)
    far = [(0, 0), (1, 6), (6, 1), (2, 5), (5, 2), (3, 4), (4, 3)]
    pieces = [pair, hop1, swap(hop1), hop2, swap(hop2), hop3, swap(hop3)]
    groups = width // head

    attended = pl.pallas_call(
        functools.partial(attend_kernel, head, far),
        out_shape=jax.ShapeDtypeStruct((n, width), queries.dtype),
        in_specs=[pl.BlockSpec(memory_space=pltpu.SMEM)] + vmem(2 + len(far)),
        out_specs=vmem(1)[0],
        scratch_shapes=[
            pltpu.VMEM((len(far), 2 * n, kv_width), keyvals.dtype),
            pltpu.VMEM((n, 2 * width), queries.dtype),
            pltpu.VMEM((groups, head + 16, n), jnp.float32),
            pltpu.VMEM((groups, 1, n), jnp.float32),
            pltpu.VMEM((1, n), jnp.float32),
        ],
        compiler_params=pltpu.CompilerParams(vmem_limit_bytes=24 << 20),
        cost_estimate=pl.CostEstimate(
            flops=4 * n * width * 12 * n,
            bytes_accessed=8 * n * width,
            transcendentals=12 * n * n * groups,
        ),
    )(seq_lengths, picks, got_q, *pieces)
    return attended.reshape(1, n, width)


def solution(mesh):
    return jax.shard_map(
        body,
        mesh=mesh,
        in_specs=(
            P("dp", "ctx", None),
            P("dp", "ctx", None),
            P("dp", "ctx"),
            P("dp", "ctx"),
            P("dp", None),
        ),
        out_specs=P("dp", "ctx", None),
        check_vma=False,
    )
```

profile of v0, /device:TPU:205, one launch (start us, length us, event | category | flops | bytes accessed | tf_op | source)
XLA Modules:
  0.0 59.7 jit_solution(7339222717481214816)
XLA Ops:
  0.0 2.0 %shard_map.57 = bf16[512,256]{1,0:T(8,128)(2,1)} custom-call(s32[1,256]{1,0:T(1,128)} %dest_ref.3, bf16[256,256]{1,0:T(8,128)(2,1)} %bitcast.12), custom_call_target="tpu_custom_call" | custom-call | flops 67108864 | bytes 393216 | tf_op jit(solution)/shard_map/pallas_call | solution.py:229
  2.0 6.8 %all-to-all-start.1 = ((bf16[16,32,256]{2,1,0:T(8,128)(2,1)}), bf16[16,32,256]{2,1,0:T(8,128)(2,1)S(1)}, u32[]{:S(2)}, u32[]{:S(2)}) async-start(bf16[16,32,256]{2,1,0:T(8,128)(2,1)} %bitcast.10), calls=%async_computation.1 | async-start | bytes 524288 | tf_op jit(solution)/shard_map/all_to_all | solution.py:242
  8.8 2.6 %shard_map.56 = bf16[512,1024]{1,0:T(8,128)(2,1)} custom-call(s32[1,256]{1,0:T(1,128)} %dest_ref.3, bf16[256,1024]{1,0:T(8,128)(2,1)} %bitcast.11), custom_call_target="tpu_custom_call" | custom-call | flops 268435456 | bytes 1572864 | tf_op jit(solution)/shard_map/pallas_call | solution.py:229
  11.4 2.0 %all-to-all-done.1 = bf16[16,32,256]{2,1,0:T(8,128)(2,1)S(1)} async-done(((bf16[16,32,256]{2,1,0:T(8,128)(2,1)}), bf16[16,32,256]{2,1,0:T(8,128)(2,1)S(1)}, u32[]{:S(2)}, u32[]{:S(2)}) %all-to-all-start.1) | async-done | bytes 262176 | tf_op jit(solution)/shard_map/all_to_all | solution.py:242
  13.4 0.0 copy-start
  13.4 6.5 %all-to-all-start = ((bf16[16,32,1024]{2,1,0:T(8,128)(2,1)}), bf16[16,32,1024]{2,1,0:T(8,128)(2,1)S(1)}, u32[]{:S(2)}, u32[]{:S(2)}) async-start(bf16[16,32,1024]{2,1,0:T(8,128)(2,1)} %bitcast.9), calls=%async_computation | async-start | bytes 2097152 | tf_op jit(solution)/shard_map/all_to_all | solution.py:242
  20.0 0.0 copy-done
  20.0 0.3 shard_map.55.picks_ref.refs_1_
  20.3 0.2 shard_map.58.own_ref
  20.5 2.4 %collective-permute-start = (bf16[256,256]{1,0:T(8,128)(2,1)S(1)}, bf16[256,256]{1,0:T(8,128)(2,1)S(1)}, u32[]{:S(2)}, u32[]{:S(2)}) collective-permute-start(bf16[256,256]{1,0:T(8,128)(2,1)S(1)} %shard_map.58.own_ref), channel_id=1, source_target_pairs={{0,1},{1,0},{2,3},{3,2},{4,5},{5,4},{6,7},{7,6},{8,9},{9,8},{10,11... | collective-permute-start | bytes 393224 | tf_op jit(solution)/shard_map/ppermute | solution.py:281
  22.9 1.0 %collective-permute-done.other_ref = bf16[256,256]{1,0:T(8,128)(2,1)S(1)} collective-permute-done((bf16[256,256]{1,0:T(8,128)(2,1)S(1)}, bf16[256,256]{1,0:T(8,128)(2,1)S(1)}, u32[]{:S(2)}, u32[]{:S(2)}) %collective-permute-start) | collective-permute-done | bytes 131104 | tf_op jit(solution)/shard_map/ppermute | solution.py:281
  23.9 0.0 copy-start.1
  24.0 1.2 %collective-permute-start.1 = (bf16[512,256]{1,0:T(8,128)(2,1)S(1)}, bf16[512,256]{1,0:T(8,128)(2,1)S(1)}, u32[]{:S(2)}, u32[]{:S(2)}) collective-permute-start(bf16[512,256]{1,0:T(8,128)(2,1)S(1)} %shard_map.59.refs_3_), channel_id=1, source_target_pairs={{0,2},{1,13},{2,4},{3,15},{4,6},{5,1},{6,8},{7,3},{8,10},{9,5},{10... | collective-permute-start | bytes 786440 | tf_op jit(solution)/shard_map/ppermute | solution.py:274
  25.2 9.1 %collective-permute-done.1.refs_4_ = bf16[512,256]{1,0:T(8,128)(2,1)S(1)} collective-permute-done((bf16[512,256]{1,0:T(8,128)(2,1)S(1)}, bf16[512,256]{1,0:T(8,128)(2,1)S(1)}, u32[]{:S(2)}, u32[]{:S(2)}) %collective-permute-start.1) | collective-permute-done | bytes 262176 | tf_op jit(solution)/shard_map/ppermute | solution.py:274
  34.3 0.0 collective-permute-start.3
  34.3 0.1 collective-permute-start.5
  34.4 0.0 collective-permute-start.2
  34.4 5.4 %collective-permute-done.3.refs_6_ = bf16[512,256]{1,0:T(8,128)(2,1)S(1)} collective-permute-done((bf16[512,256]{1,0:T(8,128)(2,1)S(1)}, bf16[512,256]{1,0:T(8,128)(2,1)S(1)}, u32[]{:S(2)}, u32[]{:S(2)}) %collective-permute-start.3) | collective-permute-done | bytes 262176 | tf_op jit(solution)/shard_map/ppermute | solution.py:274
  39.8 0.0 collective-permute-start.4
  39.8 5.5 %collective-permute-done.5.refs_8_ = bf16[512,256]{1,0:T(8,128)(2,1)S(1)} collective-permute-done((bf16[512,256]{1,0:T(8,128)(2,1)S(1)}, bf16[512,256]{1,0:T(8,128)(2,1)S(1)}, u32[]{:S(2)}, u32[]{:S(2)}) %collective-permute-start.5) | collective-permute-done | bytes 262176 | tf_op jit(solution)/shard_map/ppermute | solution.py:274
  45.4 0.0 collective-permute-start.6
  45.4 0.0 collective-permute-done.2.refs_5_
  45.4 0.0 all-to-all-done
  45.4 0.0 collective-permute-done.4.refs_7_
  45.4 1.5 %collective-permute-done.6.refs_9_ = bf16[512,256]{1,0:T(8,128)(2,1)S(1)} collective-permute-done((bf16[512,256]{1,0:T(8,128)(2,1)S(1)}, bf16[512,256]{1,0:T(8,128)(2,1)S(1)}, u32[]{:S(2)}, u32[]{:S(2)}) %collective-permute-start.6) | collective-permute-done | bytes 262176 | tf_op jit(solution)/shard_map/ppermute | solution.py:281
  46.9 0.0 copy-done.1
  46.9 12.8 %shard_map.60 = bf16[256,1024]{1,0:T(8,128)(2,1)} custom-call(s32[1,4]{1,0:T(1,128)S(1)} %copy-done.1, bf16[256,512]{1,0:T(8,128)(2,1)S(1)} %shard_map.55.picks_ref.refs_1_, bf16[512,1024]{1,0:T(8,128)(2,1)S(1)} %bitcast.7, bf16[512,256]{1,0:T(8,128)(2,1)S(1)} %shard_map.59.refs_3_, bf16[512,256]{1,0:T(8,128)(2,1)S(1)} %collective-permute-done.1.refs_4_, ...), custom_call_target="tpu_custom_call" | custom-call | flops 3221225472 | bytes 2097152 | tf_op jit(solution)/shard_map/pallas_call | solution.py:300
  (1 shorter events, 0.0 us)
Async XLA Ops:
  2.0 11.4 %all-to-all-start.1 = ((bf16[16,32,256]{2,1,0:T(8,128)(2,1)}), bf16[16,32,256]{2,1,0:T(8,128)(2,1)S(1)}, u32[]{:S(2)}, u32[]{:S(2)}) async-start(bf16[16,32,256]{2,1,0:T(8,128)(2,1)} %bitcast.10), calls=%async_computation.1 | async-start | bytes 524288 | tf_op jit(solution)/shard_map/all_to_all | solution.py:242
  13.4 6.5 %copy-start = (s32[1,256]{1,0:T(1,128)S(1)}, s32[1,256]{1,0:T(1,128)}, u32[]{:S(2)}) copy-start(s32[1,256]{1,0:T(1,128)} %source_ref.1) | copy-start | bytes 3076
  13.4 31.9 %all-to-all-start = ((bf16[16,32,1024]{2,1,0:T(8,128)(2,1)}), bf16[16,32,1024]{2,1,0:T(8,128)(2,1)S(1)}, u32[]{:S(2)}, u32[]{:S(2)}) async-start(bf16[16,32,1024]{2,1,0:T(8,128)(2,1)} %bitcast.9), calls=%async_computation | async-start | bytes 2097152 | tf_op jit(solution)/shard_map/all_to_all | solution.py:242
  20.5 3.4 %collective-permute-start = (bf16[256,256]{1,0:T(8,128)(2,1)S(1)}, bf16[256,256]{1,0:T(8,128)(2,1)S(1)}, u32[]{:S(2)}, u32[]{:S(2)}) collective-permute-start(bf16[256,256]{1,0:T(8,128)(2,1)S(1)} %shard_map.58.own_ref), channel_id=1, source_target_pairs={{0,1},{1,0},{2,3},{3,2},{4,5},{5,4},{6,7},{7,6},{8,9},{9,8},{10,11... | collective-permute-start | bytes 393224 | tf_op jit(solution)/shard_map/ppermute | solution.py:281
  23.9 23.0 %copy-start.1 = (s32[1,4]{1,0:T(1,128)S(1)}, s32[1,4]{1,0:T(1,128)}, u32[]{:S(2)}) copy-start(s32[1,4]{1,0:T(1,128)} %refs_0_.1) | copy-start | bytes 52
  24.0 10.4 %collective-permute-start.1 = (bf16[512,256]{1,0:T(8,128)(2,1)S(1)}, bf16[512,256]{1,0:T(8,128)(2,1)S(1)}, u32[]{:S(2)}, u32[]{:S(2)}) collective-permute-start(bf16[512,256]{1,0:T(8,128)(2,1)S(1)} %shard_map.59.refs_3_), channel_id=1, source_target_pairs={{0,2},{1,13},{2,4},{3,15},{4,6},{5,1},{6,8},{7,3},{8,10},{9,5},{10... | collective-permute-start | bytes 786440 | tf_op jit(solution)/shard_map/ppermute | solution.py:274
  34.3 5.5 %collective-permute-start.3 = (bf16[512,256]{1,0:T(8,128)(2,1)S(1)}, bf16[512,256]{1,0:T(8,128)(2,1)S(1)}, u32[]{:S(2)}, u32[]{:S(2)}) collective-permute-start(bf16[512,256]{1,0:T(8,128)(2,1)S(1)} %collective-permute-done.1.refs_4_), channel_id=1, source_target_pairs={{0,2},{1,15},{2,4},{3,1},{4,6},{5,3},{6,8},{7,5},{8,10},{9,7},{10,... | collective-permute-start | bytes 786440 | tf_op jit(solution)/shard_map/ppermute | solution.py:274
  34.3 11.0 %collective-permute-start.5 = (bf16[512,256]{1,0:T(8,128)(2,1)S(1)}, bf16[512,256]{1,0:T(8,128)(2,1)S(1)}, u32[]{:S(2)}, u32[]{:S(2)}) collective-permute-start(bf16[512,256]{1,0:T(8,128)(2,1)S(1)} %collective-permute-done.1.refs_4_), channel_id=1, source_target_pairs={{0,4},{1,13},{2,6},{3,15},{4,8},{5,1},{6,10},{7,3},{8,12},{9,5},{1... | collective-permute-start | bytes 786440 | tf_op jit(solution)/shard_map/ppermute | solution.py:274
  34.4 10.9 %collective-permute-start.2 = (bf16[512,256]{1,0:T(8,128)(2,1)S(1)}, bf16[512,256]{1,0:T(8,128)(2,1)S(1)}, u32[]{:S(2)}, u32[]{:S(2)}) collective-permute-start(bf16[512,256]{1,0:T(8,128)(2,1)S(1)} %collective-permute-done.1.refs_4_), channel_id=1, source_target_pairs={{0,1},{1,0},{2,3},{3,2},{4,5},{5,4},{6,7},{7,6},{8,9},{9,8},{10,11... | collective-permute-start | bytes 786440 | tf_op jit(solution)/shard_map/ppermute | solution.py:281
  39.8 5.5 %collective-permute-start.4 = (bf16[512,256]{1,0:T(8,128)(2,1)S(1)}, bf16[512,256]{1,0:T(8,128)(2,1)S(1)}, u32[]{:S(2)}, u32[]{:S(2)}) collective-permute-start(bf16[512,256]{1,0:T(8,128)(2,1)S(1)} %collective-permute-done.3.refs_6_), channel_id=1, source_target_pairs={{0,1},{1,0},{2,3},{3,2},{4,5},{5,4},{6,7},{7,6},{8,9},{9,8},{10,11... | collective-permute-start | bytes 786440 | tf_op jit(solution)/shard_map/ppermute | solution.py:281
  45.4 1.5 %collective-permute-start.6 = (bf16[512,256]{1,0:T(8,128)(2,1)S(1)}, bf16[512,256]{1,0:T(8,128)(2,1)S(1)}, u32[]{:S(2)}, u32[]{:S(2)}) collective-permute-start(bf16[512,256]{1,0:T(8,128)(2,1)S(1)} %collective-permute-done.5.refs_8_), channel_id=1, source_target_pairs={{0,1},{1,0},{2,3},{3,2},{4,5},{5,4},{6,7},{7,6},{8,9},{9,8},{10,11... | collective-permute-start | bytes 786440 | tf_op jit(solution)/shard_map/ppermute | solution.py:281
where the time goes:
time: 60 us; the launch traced here: 59.7 us
  waiting for transfers between devices  24.6 us (41%)
  Pallas kernels  17.9 us (30%)
  starting transfers between devices  17.1 us (29%)
    ppermute x3, waiting for transfers between devices, hop(): lax.ppermute(x, 'ctx', [(c, (c + (2 * up if c % 2 == 0 else -2 * down)) %...  20 us
    all_to_all x2, starting transfers between devices, exchange(): lax.all_to_all(rows.reshape(owners, capacity, rows.shape[1]), 'dp', split...  13.3 us
    pallas_call x1, Pallas kernels, body(): pl.pallas_call(functools.partial(attend_kernel, head, far), out_shape=jax...  12.8 us
    pallas_call x2, Pallas kernels, pack(): pl.pallas_call(functools.partial(pack_kernel, owners, capacity), out_shap...  4.63 us
    ppermute x4, waiting for transfers between devices, swap(): return lax.ppermute(x, 'ctx', [(c, c ^ 1) for c in range(n_ctx)])  2.5 us
    ppermute x4, starting transfers between devices, swap(): return lax.ppermute(x, 'ctx', [(c, c ^ 1) for c in range(n_ctx)])  2.44 us
    all_to_all x2, waiting for transfers between devices, exchange(): lax.all_to_all(rows.reshape(owners, capacity, rows.shape[1]), 'dp', split...  2.01 us
    ppermute x3, starting transfers between devices, hop(): lax.ppermute(x, 'ctx', [(c, (c + (2 * up if c % 2 == 0 else -2 * down)) %...  1.35 us
  transfers between devices with their start and end apart: 9, of which 6 were waited for; matrix products, arithmetic and copies ran while one was open for 0% of the time, Pallas kernels for 5%

commit v1 on v0

--- a/solution.py
+++ b/solution.py
@@ -68,7 +68,7 @@
 def attend_kernel(head, far, *refs):
     lengths_ref, picks_ref, got_ref = refs[:3]
     near = refs[3 : 3 + len(far)]
-    out_ref, kv, q_all, acc, top, over = refs[3 + len(far) :]
+    out_ref, kv, q_all, acc, top, total = refs[3 + len(far) :]
     n = picks_ref.shape[0]
     groups = out_ref.shape[1] // head
     chunk = 2 * n
@@ -77,14 +77,18 @@
     core = me - 2 * chip
 
     picks = picks_ref[...]
-    for h in range(groups):
-        exact = jnp.dot(
-            picks, got_ref[:, h * head : (h + 1) * head], preferred_element_type=jnp.float32
+    for h in range(0, groups, 2):
+        both = jnp.dot(
+            picks, got_ref[:, h * head : (h + 2) * head], preferred_element_type=jnp.float32
         ) * (LOG2E * head ** (-0.5))
-        high = exact.astype(jnp.bfloat16)
-        q_all[:, 2 * h * head : (2 * h + 1) * head] = high
-        rest = exact - high.astype(jnp.float32)
-        q_all[:, (2 * h + 1) * head : (2 * h + 2) * head] = rest.astype(jnp.bfloat16)
+        for i in range(2):
+            exact = both[:, i * head : (i + 1) * head]
+            high = exact.astype(q_all.dtype)
+            at = 2 * (h + i) * head
+            q_all[:, at : at + head] = high
+            q_all[:, at + head : at + 2 * head] = (exact - high.astype(jnp.float32)).astype(
+                q_all.dtype
+            )
 
     starts = [jnp.int32(0)]
     for i in range(lengths_ref.shape[1] - 1):
@@ -102,19 +106,20 @@
     low = start_of(q_first)
     high = start_of(q_first + n - 1)
 
-    def distance(i):
+    def place(i):
         d = jnp.int32(0)
         for j, (a, b) in enumerate(far):
             d = jnp.where(i == j, jnp.where(core == 0, a, b), d)
-        return d
-
-    for i, (ref, (a, b)) in enumerate(zip(near, far)):
-        at = (chip - jnp.where(core == 0, a, b)) * chunk
-
-        @pl.when((at >= 0) & (at + chunk > low))
+        return (chip - d) * chunk
+
+    def here(at):
+        return (at >= 0) & (at + chunk > low)
+
+    for i, ref in enumerate(near):
+
+        @pl.when(here(place(i)))
         def _():
-            kv[i, :, :head] = ref[:, :head]
-            kv[i, :, head:] = ref[:, head:]
+            kv[i] = ref[...]
 
     def tree_max(s):
         while s.shape[0] > 8:
@@ -122,16 +127,17 @@
             s = jnp.maximum(s[:half], s[half:])
         return jnp.max(s, axis=0, keepdims=True)
 
-    def step(i, at, masked, mode):
-        keys = jnp.concatenate([kv[i, :, :head]] * 2, axis=1)
-        values = jnp.concatenate(
-            [jnp.transpose(kv[i, :, head:]), jnp.ones((16, chunk), jnp.bfloat16)], axis=0
-        )
+    def fold(w):
+        return jnp.sum(w.reshape(-1, 8, w.shape[1]), axis=0)
+
+    def step(i, at, first_row, rows, masked, mode):
+        keys = jnp.concatenate([kv[i, first_row : first_row + rows, :head]] * 2, axis=1)
+        values = jnp.transpose(kv[i, first_row : first_row + rows, head:])
         if masked:
-            k_pos = at + lax.broadcasted_iota(jnp.int32, (chunk, n), 0)
+            k_pos = at + first_row + lax.broadcasted_iota(jnp.int32, (rows, n), 0)
             visible = (k_pos <= q_pos) & (k_pos >= q_start)
 
-        def qk(h):
+        def scores(h):
             s = lax.dot_general(
                 keys,
                 q_all[:, 2 * h * head : 2 * (h + 1) * head],
@@ -140,23 +146,30 @@
             )
             return jnp.where(visible, s, LOW) if masked else s
 
-        def soft(h, s):
-            if mode == "fast":
-                e = s - top[h]
-                over[...] = jnp.maximum(over[...], tree_max(e))
-                return jnp.exp2(e).astype(jnp.bfloat16), None
-            if mode == "first":
+        def weigh(h, s):
+            fade = None
+            if mode == "fixed":
+                m = top[h]
+            elif mode == "first":
                 m = tree_max(s)
                 top[h] = m
-                return jnp.exp2(s - m).astype(jnp.bfloat16), None
-            old = top[h]
-            m = jnp.maximum(old, tree_max(s))
-            top[h] = m
-            return jnp.exp2(s - m).astype(jnp.bfloat16), jnp.exp2(old - m)
-
-        def pv(h, w, fade):
+            else:
+                old = top[h]
+                m = jnp.maximum(old, tree_max(s))
+                top[h] = m
+                fade = jnp.exp2(old - m)
+            w = jnp.exp2(s - m)
+            if mode == "fixed":
+                total[h] += fold(w)
+            elif mode == "first":
+                total[h] = fold(w)
+            else:
+                total[h] = total[h] * fade + fold(w)
+            return w.astype(kv.dtype), fade
+
+        def gather(h, w, fade):
             part = jnp.dot(values, w, preferred_element_type=jnp.float32)
-            if mode == "fast":
+            if mode == "fixed":
                 acc[h] += part
             elif mode == "first":
                 acc[h] = part
@@ -167,48 +180,64 @@
         s_of, w_of = {}, {}
         for t in range(groups + 1 + lag):
             if t < groups:
-                s_of[t] = qk(t)
+                s_of[t] = scores(t)
             if 0 <= t - 1 < groups:
-                w_of[t - 1] = soft(t - 1, s_of.pop(t - 1))
+                w_of[t - 1] = weigh(t - 1, s_of.pop(t - 1))
             if 0 <= t - 1 - lag < groups:
-                pv(t - 1 - lag, *w_of.pop(t - 1 - lag))
-
-    def here(at):
-        return (at >= 0) & (at + chunk > low)
-
-    over[...] = jnp.full((1, n), LOW, jnp.float32)
-    step(0, chip * chunk, True, "first")
+                gather(t - 1 - lag, *w_of.pop(t - 1 - lag))
+
+    own = chip * chunk
+
+    @pl.when(core == 0)
+    def _():
+        step(0, own, 0, n, True, "first")
+
+    @pl.when(core != 0)
+    def _():
+        step(0, own, 0, chunk, True, "first")
 
     @pl.loop(1, len(far))
     def _(i):
-        at = (chip - distance(i)) * chunk
+        at = place(i)
         clear = (at >= high) & (at + chunk <= q_first)
+        late = low >= at + n
 
         @pl.when(here(at) & clear)
         def _():
-            step(i, at, False, "fast")
-
-        @pl.when(here(at) & jnp.logical_not(clear))
+            step(i, at, 0, chunk, False, "fixed")
+
+        @pl.when(here(at) & jnp.logical_not(clear) & late)
         def _():
-            step(i, at, True, "fast")
-
-    @pl.when(jnp.max(over[...]) > 64.0)
+            step(i, at, n, n, True, "fixed")
+
+        @pl.when(here(at) & jnp.logical_not(clear | late))
+        def _():
+            step(i, at, 0, chunk, True, "fixed")
+
+    most = total[0]
+    for h in range(1, groups):
+        most = jnp.maximum(most, total[h])
+
+    @pl.when(jnp.max(most) > 2.0**64)
     def _():
         for h in range(groups):
             top[h] = jnp.full((1, n), LOW, jnp.float32)
+            total[h] = jnp.zeros(total.shape[1:], jnp.float32)
             acc[h] = jnp.zeros(acc.shape[1:], jnp.float32)
 
         @pl.loop(0, len(far))
         def _(i):
-            at = (chip - distance(i)) * chunk
+            at = place(i)
 
             @pl.when(here(at))
             def _():
-                step(i, at, True, "slow")
+                step(i, at, 0, chunk, True, "running")
 
     for h in range(groups):
-        done = (acc[h, :head] * (1.0 / acc[h, head : head + 1])).astype(out_ref.dtype)
-        out_ref[:, h * head : (h + 1) * head] = jnp.transpose(done)
+        share = 1.0 / jnp.sum(total[h], axis=0, keepdims=True)
+        out_ref[:, h * head : (h + 1) * head] = jnp.transpose(
+            (acc[h] * share).astype(out_ref.dtype)
+        )
 
 
 def vmem(count):
@@ -305,9 +334,9 @@
         scratch_shapes=[
             pltpu.VMEM((len(far), 2 * n, kv_width), keyvals.dtype),
             pltpu.VMEM((n, 2 * width), queries.dtype),
-            pltpu.VMEM((groups, head + 16, n), jnp.float32),
+            pltpu.VMEM((groups, head, n), jnp.float32),
             pltpu.VMEM((groups, 1, n), jnp.float32),
-            pltpu.VMEM((1, n), jnp.float32),
+            pltpu.VMEM((groups, 8, n), jnp.float32),
         ],
         compiler_params=pltpu.CompilerParams(vmem_limit_bytes=24 << 20),
         cost_estimate=pl.CostEstimate(

time: 60 us -> 58.9 us (0.982)
  Pallas kernels: 17.9 us -> 16.9 us
    pallas_call x1, Pallas kernels: 12.8 us -> 11.7 us  [body(): pl.pallas_call(functools.partial(attend_kernel, head, far), out_shape=jax...]
where the time goes in v1:
time: 58.9 us; the launch traced here: 58.6 us
  waiting for transfers between devices  24.6 us (42%)
  starting transfers between devices  17.1 us (29%)
  Pallas kernels  16.9 us (29%)
    ppermute x3, waiting for transfers between devices, hop(): lax.ppermute(x, 'ctx', [(c, (c + (2 * up if c % 2 == 0 else -2 * down)) %...  20 us
    all_to_all x2, starting transfers between devices, exchange(): lax.all_to_all(rows.reshape(owners, capacity, rows.shape[1]), 'dp', split...  13.3 us
    pallas_call x1, Pallas kernels, body(): pl.pallas_call(functools.partial(attend_kernel, head, far), out_shape=jax...  11.7 us
    pallas_call x2, Pallas kernels, pack(): pl.pallas_call(functools.partial(pack_kernel, owners, capacity), out_shap...  4.63 us
    ppermute x4, waiting for transfers between devices, swap(): return lax.ppermute(x, 'ctx', [(c, c ^ 1) for c in range(n_ctx)])  2.5 us
    ppermute x4, starting transfers between devices, swap(): return lax.ppermute(x, 'ctx', [(c, c ^ 1) for c in range(n_ctx)])  2.44 us
    all_to_all x2, waiting for transfers between devices, exchange(): lax.all_to_all(rows.reshape(owners, capacity, rows.shape[1]), 'dp', split...  2.01 us
    ppermute x3, starting transfers between devices, hop(): lax.ppermute(x, 'ctx', [(c, (c + (2 * up if c % 2 == 0 else -2 * down)) %...  1.35 us
  transfers between devices with their start and end apart: 9, of which 6 were waited for; matrix products, arithmetic and copies ran while one was open for 0% of the time, Pallas kernels for 5%

profile of v1, /device:TPU:205, one launch (start us, length us, event | category | flops | bytes accessed | tf_op | source)
XLA Modules:
  0.0 58.6 jit_solution(15065919445186378789)
XLA Ops:
  0.0 2.0 %shard_map.57 = bf16[512,256]{1,0:T(8,128)(2,1)} custom-call(s32[1,256]{1,0:T(1,128)} %dest_ref.3, bf16[256,256]{1,0:T(8,128)(2,1)} %bitcast.12), custom_call_target="tpu_custom_call" | custom-call | flops 67108864 | bytes 393216 | tf_op jit(solution)/shard_map/pallas_call | solution.py:258
  2.0 6.8 %all-to-all-start.1 = ((bf16[16,32,256]{2,1,0:T(8,128)(2,1)}), bf16[16,32,256]{2,1,0:T(8,128)(2,1)S(1)}, u32[]{:S(2)}, u32[]{:S(2)}) async-start(bf16[16,32,256]{2,1,0:T(8,128)(2,1)} %bitcast.10), calls=%async_computation.1 | async-start | bytes 524288 | tf_op jit(solution)/shard_map/all_to_all | solution.py:271
  8.8 2.6 %shard_map.56 = bf16[512,1024]{1,0:T(8,128)(2,1)} custom-call(s32[1,256]{1,0:T(1,128)} %dest_ref.3, bf16[256,1024]{1,0:T(8,128)(2,1)} %bitcast.11), custom_call_target="tpu_custom_call" | custom-call | flops 268435456 | bytes 1572864 | tf_op jit(solution)/shard_map/pallas_call | solution.py:258
  11.4 2.0 %all-to-all-done.1 = bf16[16,32,256]{2,1,0:T(8,128)(2,1)S(1)} async-done(((bf16[16,32,256]{2,1,0:T(8,128)(2,1)}), bf16[16,32,256]{2,1,0:T(8,128)(2,1)S(1)}, u32[]{:S(2)}, u32[]{:S(2)}) %all-to-all-start.1) | async-done | bytes 262176 | tf_op jit(solution)/shard_map/all_to_all | solution.py:271
  13.4 0.0 copy-start
  13.4 6.5 %all-to-all-start = ((bf16[16,32,1024]{2,1,0:T(8,128)(2,1)}), bf16[16,32,1024]{2,1,0:T(8,128)(2,1)S(1)}, u32[]{:S(2)}, u32[]{:S(2)}) async-start(bf16[16,32,1024]{2,1,0:T(8,128)(2,1)} %bitcast.9), calls=%async_computation | async-start | bytes 2097152 | tf_op jit(solution)/shard_map/all_to_all | solution.py:271
  20.0 0.0 copy-done
  20.0 0.3 shard_map.55.picks_ref.refs_1_
  20.3 0.2 shard_map.58.own_ref
  20.5 2.4 %collective-permute-start = (bf16[256,256]{1,0:T(8,128)(2,1)S(1)}, bf16[256,256]{1,0:T(8,128)(2,1)S(1)}, u32[]{:S(2)}, u32[]{:S(2)}) collective-permute-start(bf16[256,256]{1,0:T(8,128)(2,1)S(1)} %shard_map.58.own_ref), channel_id=1, source_target_pairs={{0,1},{1,0},{2,3},{3,2},{4,5},{5,4},{6,7},{7,6},{8,9},{9,8},{10,11... | collective-permute-start | bytes 393224 | tf_op jit(solution)/shard_map/ppermute | solution.py:310
  22.9 1.0 %collective-permute-done.other_ref = bf16[256,256]{1,0:T(8,128)(2,1)S(1)} collective-permute-done((bf16[256,256]{1,0:T(8,128)(2,1)S(1)}, bf16[256,256]{1,0:T(8,128)(2,1)S(1)}, u32[]{:S(2)}, u32[]{:S(2)}) %collective-permute-start) | collective-permute-done | bytes 131104 | tf_op jit(solution)/shard_map/ppermute | solution.py:310
  23.9 0.0 copy-start.1
  24.0 1.2 %collective-permute-start.1 = (bf16[512,256]{1,0:T(8,128)(2,1)S(1)}, bf16[512,256]{1,0:T(8,128)(2,1)S(1)}, u32[]{:S(2)}, u32[]{:S(2)}) collective-permute-start(bf16[512,256]{1,0:T(8,128)(2,1)S(1)} %shard_map.59.refs_3_), channel_id=1, source_target_pairs={{0,2},{1,13},{2,4},{3,15},{4,6},{5,1},{6,8},{7,3},{8,10},{9,5},{10... | collective-permute-start | bytes 786440 | tf_op jit(solution)/shard_map/ppermute | solution.py:303
  25.2 9.1 %collective-permute-done.1.refs_4_ = bf16[512,256]{1,0:T(8,128)(2,1)S(1)} collective-permute-done((bf16[512,256]{1,0:T(8,128)(2,1)S(1)}, bf16[512,256]{1,0:T(8,128)(2,1)S(1)}, u32[]{:S(2)}, u32[]{:S(2)}) %collective-permute-start.1) | collective-permute-done | bytes 262176 | tf_op jit(solution)/shard_map/ppermute | solution.py:303
  34.3 0.0 collective-permute-start.3
  34.3 0.1 collective-permute-start.5
  34.4 0.0 collective-permute-start.2
  34.4 5.4 %collective-permute-done.3.refs_6_ = bf16[512,256]{1,0:T(8,128)(2,1)S(1)} collective-permute-done((bf16[512,256]{1,0:T(8,128)(2,1)S(1)}, bf16[512,256]{1,0:T(8,128)(2,1)S(1)}, u32[]{:S(2)}, u32[]{:S(2)}) %collective-permute-start.3) | collective-permute-done | bytes 262176 | tf_op jit(solution)/shard_map/ppermute | solution.py:303
  39.8 0.0 collective-permute-start.4
  39.8 5.5 %collective-permute-done.5.refs_8_ = bf16[512,256]{1,0:T(8,128)(2,1)S(1)} collective-permute-done((bf16[512,256]{1,0:T(8,128)(2,1)S(1)}, bf16[512,256]{1,0:T(8,128)(2,1)S(1)}, u32[]{:S(2)}, u32[]{:S(2)}) %collective-permute-start.5) | collective-permute-done | bytes 262176 | tf_op jit(solution)/shard_map/ppermute | solution.py:303
  45.4 0.0 collective-permute-start.6
  45.4 0.0 collective-permute-done.2.refs_5_
  45.4 0.0 all-to-all-done
  45.4 0.0 collective-permute-done.4.refs_7_
  45.4 1.5 %collective-permute-done.6.refs_9_ = bf16[512,256]{1,0:T(8,128)(2,1)S(1)} collective-permute-done((bf16[512,256]{1,0:T(8,128)(2,1)S(1)}, bf16[512,256]{1,0:T(8,128)(2,1)S(1)}, u32[]{:S(2)}, u32[]{:S(2)}) %collective-permute-start.6) | collective-permute-done | bytes 262176 | tf_op jit(solution)/shard_map/ppermute | solution.py:310
  46.9 0.0 copy-done.1
  46.9 11.7 %shard_map.60 = bf16[256,1024]{1,0:T(8,128)(2,1)} custom-call(s32[1,4]{1,0:T(1,128)S(1)} %copy-done.1, bf16[256,512]{1,0:T(8,128)(2,1)S(1)} %shard_map.55.picks_ref.refs_1_, bf16[512,1024]{1,0:T(8,128)(2,1)S(1)} %bitcast.7, bf16[512,256]{1,0:T(8,128)(2,1)S(1)} %shard_map.59.refs_3_, bf16[512,256]{1,0:T(8,128)(2,1)S(1)} %collective-permute-done.1.refs_4_, ...), custom_call_target="tpu_custom_call" | custom-call | flops 3221225472 | bytes 2097152 | tf_op jit(solution)/shard_map/pallas_call | solution.py:329
  (1 shorter events, 0.0 us)
Async XLA Ops:
  2.0 11.4 %all-to-all-start.1 = ((bf16[16,32,256]{2,1,0:T(8,128)(2,1)}), bf16[16,32,256]{2,1,0:T(8,128)(2,1)S(1)}, u32[]{:S(2)}, u32[]{:S(2)}) async-start(bf16[16,32,256]{2,1,0:T(8,128)(2,1)} %bitcast.10), calls=%async_computation.1 | async-start | bytes 524288 | tf_op jit(solution)/shard_map/all_to_all | solution.py:271
  13.4 6.5 %copy-start = (s32[1,256]{1,0:T(1,128)S(1)}, s32[1,256]{1,0:T(1,128)}, u32[]{:S(2)}) copy-start(s32[1,256]{1,0:T(1,128)} %source_ref.1) | copy-start | bytes 3076
  13.4 31.9 %all-to-all-start = ((bf16[16,32,1024]{2,1,0:T(8,128)(2,1)}), bf16[16,32,1024]{2,1,0:T(8,128)(2,1)S(1)}, u32[]{:S(2)}, u32[]{:S(2)}) async-start(bf16[16,32,1024]{2,1,0:T(8,128)(2,1)} %bitcast.9), calls=%async_computation | async-start | bytes 2097152 | tf_op jit(solution)/shard_map/all_to_all | solution.py:271
  20.5 3.4 %collective-permute-start = (bf16[256,256]{1,0:T(8,128)(2,1)S(1)}, bf16[256,256]{1,0:T(8,128)(2,1)S(1)}, u32[]{:S(2)}, u32[]{:S(2)}) collective-permute-start(bf16[256,256]{1,0:T(8,128)(2,1)S(1)} %shard_map.58.own_ref), channel_id=1, source_target_pairs={{0,1},{1,0},{2,3},{3,2},{4,5},{5,4},{6,7},{7,6},{8,9},{9,8},{10,11... | collective-permute-start | bytes 393224 | tf_op jit(solution)/shard_map/ppermute | solution.py:310
  23.9 23.0 %copy-start.1 = (s32[1,4]{1,0:T(1,128)S(1)}, s32[1,4]{1,0:T(1,128)}, u32[]{:S(2)}) copy-start(s32[1,4]{1,0:T(1,128)} %refs_0_.1) | copy-start | bytes 52
  24.0 10.4 %collective-permute-start.1 = (bf16[512,256]{1,0:T(8,128)(2,1)S(1)}, bf16[512,256]{1,0:T(8,128)(2,1)S(1)}, u32[]{:S(2)}, u32[]{:S(2)}) collective-permute-start(bf16[512,256]{1,0:T(8,128)(2,1)S(1)} %shard_map.59.refs_3_), channel_id=1, source_target_pairs={{0,2},{1,13},{2,4},{3,15},{4,6},{5,1},{6,8},{7,3},{8,10},{9,5},{10... | collective-permute-start | bytes 786440 | tf_op jit(solution)/shard_map/ppermute | solution.py:303
  34.3 5.5 %collective-permute-start.3 = (bf16[512,256]{1,0:T(8,128)(2,1)S(1)}, bf16[512,256]{1,0:T(8,128)(2,1)S(1)}, u32[]{:S(2)}, u32[]{:S(2)}) collective-permute-start(bf16[512,256]{1,0:T(8,128)(2,1)S(1)} %collective-permute-done.1.refs_4_), channel_id=1, source_target_pairs={{0,2},{1,15},{2,4},{3,1},{4,6},{5,3},{6,8},{7,5},{8,10},{9,7},{10,... | collective-permute-start | bytes 786440 | tf_op jit(solution)/shard_map/ppermute | solution.py:303
  34.3 11.0 %collective-permute-start.5 = (bf16[512,256]{1,0:T(8,128)(2,1)S(1)}, bf16[512,256]{1,0:T(8,128)(2,1)S(1)}, u32[]{:S(2)}, u32[]{:S(2)}) collective-permute-start(bf16[512,256]{1,0:T(8,128)(2,1)S(1)} %collective-permute-done.1.refs_4_), channel_id=1, source_target_pairs={{0,4},{1,13},{2,6},{3,15},{4,8},{5,1},{6,10},{7,3},{8,12},{9,5},{1... | collective-permute-start | bytes 786440 | tf_op jit(solution)/shard_map/ppermute | solution.py:303
  34.4 10.9 %collective-permute-start.2 = (bf16[512,256]{1,0:T(8,128)(2,1)S(1)}, bf16[512,256]{1,0:T(8,128)(2,1)S(1)}, u32[]{:S(2)}, u32[]{:S(2)}) collective-permute-start(bf16[512,256]{1,0:T(8,128)(2,1)S(1)} %collective-permute-done.1.refs_4_), channel_id=1, source_target_pairs={{0,1},{1,0},{2,3},{3,2},{4,5},{5,4},{6,7},{7,6},{8,9},{9,8},{10,11... | collective-permute-start | bytes 786440 | tf_op jit(solution)/shard_map/ppermute | solution.py:310
  39.8 5.5 %collective-permute-start.4 = (bf16[512,256]{1,0:T(8,128)(2,1)S(1)}, bf16[512,256]{1,0:T(8,128)(2,1)S(1)}, u32[]{:S(2)}, u32[]{:S(2)}) collective-permute-start(bf16[512,256]{1,0:T(8,128)(2,1)S(1)} %collective-permute-done.3.refs_6_), channel_id=1, source_target_pairs={{0,1},{1,0},{2,3},{3,2},{4,5},{5,4},{6,7},{7,6},{8,9},{9,8},{10,11... | collective-permute-start | bytes 786440 | tf_op jit(solution)/shard_map/ppermute | solution.py:310
  45.4 1.5 %collective-permute-start.6 = (bf16[512,256]{1,0:T(8,128)(2,1)S(1)}, bf16[512,256]{1,0:T(8,128)(2,1)S(1)}, u32[]{:S(2)}, u32[]{:S(2)}) collective-permute-start(bf16[512,256]{1,0:T(8,128)(2,1)S(1)} %collective-permute-done.5.refs_8_), channel_id=1, source_target_pairs={{0,1},{1,0},{2,3},{3,2},{4,5},{5,4},{6,7},{7,6},{8,9},{9,8},{10,11... | collective-permute-start | bytes 786440 | tf_op jit(solution)/shard_map/ppermute | solution.py:310

commit v2 on v1

--- a/solution.py
+++ b/solution.py
@@ -1,4 +1,5 @@
 import functools
+import typing
 
 import jax
 import jax.numpy as jnp
@@ -65,18 +66,8 @@
     out_ref[pl.ds(pl.multiple_of((1 - core) * n, n), n), :] = other_ref[...]
 
 
-def attend_kernel(head, far, *refs):
-    lengths_ref, picks_ref, got_ref = refs[:3]
-    near = refs[3 : 3 + len(far)]
-    out_ref, kv, q_all, acc, top, total = refs[3 + len(far) :]
-    n = picks_ref.shape[0]
-    groups = out_ref.shape[1] // head
-    chunk = 2 * n
-    me = lax.axis_index("ctx")
-    chip = me // 2
-    core = me - 2 * chip
-
-    picks = picks_ref[...]
+def split_query(head, picks, got_ref, q_all):
+    groups = got_ref.shape[1] // head
     for h in range(0, groups, 2):
         both = jnp.dot(
             picks, got_ref[:, h * head : (h + 2) * head], preferred_element_type=jnp.float32
@@ -90,6 +81,25 @@
                 q_all.dtype
             )
 
+
+class Block(typing.NamedTuple):
+    core: jax.Array
+    own: jax.Array
+    place: typing.Callable
+    here: typing.Callable
+    clear: typing.Callable
+    late: typing.Callable
+    step: typing.Callable
+
+
+def block_of(head, far, lengths_ref, kv, q_all, acc, top, total):
+    n = q_all.shape[0]
+    groups = acc.shape[0]
+    chunk = 2 * n
+    me = lax.axis_index("ctx")
+    chip = me // 2
+    core = me - 2 * chip
+
     starts = [jnp.int32(0)]
     for i in range(lengths_ref.shape[1] - 1):
         starts.append(starts[-1] + lengths_ref[0, i])
@@ -107,19 +117,16 @@
     high = start_of(q_first + n - 1)
 
     def place(i):
-        d = jnp.int32(0)
-        for j, (a, b) in enumerate(far):
-            d = jnp.where(i == j, jnp.where(core == 0, a, b), d)
-        return (chip - d) * chunk
+        return (chip - jnp.where(core == 0, far[i][0], far[i][1])) * chunk
 
     def here(at):
         return (at >= 0) & (at + chunk > low)
 
-    for i, ref in enumerate(near):
-
-        @pl.when(here(place(i)))
-        def _():
-            kv[i] = ref[...]
+    def clear(at):
+        return (at >= high) & (at + chunk <= q_first)
+
+    def late(at):
+        return low >= at + n
 
     def tree_max(s):
         while s.shape[0] > 8:
@@ -130,11 +137,12 @@
     def fold(w):
         return jnp.sum(w.reshape(-1, 8, w.shape[1]), axis=0)
 
-    def step(i, at, first_row, rows, masked, mode):
-        keys = jnp.concatenate([kv[i, first_row : first_row + rows, :head]] * 2, axis=1)
-        values = jnp.transpose(kv[i, first_row : first_row + rows, head:])
+    def step(row, rows, position, masked, mode):
+        row = pl.multiple_of(row, n)
+        keys = jnp.concatenate([kv[pl.ds(row, rows), :head]] * 2, axis=1)
+        values = jnp.transpose(kv[pl.ds(row, rows), head:])
         if masked:
-            k_pos = at + first_row + lax.broadcasted_iota(jnp.int32, (rows, n), 0)
+            k_pos = position + lax.broadcasted_iota(jnp.int32, (rows, n), 0)
             visible = (k_pos <= q_pos) & (k_pos >= q_start)
 
         def scores(h):
@@ -186,33 +194,97 @@
             if 0 <= t - 1 - lag < groups:
                 gather(t - 1 - lag, *w_of.pop(t - 1 - lag))
 
-    own = chip * chunk
-
-    @pl.when(core == 0)
-    def _():
-        step(0, own, 0, n, True, "first")
-
-    @pl.when(core != 0)
-    def _():
-        step(0, own, 0, chunk, True, "first")
-
-    @pl.loop(1, len(far))
-    def _(i):
-        at = place(i)
-        clear = (at >= high) & (at + chunk <= q_first)
-        late = low >= at + n
-
-        @pl.when(here(at) & clear)
+    return Block(core, chip * chunk, place, here, clear, late, step)
+
+
+def attend_kernel(head, far, *refs):
+    lengths_ref, picks_ref, got_ref = refs[:3]
+    near = refs[3:-6]
+    q_all, acc, top, total, kv, at_of = refs[-6:]
+    n = picks_ref.shape[0]
+    chunk = 2 * n
+    split_query(head, picks_ref[...], got_ref, q_all)
+    block = block_of(head, far, lengths_ref, kv, q_all, acc, top, total)
+
+    last = len(near) - 1
+    kv[0:chunk] = near[0][...]
+    plain = jnp.int32(0)
+    edged = jnp.int32(0)
+    for i in range(1, len(near)):
+        at = block.place(i)
+        is_here = block.here(at)
+        is_clear = block.clear(at)
+        slot = jnp.where(is_clear, 1 + plain, last - edged)
+
+        @pl.when(is_here)
         def _():
-            step(i, at, 0, chunk, False, "fixed")
-
-        @pl.when(here(at) & jnp.logical_not(clear) & late)
+            kv[pl.ds(pl.multiple_of(slot * chunk, chunk), chunk)] = near[i][...]
+            at_of[slot] = at
+
+        plain += jnp.where(is_here & is_clear, 1, 0)
+        edged += jnp.where(is_here & jnp.logical_not(is_clear), 1, 0)
+
+    @pl.when(block.core == 0)
+    def _():
+        block.step(0, n, block.own, True, "first")
+
+    @pl.when(block.core != 0)
+    def _():
+        block.step(0, chunk, block.own, True, "first")
+
+    @pl.loop(0, plain // 2)
+    def _(p):
+        block.step((1 + 2 * p) * chunk, 2 * chunk, 0, False, "fixed")
+
+    @pl.when(lax.rem(plain, 2) == 1)
+    def _():
+        block.step(plain * chunk, chunk, 0, False, "fixed")
+
+    @pl.loop(0, edged)
+    def _(j):
+        slot = last - j
+        at = at_of[slot]
+
+        @pl.when(block.late(at))
         def _():
-            step(i, at, n, n, True, "fixed")
-
-        @pl.when(here(at) & jnp.logical_not(clear | late))
+            block.step(slot * chunk + n, n, at + n, True, "fixed")
+
+        @pl.when(jnp.logical_not(block.late(at)))
         def _():
-            step(i, at, 0, chunk, True, "fixed")
+            block.step(slot * chunk, chunk, at, True, "fixed")
+
+
+def finish_kernel(head, far, *refs):
+    lengths_ref, q_all, acc_ref, top_ref, total_ref = refs[:5]
+    near = refs[5:-5]
+    out_ref, kv, acc, top, total = refs[-5:]
+    n = q_all.shape[0]
+    groups = acc.shape[0]
+    chunk = 2 * n
+    acc[...] = acc_ref[...]
+    top[...] = top_ref[...]
+    total[...] = total_ref[...]
+    block = block_of(head, far, lengths_ref, kv, q_all, acc, top, total)
+    at = block.place(len(near) - 1)
+    is_here = block.here(at)
+    is_clear = block.clear(at)
+    is_late = block.late(at)
+
+    @pl.when(is_here)
+    def _():
+        kv[...] = near[-1][...]
+
+    @pl.when(is_here & is_clear)
+    def _():
+        block.step(0, chunk, at, False, "fixed")
+
+    @pl.when(is_here & jnp.logical_not(is_clear) & is_late)
+    def _():
+        block.step(n, n, at + n, True, "fixed")
+
+    @pl.when(is_here & jnp.logical_not(is_clear | is_late))
+    def _():
+        block.step(0, chunk, at, True, "fixed")
 
     most = total[0]
     for h in range(1, groups):
@@ -225,13 +297,19 @@
             total[h] = jnp.zeros(total.shape[1:], jnp.float32)
             acc[h] = jnp.zeros(acc.shape[1:], jnp.float32)
 
-        @pl.loop(0, len(far))
+        @pl.loop(0, len(near))
         def _(i):
-            at = place(i)
-
-            @pl.when(here(at))
+            place = block.place(0)
+            for j, ref in enumerate(near):
+                place = jnp.where(i == j, block.place(j), place)
+
+                @pl.when(i == j)
+                def _():
+                    kv[...] = ref[...]
+
+            @pl.when(block.here(place))
             def _():
-                step(i, at, 0, chunk, True, "running")
+                block.step(0, chunk, place, True, "running")
 
     for h in range(groups):
         share = 1.0 / jnp.sum(total[h], axis=0, keepdims=True)
@@ -323,28 +401,50 @@
     hop2 = hop(hop1, 1, 1)
     hop3 = hop(hop1, 2, 2)
     far = [(0, 0), (1, 6), (6, 1), (2, 5), (5, 2), (3, 4), (4, 3)]
-    pieces = [pair, hop1, swap(hop1), hop2, swap(hop2), hop3, swap(hop3)]
+    last = swap(hop3)
+    pieces = [pair, hop1, swap(hop1), hop2, swap(hop2), hop3, last]
     groups = width // head
-
-    attended = pl.pallas_call(
+    state = (
+        jax.ShapeDtypeStruct((n, 2 * width), queries.dtype),
+        jax.ShapeDtypeStruct((groups, head, n), jnp.float32),
+        jax.ShapeDtypeStruct((groups, 1, n), jnp.float32),
+        jax.ShapeDtypeStruct((groups, 8, n), jnp.float32),
+    )
+
+    sums = pl.pallas_call(
         functools.partial(attend_kernel, head, far),
-        out_shape=jax.ShapeDtypeStruct((n, width), queries.dtype),
-        in_specs=[pl.BlockSpec(memory_space=pltpu.SMEM)] + vmem(2 + len(far)),
-        out_specs=vmem(1)[0],
+        out_shape=state,
+        in_specs=[pl.BlockSpec(memory_space=pltpu.SMEM)] + vmem(1 + len(far)),
+        out_specs=tuple(vmem(len(state))),
         scratch_shapes=[
-            pltpu.VMEM((len(far), 2 * n, kv_width), keyvals.dtype),
-            pltpu.VMEM((n, 2 * width), queries.dtype),
-            pltpu.VMEM((groups, head, n), jnp.float32),
-            pltpu.VMEM((groups, 1, n), jnp.float32),
-            pltpu.VMEM((groups, 8, n), jnp.float32),
+            pltpu.VMEM((2 * n * (len(far) - 1), kv_width), keyvals.dtype),
+            pltpu.SMEM((len(far),), jnp.int32),
         ],
         compiler_params=pltpu.CompilerParams(vmem_limit_bytes=24 << 20),
         cost_estimate=pl.CostEstimate(
-            flops=4 * n * width * 12 * n,
+            flops=4 * n * width * 10 * n,
             bytes_accessed=8 * n * width,
-            transcendentals=12 * n * n * groups,
-        ),
-    )(seq_lengths, picks, got_q, *pieces)
+            transcendentals=10 * n * n * groups,
+        ),
+    )(seq_lengths, picks, got_q, *pieces[:-1])
+    attended = pl.pallas_call(
+        functools.partial(finish_kernel, head, far),
+        out_shape=jax.ShapeDtypeStruct((n, width), queries.dtype),
+        in_specs=[pl.BlockSpec(memory_space=pltpu.SMEM)] + vmem(len(state) + len(far)),
+        out_specs=vmem(1)[0],
+        scratch_shapes=[
+            pltpu.VMEM((2 * n, kv_width), keyvals.dtype),
+            pltpu.VMEM(state[1].shape, jnp.float32),
+            pltpu.VMEM(state[2].shape, jnp.float32),
+            pltpu.VMEM(state[3].shape, jnp.float32),
+        ],
+        compiler_params=pltpu.CompilerParams(vmem_limit_bytes=24 << 20),
+        cost_estimate=pl.CostEstimate(
+            flops=4 * n * width * 2 * n,
+            bytes_accessed=8 * n * width,
+            transcendentals=2 * n * n * groups,
+        ),
+    )(seq_lengths, *sums, *pieces)
     return attended.reshape(1, n, width)
 
 

time: 58.9 us -> 58 us (0.985)
  waiting for transfers between devices: 24.6 us -> 23 us
  Pallas kernels: 16.9 us -> 17.5 us
    ppermute x4, waiting for transfers between devices: 2.5 us -> 0.99 us  [swap(): return lax.ppermute(x, 'ctx', [(c, c ^ 1) for c in range(n_ctx)])]
    pallas_call x1 -> x2, Pallas kernels: 11.7 us -> 12.3 us  [the longest x1 9.17 us: body(): pl.pallas_call(functools.partial(attend_kernel, head, far), out_shape=sta...]
  transfers between devices with their start and end apart: 9 -> 9, of which waited for: 6 -> 5; matrix products, arithmetic and copies ran while one was open for 0% -> 0% of each run, Pallas kernels for 5% -> 21%
where the time goes in v2:
time: 58 us; the launch traced here: 57.8 us
  waiting for transfers between devices  23 us (40%)
  Pallas kernels  17.5 us (30%)
  starting transfers between devices  17.1 us (29%)
    ppermute x3, waiting for transfers between devices, hop(): lax.ppermute(x, 'ctx', [(c, (c + (2 * up if c % 2 == 0 else -2 * down)) %...  20 us
    all_to_all x2, starting transfers between devices, exchange(): lax.all_to_all(rows.reshape(owners, capacity, rows.shape[1]), 'dp', split...  13.3 us
    pallas_call x1, Pallas kernels, body(): pl.pallas_call(functools.partial(attend_kernel, head, far), out_shape=sta...  9.17 us
    pallas_call x2, Pallas kernels, pack(): pl.pallas_call(functools.partial(pack_kernel, owners, capacity), out_shap...  4.63 us
    pallas_call x1, Pallas kernels, body(): pl.pallas_call(functools.partial(finish_kernel, head, far), out_shape=jax...  3.17 us
    ppermute x4, starting transfers between devices, swap(): return lax.ppermute(x, 'ctx', [(c, c ^ 1) for c in range(n_ctx)])  2.43 us
    all_to_all x2, waiting for transfers between devices, exchange(): lax.all_to_all(rows.reshape(owners, capacity, rows.shape[1]), 'dp', split...  2.01 us
    ppermute x3, starting transfers between devices, hop(): lax.ppermute(x, 'ctx', [(c, (c + (2 * up if c % 2 == 0 else -2 * down)) %...  1.38 us
  transfers between devices with their start and end apart: 9, of which 5 were waited for; matrix products, arithmetic and copies ran while one was open for 0% of the time, Pallas kernels for 21%

profile of v2, /device:TPU:205, one launch (start us, length us, event | category | flops | bytes accessed | tf_op | source)
XLA Modules:
  0.0 57.8 jit_solution(1944820990029723306)
XLA Ops:
  0.0 2.0 %shard_map.57 = bf16[512,256]{1,0:T(8,128)(2,1)} custom-call(s32[1,256]{1,0:T(1,128)} %dest_ref.3, bf16[256,256]{1,0:T(8,128)(2,1)} %bitcast.12), custom_call_target="tpu_custom_call" | custom-call | flops 67108864 | bytes 393216 | tf_op jit(solution)/shard_map/pallas_call | solution.py:336
  2.0 6.8 %all-to-all-start.1 = ((bf16[16,32,256]{2,1,0:T(8,128)(2,1)}), bf16[16,32,256]{2,1,0:T(8,128)(2,1)S(1)}, u32[]{:S(2)}, u32[]{:S(2)}) async-start(bf16[16,32,256]{2,1,0:T(8,128)(2,1)} %bitcast.10), calls=%async_computation.1 | async-start | bytes 524288 | tf_op jit(solution)/shard_map/all_to_all | solution.py:349
  8.8 2.6 %shard_map.56 = bf16[512,1024]{1,0:T(8,128)(2,1)} custom-call(s32[1,256]{1,0:T(1,128)} %dest_ref.3, bf16[256,1024]{1,0:T(8,128)(2,1)} %bitcast.11), custom_call_target="tpu_custom_call" | custom-call | flops 268435456 | bytes 1572864 | tf_op jit(solution)/shard_map/pallas_call | solution.py:336
  11.4 2.0 %all-to-all-done.1 = bf16[16,32,256]{2,1,0:T(8,128)(2,1)S(1)} async-done(((bf16[16,32,256]{2,1,0:T(8,128)(2,1)}), bf16[16,32,256]{2,1,0:T(8,128)(2,1)S(1)}, u32[]{:S(2)}, u32[]{:S(2)}) %all-to-all-start.1) | async-done | bytes 262176 | tf_op jit(solution)/shard_map/all_to_all | solution.py:349
  13.4 0.0 copy-start
  13.4 6.5 %all-to-all-start = ((bf16[16,32,1024]{2,1,0:T(8,128)(2,1)}), bf16[16,32,1024]{2,1,0:T(8,128)(2,1)S(1)}, u32[]{:S(2)}, u32[]{:S(2)}) async-start(bf16[16,32,1024]{2,1,0:T(8,128)(2,1)} %bitcast.9), calls=%async_computation | async-start | bytes 2097152 | tf_op jit(solution)/shard_map/all_to_all | solution.py:349
  20.0 0.0 copy-done
  20.0 0.3 shard_map.55.picks_ref.refs_1_
  20.3 0.2 shard_map.58.own_ref
  20.5 2.4 %collective-permute-start = (bf16[256,256]{1,0:T(8,128)(2,1)S(1)}, bf16[256,256]{1,0:T(8,128)(2,1)S(1)}, u32[]{:S(2)}, u32[]{:S(2)}) collective-permute-start(bf16[256,256]{1,0:T(8,128)(2,1)S(1)} %shard_map.58.own_ref), channel_id=1, source_target_pairs={{0,1},{1,0},{2,3},{3,2},{4,5},{5,4},{6,7},{7,6},{8,9},{9,8},{10,11... | collective-permute-start | bytes 393224 | tf_op jit(solution)/shard_map/ppermute | solution.py:388
  22.9 1.0 %collective-permute-done.other_ref = bf16[256,256]{1,0:T(8,128)(2,1)S(1)} collective-permute-done((bf16[256,256]{1,0:T(8,128)(2,1)S(1)}, bf16[256,256]{1,0:T(8,128)(2,1)S(1)}, u32[]{:S(2)}, u32[]{:S(2)}) %collective-permute-start) | collective-permute-done | bytes 131104 | tf_op jit(solution)/shard_map/ppermute | solution.py:388
  23.9 0.0 copy-start.1
  24.0 1.3 %collective-permute-start.1 = (bf16[512,256]{1,0:T(8,128)(2,1)S(1)}, bf16[512,256]{1,0:T(8,128)(2,1)S(1)}, u32[]{:S(2)}, u32[]{:S(2)}) collective-permute-start(bf16[512,256]{1,0:T(8,128)(2,1)S(1)} %shard_map.59.refs_3_.refs_5_), channel_id=1, source_target_pairs={{0,2},{1,13},{2,4},{3,15},{4,6},{5,1},{6,8},{7,3},{8,10},{9,5},{10... | collective-permute-start | bytes 786440 | tf_op jit(solution)/shard_map/ppermute | solution.py:381
  25.2 9.1 %collective-permute-done.1.refs_4_.refs_6_ = bf16[512,256]{1,0:T(8,128)(2,1)S(1)} collective-permute-done((bf16[512,256]{1,0:T(8,128)(2,1)S(1)}, bf16[512,256]{1,0:T(8,128)(2,1)S(1)}, u32[]{:S(2)}, u32[]{:S(2)}) %collective-permute-start.1) | collective-permute-done | bytes 262176 | tf_op jit(solution)/shard_map/ppermute | solution.py:381
  34.3 0.0 collective-permute-start.3
  34.3 0.1 collective-permute-start.5
  34.4 0.0 collective-permute-start.2
  34.4 5.4 %collective-permute-done.3.refs_6_.refs_8_ = bf16[512,256]{1,0:T(8,128)(2,1)S(1)} collective-permute-done((bf16[512,256]{1,0:T(8,128)(2,1)S(1)}, bf16[512,256]{1,0:T(8,128)(2,1)S(1)}, u32[]{:S(2)}, u32[]{:S(2)}) %collective-permute-start.3) | collective-permute-done | bytes 262176 | tf_op jit(solution)/shard_map/ppermute | solution.py:381
  39.8 0.0 collective-permute-start.4
  39.8 5.5 %collective-permute-done.5.refs_8_.refs_10_ = bf16[512,256]{1,0:T(8,128)(2,1)S(1)} collective-permute-done((bf16[512,256]{1,0:T(8,128)(2,1)S(1)}, bf16[512,256]{1,0:T(8,128)(2,1)S(1)}, u32[]{:S(2)}, u32[]{:S(2)}) %collective-permute-start.5) | collective-permute-done | bytes 262176 | tf_op jit(solution)/shard_map/ppermute | solution.py:381
  45.4 0.0 collective-permute-start.6
  45.4 0.0 collective-permute-done.2.refs_5_.refs_7_
  45.4 0.0 all-to-all-done
  45.4 0.0 collective-permute-done.4.refs_7_.refs_9_
  45.4 0.0 copy-done.1
  45.4 9.2 %shard_map.60 = (bf16[256,2048]{1,0:T(8,128)(2,1)S(1)}, f32[8,128,256]{2,1,0:T(8,128)S(1)}, f32[8,1,256]{2,1,0:T(1,128)S(1)}, f32[8,8,256]{2,1,0:T(8,128)S(1)}) custom-call(s32[1,4]{1,0:T(1,128)S(1)} %copy-done.1, bf16[256,512]{1,0:T(8,128)(2,1)S(1)} %shard_map.55.picks_ref.refs_1_, bf16[512,1024]{1,0:T(8,128)(2,1)S(1)} %bitcast.7, ...), custom_call_target="tpu_custom_call" | custom-call | flops 2684354560 | bytes 2097152 | tf_op jit(solution)/shard_map/pallas_call | solution.py:414
  54.6 0.0 collective-permute-done.6.refs_11_
  54.6 3.2 %shard_map.61 = bf16[256,1024]{1,0:T(8,128)(2,1)} custom-call(s32[1,4]{1,0:T(1,128)S(1)} %copy-done.1, bf16[256,2048]{1,0:T(8,128)(2,1)S(1)} %get-tuple-element.9.refs_1_, f32[8,128,256]{2,1,0:T(8,128)S(1)} %get-tuple-element.10.refs_2_, f32[8,1,256]{2,1,0:T(1,128)S(1)} %get-tuple-element.11.refs_3_, f32[8,8,256]{2,1,0:T(8,128)S(1)} %get-tuple-element.12.refs_4_, ...), custom_call_target="tpu_custom_call" | custom-call | flops 536870912 | bytes 2097152 | tf_op jit(solution)/shard_map/pallas_call | solution.py:430
  (1 shorter events, 0.0 us)
Async XLA Ops:
  2.0 11.4 %all-to-all-start.1 = ((bf16[16,32,256]{2,1,0:T(8,128)(2,1)}), bf16[16,32,256]{2,1,0:T(8,128)(2,1)S(1)}, u32[]{:S(2)}, u32[]{:S(2)}) async-start(bf16[16,32,256]{2,1,0:T(8,128)(2,1)} %bitcast.10), calls=%async_computation.1 | async-start | bytes 524288 | tf_op jit(solution)/shard_map/all_to_all | solution.py:349
  13.4 6.6 %copy-start = (s32[1,256]{1,0:T(1,128)S(1)}, s32[1,256]{1,0:T(1,128)}, u32[]{:S(2)}) copy-start(s32[1,256]{1,0:T(1,128)} %source_ref.1) | copy-start | bytes 3076
  13.4 32.0 %all-to-all-start = ((bf16[16,32,1024]{2,1,0:T(8,128)(2,1)}), bf16[16,32,1024]{2,1,0:T(8,128)(2,1)S(1)}, u32[]{:S(2)}, u32[]{:S(2)}) async-start(bf16[16,32,1024]{2,1,0:T(8,128)(2,1)} %bitcast.9), calls=%async_computation | async-start | bytes 2097152 | tf_op jit(solution)/shard_map/all_to_all | solution.py:349
  20.5 3.4 %collective-permute-start = (bf16[256,256]{1,0:T(8,128)(2,1)S(1)}, bf16[256,256]{1,0:T(8,128)(2,1)S(1)}, u32[]{:S(2)}, u32[]{:S(2)}) collective-permute-start(bf16[256,256]{1,0:T(8,128)(2,1)S(1)} %shard_map.58.own_ref), channel_id=1, source_target_pairs={{0,1},{1,0},{2,3},{3,2},{4,5},{5,4},{6,7},{7,6},{8,9},{9,8},{10,11... | collective-permute-start | bytes 393224 | tf_op jit(solution)/shard_map/ppermute | solution.py:388
  23.9 21.5 %copy-start.1 = (s32[1,4]{1,0:T(1,128)S(1)}, s32[1,4]{1,0:T(1,128)}, u32[]{:S(2)}) copy-start(s32[1,4]{1,0:T(1,128)} %refs_0_.3) | copy-start | bytes 52
  24.0 10.4 %collective-permute-start.1 = (bf16[512,256]{1,0:T(8,128)(2,1)S(1)}, bf16[512,256]{1,0:T(8,128)(2,1)S(1)}, u32[]{:S(2)}, u32[]{:S(2)}) collective-permute-start(bf16[512,256]{1,0:T(8,128)(2,1)S(1)} %shard_map.59.refs_3_.refs_5_), channel_id=1, source_target_pairs={{0,2},{1,13},{2,4},{3,15},{4,6},{5,1},{6,8},{7,3},{8,10},{9,5},{10... | collective-permute-start | bytes 786440 | tf_op jit(solution)/shard_map/ppermute | solution.py:381
  34.3 5.5 %collective-permute-start.3 = (bf16[512,256]{1,0:T(8,128)(2,1)S(1)}, bf16[512,256]{1,0:T(8,128)(2,1)S(1)}, u32[]{:S(2)}, u32[]{:S(2)}) collective-permute-start(bf16[512,256]{1,0:T(8,128)(2,1)S(1)} %collective-permute-done.1.refs_4_.refs_6_), channel_id=1, source_target_pairs={{0,2},{1,15},{2,4},{3,1},{4,6},{5,3},{6,8},{7,5},{8,10},{9,7},{10,... | collective-permute-start | bytes 786440 | tf_op jit(solution)/shard_map/ppermute | solution.py:381
  34.3 11.1 %collective-permute-start.5 = (bf16[512,256]{1,0:T(8,128)(2,1)S(1)}, bf16[512,256]{1,0:T(8,128)(2,1)S(1)}, u32[]{:S(2)}, u32[]{:S(2)}) collective-permute-start(bf16[512,256]{1,0:T(8,128)(2,1)S(1)} %collective-permute-done.1.refs_4_.refs_6_), channel_id=1, source_target_pairs={{0,4},{1,13},{2,6},{3,15},{4,8},{5,1},{6,10},{7,3},{8,12},{9,5},{1... | collective-permute-start | bytes 786440 | tf_op jit(solution)/shard_map/ppermute | solution.py:381
  34.4 10.9 %collective-permute-start.2 = (bf16[512,256]{1,0:T(8,128)(2,1)S(1)}, bf16[512,256]{1,0:T(8,128)(2,1)S(1)}, u32[]{:S(2)}, u32[]{:S(2)}) collective-permute-start(bf16[512,256]{1,0:T(8,128)(2,1)S(1)} %collective-permute-done.1.refs_4_.refs_6_), channel_id=1, source_target_pairs={{0,1},{1,0},{2,3},{3,2},{4,5},{5,4},{6,7},{7,6},{8,9},{9,8},{10,11... | collective-permute-start | bytes 786440 | tf_op jit(solution)/shard_map/ppermute | solution.py:388
  39.8 5.6 %collective-permute-start.4 = (bf16[512,256]{1,0:T(8,128)(2,1)S(1)}, bf16[512,256]{1,0:T(8,128)(2,1)S(1)}, u32[]{:S(2)}, u32[]{:S(2)}) collective-permute-start(bf16[512,256]{1,0:T(8,128)(2,1)S(1)} %collective-permute-done.3.refs_6_.refs_8_), channel_id=1, source_target_pairs={{0,1},{1,0},{2,3},{3,2},{4,5},{5,4},{6,7},{7,6},{8,9},{9,8},{10,11... | collective-permute-start | bytes 786440 | tf_op jit(solution)/shard_map/ppermute | solution.py:388
  45.4 9.2 %collective-permute-start.6 = (bf16[512,256]{1,0:T(8,128)(2,1)S(1)}, bf16[512,256]{1,0:T(8,128)(2,1)S(1)}, u32[]{:S(2)}, u32[]{:S(2)}) collective-permute-start(bf16[512,256]{1,0:T(8,128)(2,1)S(1)} %collective-permute-done.5.refs_8_.refs_10_), channel_id=1, source_target_pairs={{0,1},{1,0},{2,3},{3,2},{4,5},{5,4},{6,7},{7,6},{8,9},{9,8},{10,11... | collective-permute-start | bytes 786440 | tf_op jit(solution)/shard_map/ppermute | solution.py:388

commit v3 on v2

--- a/solution.py
+++ b/solution.py
@@ -26,14 +26,33 @@
     return labels * capacity + rank.astype(jnp.int32)
 
 
-def pack_kernel(owners, capacity, dest_ref, rows_ref, out_ref):
-    slots = slots_of(dest_ref[...], owners, capacity)
-    n = slots.shape[1]
-    hot = lax.broadcasted_iota(jnp.int32, (owners * capacity, n), 0) == slots
-    picks = jnp.where(hot, 1.0, 0.0).astype(jnp.bfloat16)
-    out_ref[...] = jnp.dot(
-        picks, rows_ref[...], preferred_element_type=jnp.float32
-    ).astype(out_ref.dtype)
+def pack_kernel(owners, capacity, dest_hbm, rows_hbm, out_hbm, dest, rows, packed, sems):
+    slots = owners * capacity
+    n = rows.shape[0]
+    fetch_dest = pltpu.make_async_copy(dest_hbm, dest, sems.at[0])
+    fetch_rows = pltpu.make_async_copy(rows_hbm, rows, sems.at[1])
+    fetch_dest.start()
+    fetch_rows.start()
+    fetch_dest.wait()
+    slot = slots_of(dest[...], owners, capacity)
+    half = slots // 2
+    hot = [
+        half * i + lax.broadcasted_iota(jnp.int32, (half, n), 0) == slot for i in range(2)
+    ]
+    picks = [jnp.where(h, 1.0, 0.0).astype(jnp.bfloat16) for h in hot]
+    fetch_rows.wait()
+    puts = []
+    for i in range(2):
+        part = pl.ds(half * i, half)
+        packed[part, :] = jnp.dot(
+            picks[i], rows[...], preferred_element_type=jnp.float32
+        ).astype(packed.dtype)
+        puts.append(
+            pltpu.make_async_copy(packed.at[part, :], out_hbm.at[part, :], sems.at[2 + i])
+        )
+        puts[i].start()
+    for put in puts:
+        put.wait()
 
 
 def picks_of(source_ref, owners, capacity):
@@ -199,9 +218,10 @@
 
 def attend_kernel(head, far, *refs):
     lengths_ref, picks_ref, got_ref = refs[:3]
-    near = refs[3:-6]
-    q_all, acc, top, total, kv, at_of = refs[-6:]
+    near = refs[3:-9]
+    out_ref, kv, q_all, acc, top, total, done, at_of, sems = refs[-9:]
     n = picks_ref.shape[0]
+    groups = acc.shape[0]
     chunk = 2 * n
     split_query(head, picks_ref[...], got_ref, q_all)
     block = block_of(head, far, lengths_ref, kv, q_all, acc, top, total)
@@ -253,39 +273,6 @@
         def _():
             block.step(slot * chunk, chunk, at, True, "fixed")
 
-
-def finish_kernel(head, far, *refs):
-    lengths_ref, q_all, acc_ref, top_ref, total_ref = refs[:5]
-    near = refs[5:-5]
-    out_ref, kv, acc, top, total = refs[-5:]
-    n = q_all.shape[0]
-    groups = acc.shape[0]
-    chunk = 2 * n
-    acc[...] = acc_ref[...]
-    top[...] = top_ref[...]
-    total[...] = total_ref[...]
-    block = block_of(head, far, lengths_ref, kv, q_all, acc, top, total)
-    at = block.place(len(near) - 1)
-    is_here = block.here(at)
-    is_clear = block.clear(at)
-    is_late = block.late(at)
-
-    @pl.when(is_here)
-    def _():
-        kv[...] = near[-1][...]
-
-    @pl.when(is_here & is_clear)
-    def _():
-        block.step(0, chunk, at, False, "fixed")
-
-    @pl.when(is_here & jnp.logical_not(is_clear) & is_late)
-    def _():
-        block.step(n, n, at + n, True, "fixed")
-
-    @pl.when(is_here & jnp.logical_not(is_clear | is_late))
-    def _():
-        block.step(0, chunk, at, True, "fixed")
-
     most = total[0]
     for h in range(1, groups):
         most = jnp.maximum(most, total[h])
@@ -299,23 +286,29 @@
 
         @pl.loop(0, len(near))
         def _(i):
-            place = block.place(0)
+            at = block.place(0)
             for j, ref in enumerate(near):
-                place = jnp.where(i == j, block.place(j), place)
+                at = jnp.where(i == j, block.place(j), at)
 
                 @pl.when(i == j)
                 def _():
-                    kv[...] = ref[...]
-
-            @pl.when(block.here(place))
+                    kv[0:chunk] = ref[...]
+
+            @pl.when(block.here(at))
             def _():
-                block.step(0, chunk, place, True, "running")
-
+                block.step(0, chunk, at, True, "running")
+
+    copies = []
     for h in range(groups):
+        columns = pl.ds(h * head, head)
         share = 1.0 / jnp.sum(total[h], axis=0, keepdims=True)
-        out_ref[:, h * head : (h + 1) * head] = jnp.transpose(
-            (acc[h] * share).astype(out_ref.dtype)
+        done[:, columns] = jnp.transpose((acc[h] * share).astype(done.dtype))
+        copies.append(
+            pltpu.make_async_copy(done.at[:, columns], out_ref.at[:, columns], sems.at[h])
         )
+        copies[-1].start()
+    for copy in copies:
+        copy.wait()
 
 
 def vmem(count):
@@ -336,8 +329,14 @@
         return pl.pallas_call(
             functools.partial(pack_kernel, owners, capacity),
             out_shape=jax.ShapeDtypeStruct((slots, rows.shape[1]), rows.dtype),
-            in_specs=vmem(2),
-            out_specs=vmem(1)[0],
+            in_specs=[pl.BlockSpec(memory_space=pl.ANY)] * 2,
+            out_specs=pl.BlockSpec(memory_space=pl.ANY),
+            scratch_shapes=[
+                pltpu.VMEM(dest_bin.shape, dest_bin.dtype),
+                pltpu.VMEM(rows.shape, rows.dtype),
+                pltpu.VMEM((slots, rows.shape[1]), rows.dtype),
+                pltpu.SemaphoreType.DMA((4,)),
+            ],
             cost_estimate=pl.CostEstimate(
                 flops=2 * slots * n * rows.shape[1],
                 bytes_accessed=6 * n * rows.shape[1],
@@ -401,50 +400,31 @@
     hop2 = hop(hop1, 1, 1)
     hop3 = hop(hop1, 2, 2)
     far = [(0, 0), (1, 6), (6, 1), (2, 5), (5, 2), (3, 4), (4, 3)]
-    last = swap(hop3)
-    pieces = [pair, hop1, swap(hop1), hop2, swap(hop2), hop3, last]
+    pieces = [pair, hop1, swap(hop1), hop2, swap(hop2), hop3, swap(hop3)]
     groups = width // head
-    state = (
-        jax.ShapeDtypeStruct((n, 2 * width), queries.dtype),
-        jax.ShapeDtypeStruct((groups, head, n), jnp.float32),
-        jax.ShapeDtypeStruct((groups, 1, n), jnp.float32),
-        jax.ShapeDtypeStruct((groups, 8, n), jnp.float32),
-    )
-
-    sums = pl.pallas_call(
+
+    attended = pl.pallas_call(
         functools.partial(attend_kernel, head, far),
-        out_shape=state,
-        in_specs=[pl.BlockSpec(memory_space=pltpu.SMEM)] + vmem(1 + len(far)),
-        out_specs=tuple(vmem(len(state))),
+        out_shape=jax.ShapeDtypeStruct((n, width), queries.dtype),
+        in_specs=[pl.BlockSpec(memory_space=pltpu.SMEM)] + vmem(2 + len(far)),
+        out_specs=pl.BlockSpec(memory_space=pl.ANY),
         scratch_shapes=[
-            pltpu.VMEM((2 * n * (len(far) - 1), kv_width), keyvals.dtype),
+            pltpu.VMEM((2 * n * len(far), kv_width), keyvals.dtype),
+            pltpu.VMEM((n, 2 * width), queries.dtype),
+            pltpu.VMEM((groups, head, n), jnp.float32),
+            pltpu.VMEM((groups, 1, n), jnp.float32),
+            pltpu.VMEM((groups, 8, n), jnp.float32),
+            pltpu.VMEM((n, width), queries.dtype),
             pltpu.SMEM((len(far),), jnp.int32),
+            pltpu.SemaphoreType.DMA((groups,)),
         ],
-        compiler_params=pltpu.CompilerParams(vmem_limit_bytes=24 << 20),
+        compiler_params=pltpu.CompilerParams(vmem_limit_bytes=28 << 20),
         cost_estimate=pl.CostEstimate(
-            flops=4 * n * width * 10 * n,
+            flops=4 * n * width * 12 * n,
             bytes_accessed=8 * n * width,
-            transcendentals=10 * n * n * groups,
+            transcendentals=12 * n * n * groups,
         ),
-    )(seq_lengths, picks, got_q, *pieces[:-1])
-    attended = pl.pallas_call(
-        functools.partial(finish_kernel, head, far),
-        out_shape=jax.ShapeDtypeStruct((n, width), queries.dtype),
-        in_specs=[pl.BlockSpec(memory_space=pltpu.SMEM)] + vmem(len(state) + len(far)),
-        out_specs=vmem(1)[0],
-        scratch_shapes=[
-            pltpu.VMEM((2 * n, kv_width), keyvals.dtype),
-            pltpu.VMEM(state[1].shape, jnp.float32),
-            pltpu.VMEM(state[2].shape, jnp.float32),
-            pltpu.VMEM(state[3].shape, jnp.float32),
-        ],
-        compiler_params=pltpu.CompilerParams(vmem_limit_bytes=24 << 20),
-        cost_estimate=pl.CostEstimate(
-            flops=4 * n * width * 2 * n,
-            bytes_accessed=8 * n * width,
-            transcendentals=2 * n * n * groups,
-        ),
-    )(seq_lengths, *sums, *pieces)
+    )(seq_lengths, picks, got_q, *pieces)
     return attended.reshape(1, n, width)
 
 

time: 58 us -> 59 us (1.017)
  waiting for transfers between devices: 23 us -> 24.8 us
  Pallas kernels: 17.5 us -> 16.6 us
    ppermute x4, waiting for transfers between devices: 0.99 us -> 2.5 us  [swap(): return lax.ppermute(x, 'ctx', [(c, c ^ 1) for c in range(n_ctx)])]
    pallas_call x2 -> x1, Pallas kernels: 12.3 us -> 11.8 us  [body(): pl.pallas_call(functools.partial(attend_kernel, head, far), out_shape=jax...]
  transfers between devices with their start and end apart: 9 -> 9, of which waited for: 5 -> 6; matrix products, arithmetic and copies ran while one was open for 0% -> 0% of each run, Pallas kernels for 21% -> 5%
where the time goes in v3:
time: 59 us; the launch traced here: 58.7 us
  waiting for transfers between devices  24.8 us (42%)
  starting transfers between devices  17.1 us (29%)
  Pallas kernels  16.6 us (28%)
    ppermute x3, waiting for transfers between devices, hop(): lax.ppermute(x, 'ctx', [(c, (c + (2 * up if c % 2 == 0 else -2 * down)) %...  20 us
    all_to_all x2, starting transfers between devices, exchange(): lax.all_to_all(rows.reshape(owners, capacity, rows.shape[1]), 'dp', split...  13.3 us
    pallas_call x1, Pallas kernels, body(): pl.pallas_call(functools.partial(attend_kernel, head, far), out_shape=jax...  11.8 us
    pallas_call x2, Pallas kernels, pack(): pl.pallas_call(functools.partial(pack_kernel, owners, capacity), out_shap...  4.26 us
    ppermute x4, waiting for transfers between devices, swap(): return lax.ppermute(x, 'ctx', [(c, c ^ 1) for c in range(n_ctx)])  2.5 us
    ppermute x4, starting transfers between devices, swap(): return lax.ppermute(x, 'ctx', [(c, c ^ 1) for c in range(n_ctx)])  2.43 us
    all_to_all x2, waiting for transfers between devices, exchange(): lax.all_to_all(rows.reshape(owners, capacity, rows.shape[1]), 'dp', split...  2.26 us
    ppermute x3, starting transfers between devices, hop(): lax.ppermute(x, 'ctx', [(c, (c + (2 * up if c % 2 == 0 else -2 * down)) %...  1.38 us
  transfers between devices with their start and end apart: 9, of which 6 were waited for; matrix products, arithmetic and copies ran while one was open for 0% of the time, Pallas kernels for 5%

profile of v3, /device:TPU:205, one launch (start us, length us, event | category | flops | bytes accessed | tf_op | source)
XLA Modules:
  0.0 58.7 jit_solution(6188923107145368413)
XLA Ops:
  0.0 1.9 %shard_map.57 = bf16[512,256]{1,0:T(8,128)(2,1)} custom-call(s32[1,256]{1,0:T(1,128)} %dest_hbm.3, bf16[256,256]{1,0:T(8,128)(2,1)} %bitcast.12), custom_call_target="tpu_custom_call" | custom-call | flops 67108864 | bytes 393216 | tf_op jit(solution)/shard_map/pallas_call | solution.py:329
  1.9 6.8 %all-to-all-start.1 = ((bf16[16,32,256]{2,1,0:T(8,128)(2,1)}), bf16[16,32,256]{2,1,0:T(8,128)(2,1)S(1)}, u32[]{:S(2)}, u32[]{:S(2)}) async-start(bf16[16,32,256]{2,1,0:T(8,128)(2,1)} %bitcast.10), calls=%async_computation.1 | async-start | bytes 524288 | tf_op jit(solution)/shard_map/all_to_all | solution.py:348
  8.7 2.4 %shard_map.56 = bf16[512,1024]{1,0:T(8,128)(2,1)} custom-call(s32[1,256]{1,0:T(1,128)} %dest_hbm.3, bf16[256,1024]{1,0:T(8,128)(2,1)} %bitcast.11), custom_call_target="tpu_custom_call" | custom-call | flops 268435456 | bytes 1572864 | tf_op jit(solution)/shard_map/pallas_call | solution.py:329
  11.1 2.3 %all-to-all-done.1 = bf16[16,32,256]{2,1,0:T(8,128)(2,1)S(1)} async-done(((bf16[16,32,256]{2,1,0:T(8,128)(2,1)}), bf16[16,32,256]{2,1,0:T(8,128)(2,1)S(1)}, u32[]{:S(2)}, u32[]{:S(2)}) %all-to-all-start.1) | async-done | bytes 262176 | tf_op jit(solution)/shard_map/all_to_all | solution.py:348
  13.3 0.0 copy-start
  13.3 6.5 %all-to-all-start = ((bf16[16,32,1024]{2,1,0:T(8,128)(2,1)}), bf16[16,32,1024]{2,1,0:T(8,128)(2,1)S(1)}, u32[]{:S(2)}, u32[]{:S(2)}) async-start(bf16[16,32,1024]{2,1,0:T(8,128)(2,1)} %bitcast.9), calls=%async_computation | async-start | bytes 2097152 | tf_op jit(solution)/shard_map/all_to_all | solution.py:348
  19.9 0.0 copy-done
  19.9 0.3 shard_map.55.picks_ref.refs_1_
  20.2 0.2 shard_map.58.own_ref
  20.4 2.4 %collective-permute-start = (bf16[256,256]{1,0:T(8,128)(2,1)S(1)}, bf16[256,256]{1,0:T(8,128)(2,1)S(1)}, u32[]{:S(2)}, u32[]{:S(2)}) collective-permute-start(bf16[256,256]{1,0:T(8,128)(2,1)S(1)} %shard_map.58.own_ref), channel_id=1, source_target_pairs={{0,1},{1,0},{2,3},{3,2},{4,5},{5,4},{6,7},{7,6},{8,9},{9,8},{10,11... | collective-permute-start | bytes 393224 | tf_op jit(solution)/shard_map/ppermute | solution.py:387
  22.8 1.0 %collective-permute-done.other_ref = bf16[256,256]{1,0:T(8,128)(2,1)S(1)} collective-permute-done((bf16[256,256]{1,0:T(8,128)(2,1)S(1)}, bf16[256,256]{1,0:T(8,128)(2,1)S(1)}, u32[]{:S(2)}, u32[]{:S(2)}) %collective-permute-start) | collective-permute-done | bytes 131104 | tf_op jit(solution)/shard_map/ppermute | solution.py:387
  23.8 0.0 copy-start.1
  23.9 1.3 %collective-permute-start.1 = (bf16[512,256]{1,0:T(8,128)(2,1)S(1)}, bf16[512,256]{1,0:T(8,128)(2,1)S(1)}, u32[]{:S(2)}, u32[]{:S(2)}) collective-permute-start(bf16[512,256]{1,0:T(8,128)(2,1)S(1)} %shard_map.59.refs_3_), channel_id=1, source_target_pairs={{0,2},{1,13},{2,4},{3,15},{4,6},{5,1},{6,8},{7,3},{8,10},{9,5},{10... | collective-permute-start | bytes 786440 | tf_op jit(solution)/shard_map/ppermute | solution.py:380
  25.1 9.1 %collective-permute-done.1.refs_4_ = bf16[512,256]{1,0:T(8,128)(2,1)S(1)} collective-permute-done((bf16[512,256]{1,0:T(8,128)(2,1)S(1)}, bf16[512,256]{1,0:T(8,128)(2,1)S(1)}, u32[]{:S(2)}, u32[]{:S(2)}) %collective-permute-start.1) | collective-permute-done | bytes 262176 | tf_op jit(solution)/shard_map/ppermute | solution.py:380
  34.2 0.0 collective-permute-start.3
  34.2 0.1 collective-permute-start.5
  34.3 0.0 collective-permute-start.2
  34.3 5.4 %collective-permute-done.3.refs_6_ = bf16[512,256]{1,0:T(8,128)(2,1)S(1)} collective-permute-done((bf16[512,256]{1,0:T(8,128)(2,1)S(1)}, bf16[512,256]{1,0:T(8,128)(2,1)S(1)}, u32[]{:S(2)}, u32[]{:S(2)}) %collective-permute-start.3) | collective-permute-done | bytes 262176 | tf_op jit(solution)/shard_map/ppermute | solution.py:380
  39.7 0.0 collective-permute-start.4
  39.7 5.5 %collective-permute-done.5.refs_8_ = bf16[512,256]{1,0:T(8,128)(2,1)S(1)} collective-permute-done((bf16[512,256]{1,0:T(8,128)(2,1)S(1)}, bf16[512,256]{1,0:T(8,128)(2,1)S(1)}, u32[]{:S(2)}, u32[]{:S(2)}) %collective-permute-start.5) | collective-permute-done | bytes 262176 | tf_op jit(solution)/shard_map/ppermute | solution.py:380
  45.3 0.0 collective-permute-start.6
  45.3 0.0 collective-permute-done.2.refs_5_
  45.3 0.0 all-to-all-done
  45.3 0.0 collective-permute-done.4.refs_7_
  45.3 1.5 %collective-permute-done.6.refs_9_ = bf16[512,256]{1,0:T(8,128)(2,1)S(1)} collective-permute-done((bf16[512,256]{1,0:T(8,128)(2,1)S(1)}, bf16[512,256]{1,0:T(8,128)(2,1)S(1)}, u32[]{:S(2)}, u32[]{:S(2)}) %collective-permute-start.6) | collective-permute-done | bytes 262176 | tf_op jit(solution)/shard_map/ppermute | solution.py:387
  46.8 0.0 copy-done.1
  46.8 11.8 %shard_map.60 = bf16[256,1024]{1,0:T(8,128)(2,1)} custom-call(s32[1,4]{1,0:T(1,128)S(1)} %copy-done.1, bf16[256,512]{1,0:T(8,128)(2,1)S(1)} %shard_map.55.picks_ref.refs_1_, bf16[512,1024]{1,0:T(8,128)(2,1)S(1)} %bitcast.7, bf16[512,256]{1,0:T(8,128)(2,1)S(1)} %shard_map.59.refs_3_, bf16[512,256]{1,0:T(8,128)(2,1)S(1)} %collective-permute-done.1.refs_4_, ...), custom_call_target="tpu_custom_call" | custom-call | flops 3221225472 | bytes 2097152 | tf_op jit(solution)/shard_map/pallas_call | solution.py:406
  (1 shorter events, 0.0 us)
Async XLA Ops:
  1.9 11.4 %all-to-all-start.1 = ((bf16[16,32,256]{2,1,0:T(8,128)(2,1)}), bf16[16,32,256]{2,1,0:T(8,128)(2,1)S(1)}, u32[]{:S(2)}, u32[]{:S(2)}) async-start(bf16[16,32,256]{2,1,0:T(8,128)(2,1)} %bitcast.10), calls=%async_computation.1 | async-start | bytes 524288 | tf_op jit(solution)/shard_map/all_to_all | solution.py:348
  13.3 6.5 %copy-start = (s32[1,256]{1,0:T(1,128)S(1)}, s32[1,256]{1,0:T(1,128)}, u32[]{:S(2)}) copy-start(s32[1,256]{1,0:T(1,128)} %source_ref.1) | copy-start | bytes 3076
  13.3 31.9 %all-to-all-start = ((bf16[16,32,1024]{2,1,0:T(8,128)(2,1)}), bf16[16,32,1024]{2,1,0:T(8,128)(2,1)S(1)}, u32[]{:S(2)}, u32[]{:S(2)}) async-start(bf16[16,32,1024]{2,1,0:T(8,128)(2,1)} %bitcast.9), calls=%async_computation | async-start | bytes 2097152 | tf_op jit(solution)/shard_map/all_to_all | solution.py:348
  20.4 3.4 %collective-permute-start = (bf16[256,256]{1,0:T(8,128)(2,1)S(1)}, bf16[256,256]{1,0:T(8,128)(2,1)S(1)}, u32[]{:S(2)}, u32[]{:S(2)}) collective-permute-start(bf16[256,256]{1,0:T(8,128)(2,1)S(1)} %shard_map.58.own_ref), channel_id=1, source_target_pairs={{0,1},{1,0},{2,3},{3,2},{4,5},{5,4},{6,7},{7,6},{8,9},{9,8},{10,11... | collective-permute-start | bytes 393224 | tf_op jit(solution)/shard_map/ppermute | solution.py:387
  23.8 23.0 %copy-start.1 = (s32[1,4]{1,0:T(1,128)S(1)}, s32[1,4]{1,0:T(1,128)}, u32[]{:S(2)}) copy-start(s32[1,4]{1,0:T(1,128)} %refs_0_.1) | copy-start | bytes 52
  23.9 10.4 %collective-permute-start.1 = (bf16[512,256]{1,0:T(8,128)(2,1)S(1)}, bf16[512,256]{1,0:T(8,128)(2,1)S(1)}, u32[]{:S(2)}, u32[]{:S(2)}) collective-permute-start(bf16[512,256]{1,0:T(8,128)(2,1)S(1)} %shard_map.59.refs_3_), channel_id=1, source_target_pairs={{0,2},{1,13},{2,4},{3,15},{4,6},{5,1},{6,8},{7,3},{8,10},{9,5},{10... | collective-permute-start | bytes 786440 | tf_op jit(solution)/shard_map/ppermute | solution.py:380
  34.2 5.5 %collective-permute-start.3 = (bf16[512,256]{1,0:T(8,128)(2,1)S(1)}, bf16[512,256]{1,0:T(8,128)(2,1)S(1)}, u32[]{:S(2)}, u32[]{:S(2)}) collective-permute-start(bf16[512,256]{1,0:T(8,128)(2,1)S(1)} %collective-permute-done.1.refs_4_), channel_id=1, source_target_pairs={{0,2},{1,15},{2,4},{3,1},{4,6},{5,3},{6,8},{7,5},{8,10},{9,7},{10,... | collective-permute-start | bytes 786440 | tf_op jit(solution)/shard_map/ppermute | solution.py:380
  34.2 11.0 %collective-permute-start.5 = (bf16[512,256]{1,0:T(8,128)(2,1)S(1)}, bf16[512,256]{1,0:T(8,128)(2,1)S(1)}, u32[]{:S(2)}, u32[]{:S(2)}) collective-permute-start(bf16[512,256]{1,0:T(8,128)(2,1)S(1)} %collective-permute-done.1.refs_4_), channel_id=1, source_target_pairs={{0,4},{1,13},{2,6},{3,15},{4,8},{5,1},{6,10},{7,3},{8,12},{9,5},{1... | collective-permute-start | bytes 786440 | tf_op jit(solution)/shard_map/ppermute | solution.py:380
  34.3 10.9 %collective-permute-start.2 = (bf16[512,256]{1,0:T(8,128)(2,1)S(1)}, bf16[512,256]{1,0:T(8,128)(2,1)S(1)}, u32[]{:S(2)}, u32[]{:S(2)}) collective-permute-start(bf16[512,256]{1,0:T(8,128)(2,1)S(1)} %collective-permute-done.1.refs_4_), channel_id=1, source_target_pairs={{0,1},{1,0},{2,3},{3,2},{4,5},{5,4},{6,7},{7,6},{8,9},{9,8},{10,11... | collective-permute-start | bytes 786440 | tf_op jit(solution)/shard_map/ppermute | solution.py:387
  39.7 5.5 %collective-permute-start.4 = (bf16[512,256]{1,0:T(8,128)(2,1)S(1)}, bf16[512,256]{1,0:T(8,128)(2,1)S(1)}, u32[]{:S(2)}, u32[]{:S(2)}) collective-permute-start(bf16[512,256]{1,0:T(8,128)(2,1)S(1)} %collective-permute-done.3.refs_6_), channel_id=1, source_target_pairs={{0,1},{1,0},{2,3},{3,2},{4,5},{5,4},{6,7},{7,6},{8,9},{9,8},{10,11... | collective-permute-start | bytes 786440 | tf_op jit(solution)/shard_map/ppermute | solution.py:387
  45.3 1.5 %collective-permute-start.6 = (bf16[512,256]{1,0:T(8,128)(2,1)S(1)}, bf16[512,256]{1,0:T(8,128)(2,1)S(1)}, u32[]{:S(2)}, u32[]{:S(2)}) collective-permute-start(bf16[512,256]{1,0:T(8,128)(2,1)S(1)} %collective-permute-done.5.refs_8_), channel_id=1, source_target_pairs={{0,1},{1,0},{2,3},{3,2},{4,5},{5,4},{6,7},{7,6},{8,9},{9,8},{10,11... | collective-permute-start | bytes 786440 | tf_op jit(solution)/shard_map/ppermute | solution.py:387

commit v4 on v3

--- a/solution.py
+++ b/solution.py
@@ -216,62 +216,75 @@
     return Block(core, chip * chunk, place, here, clear, late, step)
 
 
-def attend_kernel(head, far, *refs):
-    lengths_ref, picks_ref, got_ref = refs[:3]
-    near = refs[3:-9]
-    out_ref, kv, q_all, acc, top, total, done, at_of, sems = refs[-9:]
-    n = picks_ref.shape[0]
+def part_kernel(head, far, first, final, *refs):
+    lengths_ref = refs[0]
+    if first:
+        picks_ref, got_ref = refs[1:3]
+        near = refs[3 : 3 + len(far)]
+        q_all, acc, top, total, kv = refs[3 + len(far) :]
+        split_query(head, picks_ref[...], got_ref, q_all)
+    else:
+        q_all, acc_ref, top_ref, total_ref = refs[1:5]
+        near = refs[5 : 5 + len(far)]
+        if final:
+            out_ref, kv, acc, top, total, done, sems = refs[5 + len(far) :]
+            top[...] = top_ref[...]
+        else:
+            acc, total, kv = refs[5 + len(far) :]
+            top = top_ref
+        acc[...] = acc_ref[...]
+        total[...] = total_ref[...]
+    n = q_all.shape[0]
     groups = acc.shape[0]
     chunk = 2 * n
-    split_query(head, picks_ref[...], got_ref, q_all)
     block = block_of(head, far, lengths_ref, kv, q_all, acc, top, total)
 
-    last = len(near) - 1
-    kv[0:chunk] = near[0][...]
-    plain = jnp.int32(0)
-    edged = jnp.int32(0)
-    for i in range(1, len(near)):
-        at = block.place(i)
+    def place(i, count):
+        at = block.place(0)
+        for j in range(1, count):
+            at = jnp.where(i == j, block.place(j), at)
+        return at
+
+    skip = 1 if first else 0
+    fresh = kv.shape[0] // chunk
+    names = far[:fresh]
+    for i in range(len(names)):
+
+        @pl.when(block.here(block.place(i)))
+        def _():
+            kv[i * chunk : (i + 1) * chunk] = near[i][...]
+
+    if first:
+
+        @pl.when(block.core == 0)
+        def _():
+            block.step(0, n, block.own, True, "first")
+
+        @pl.when(block.core != 0)
+        def _():
+            block.step(0, chunk, block.own, True, "first")
+
+    @pl.loop(skip, len(names))
+    def _(i):
+        at = place(i, len(names))
         is_here = block.here(at)
         is_clear = block.clear(at)
-        slot = jnp.where(is_clear, 1 + plain, last - edged)
-
-        @pl.when(is_here)
-        def _():
-            kv[pl.ds(pl.multiple_of(slot * chunk, chunk), chunk)] = near[i][...]
-            at_of[slot] = at
-
-        plain += jnp.where(is_here & is_clear, 1, 0)
-        edged += jnp.where(is_here & jnp.logical_not(is_clear), 1, 0)
-
-    @pl.when(block.core == 0)
-    def _():
-        block.step(0, n, block.own, True, "first")
-
-    @pl.when(block.core != 0)
-    def _():
-        block.step(0, chunk, block.own, True, "first")
-
-    @pl.loop(0, plain // 2)
-    def _(p):
-        block.step((1 + 2 * p) * chunk, 2 * chunk, 0, False, "fixed")
-
-    @pl.when(lax.rem(plain, 2) == 1)
-    def _():
-        block.step(plain * chunk, chunk, 0, False, "fixed")
-
-    @pl.loop(0, edged)
-    def _(j):
-        slot = last - j
-        at = at_of[slot]
-
-        @pl.when(block.late(at))
-        def _():
-            block.step(slot * chunk + n, n, at + n, True, "fixed")
-
-        @pl.when(jnp.logical_not(block.late(at)))
-        def _():
-            block.step(slot * chunk, chunk, at, True, "fixed")
+        is_late = block.late(at)
+
+        @pl.when(is_here & is_clear)
+        def _():
+            block.step(i * chunk, chunk, at, False, "fixed")
+
+        @pl.when(is_here & jnp.logical_not(is_clear) & is_late)
+        def _():
+            block.step(i * chunk + n, n, at + n, True, "fixed")
+
+        @pl.when(is_here & jnp.logical_not(is_clear | is_late))
+        def _():
+            block.step(i * chunk, chunk, at, True, "fixed")
+
+    if not final:
+        return
 
     most = total[0]
     for h in range(1, groups):
@@ -284,11 +297,11 @@
             total[h] = jnp.zeros(total.shape[1:], jnp.float32)
             acc[h] = jnp.zeros(acc.shape[1:], jnp.float32)
 
-        @pl.loop(0, len(near))
-        def _(i):
-            at = block.place(0)
+        @pl.loop(0, len(far))
+        def _(t):
+            i = len(far) - 1 - t
+            at = place(i, len(far))
             for j, ref in enumerate(near):
-                at = jnp.where(i == j, block.place(j), at)
 
                 @pl.when(i == j)
                 def _():
@@ -372,7 +385,9 @@
         out_specs=vmem(1)[0],
         compiler_params=pltpu.CompilerParams(vmem_limit_bytes=12 << 20),
         cost_estimate=pl.CostEstimate(
-            flops=2 * slots * n * kv_width, bytes_accessed=6 * n * kv_width, transcendentals=0
+            flops=2 * slots * n * kv_width,
+            bytes_accessed=6 * n * kv_width,
+            transcendentals=0,
         ),
     )(picks, got_kv)
 
@@ -399,32 +414,49 @@
     hop1 = hop(pair, 1, 2)
     hop2 = hop(hop1, 1, 1)
     hop3 = hop(hop1, 2, 2)
-    far = [(0, 0), (1, 6), (6, 1), (2, 5), (5, 2), (3, 4), (4, 3)]
-    pieces = [pair, hop1, swap(hop1), hop2, swap(hop2), hop3, swap(hop3)]
     groups = width // head
-
-    attended = pl.pallas_call(
-        functools.partial(attend_kernel, head, far),
-        out_shape=jax.ShapeDtypeStruct((n, width), queries.dtype),
-        in_specs=[pl.BlockSpec(memory_space=pltpu.SMEM)] + vmem(2 + len(far)),
-        out_specs=pl.BlockSpec(memory_space=pl.ANY),
-        scratch_shapes=[
-            pltpu.VMEM((2 * n * len(far), kv_width), keyvals.dtype),
-            pltpu.VMEM((n, 2 * width), queries.dtype),
-            pltpu.VMEM((groups, head, n), jnp.float32),
-            pltpu.VMEM((groups, 1, n), jnp.float32),
-            pltpu.VMEM((groups, 8, n), jnp.float32),
+    query = jax.ShapeDtypeStruct((n, 2 * width), queries.dtype)
+    sums = jax.ShapeDtypeStruct((groups, head, n), jnp.float32)
+    tops = jax.ShapeDtypeStruct((groups, 1, n), jnp.float32)
+    totals = jax.ShapeDtypeStruct((groups, 8, n), jnp.float32)
+
+    def attend(pieces, fresh, inputs, outputs, scratch, first=False, final=False):
+        return pl.pallas_call(
+            functools.partial(part_kernel, head, [f for f, _ in pieces], first, final),
+            out_shape=outputs,
+            in_specs=[pl.BlockSpec(memory_space=pltpu.SMEM)] + vmem(len(inputs) + len(pieces)),
+            out_specs=pl.BlockSpec(memory_space=pl.ANY) if final else tuple(vmem(len(outputs))),
+            scratch_shapes=[pltpu.VMEM((2 * n * fresh, kv_width), keyvals.dtype)] + scratch,
+            compiler_params=pltpu.CompilerParams(vmem_limit_bytes=20 << 20),
+            cost_estimate=pl.CostEstimate(
+                flops=8 * n * n * width * fresh,
+                bytes_accessed=8 * n * width,
+                transcendentals=2 * n * n * groups * fresh,
+            ),
+        )(seq_lengths, *inputs, *[x for _, x in pieces])
+
+    swapped1 = swap(hop1)
+    early = [((0, 0), pair), ((1, 6), hop1), ((6, 1), swapped1)]
+    middle = [((2, 5), hop2), ((5, 2), swap(hop2))]
+    late = [((3, 4), hop3), ((4, 3), swap(hop3))]
+    q_all, acc, top, total = attend(
+        early, 3, (picks, got_q), (query, sums, tops, totals), [], first=True
+    )
+    acc, total = attend(middle, 2, (q_all, acc, top, total), (sums, totals), [])
+    attended = attend(
+        late + middle + early[::-1],
+        2,
+        (q_all, acc, top, total),
+        jax.ShapeDtypeStruct((n, width), queries.dtype),
+        [
+            pltpu.VMEM(sums.shape, jnp.float32),
+            pltpu.VMEM(tops.shape, jnp.float32),
+            pltpu.VMEM(totals.shape, jnp.float32),
             pltpu.VMEM((n, width), queries.dtype),
-            pltpu.SMEM((len(far),), jnp.int32),
             pltpu.SemaphoreType.DMA((groups,)),
         ],
-        compiler_params=pltpu.CompilerParams(vmem_limit_bytes=28 << 20),
-        cost_estimate=pl.CostEstimate(
-            flops=4 * n * width * 12 * n,
-            bytes_accessed=8 * n * width,
-            transcendentals=12 * n * n * groups,
-        ),
-    )(seq_lengths, picks, got_q, *pieces)
+        final=True,
+    )
     return attended.reshape(1, n, width)
 
 

time: 59 us -> 58.8 us (level)
  the two profiles are of different devices: /device:TPU:205 before, /device:TPU:194 now
where the time goes in v4:
time: 58.8 us; the launch traced here: 58.5 us
  starting transfers between devices  27.1 us (46%)
  Pallas kernels  17.7 us (30%)
  waiting for transfers between devices  13.5 us (23%)
    all_to_all x2, starting transfers between devices, exchange(): lax.all_to_all(rows.reshape(owners, capacity, rows.shape[1]), 'dp', split...  13 us
    pallas_call x3, Pallas kernels, attend(): pl.pallas_call(functools.partial(part_kernel, head, [f for f, _ in pieces...  12.9 us
    ppermute x4, starting transfers between devices, swap(): return lax.ppermute(x, 'ctx', [(c, c ^ 1) for c in range(n_ctx)])  11.3 us
    ppermute x3, waiting for transfers between devices, hop(): lax.ppermute(x, 'ctx', [(c, (c + (2 * up if c % 2 == 0 else -2 * down)) %...  7.71 us
    all_to_all x2, waiting for transfers between devices, exchange(): lax.all_to_all(rows.reshape(owners, capacity, rows.shape[1]), 'dp', split...  4.42 us
    pallas_call x2, Pallas kernels, pack(): pl.pallas_call(functools.partial(pack_kernel, owners, capacity), out_shap...  4.26 us
    ppermute x3, starting transfers between devices, hop(): lax.ppermute(x, 'ctx', [(c, (c + (2 * up if c % 2 == 0 else -2 * down)) %...  2.75 us
    ppermute x4, waiting for transfers between devices, swap(): return lax.ppermute(x, 'ctx', [(c, c ^ 1) for c in range(n_ctx)])  1.34 us
  transfers between devices with their start and end apart: 9, of which 5 were waited for; matrix products, arithmetic and copies ran while one was open for 0% of the time, Pallas kernels for 19%

profile of v4, /device:TPU:194, one launch (start us, length us, event | category | flops | bytes accessed | tf_op | source)
XLA Modules:
  0.0 58.5 jit_solution(6858451986916664410)
XLA Ops:
  0.0 1.9 %shard_map.57 = bf16[512,256]{1,0:T(8,128)(2,1)} custom-call(s32[1,256]{1,0:T(1,128)} %dest_hbm.3, bf16[256,256]{1,0:T(8,128)(2,1)} %bitcast.12), custom_call_target="tpu_custom_call" | custom-call | flops 67108864 | bytes 393216 | tf_op jit(solution)/shard_map/pallas_call | solution.py:342
  1.9 7.5 %all-to-all-start.1 = ((bf16[16,32,256]{2,1,0:T(8,128)(2,1)}), bf16[16,32,256]{2,1,0:T(8,128)(2,1)S(1)}, u32[]{:S(2)}, u32[]{:S(2)}) async-start(bf16[16,32,256]{2,1,0:T(8,128)(2,1)} %bitcast.10), calls=%async_computation.1 | async-start | bytes 524288 | tf_op jit(solution)/shard_map/all_to_all | solution.py:361
  9.4 2.4 %shard_map.56 = bf16[512,1024]{1,0:T(8,128)(2,1)} custom-call(s32[1,256]{1,0:T(1,128)} %dest_hbm.3, bf16[256,1024]{1,0:T(8,128)(2,1)} %bitcast.11), custom_call_target="tpu_custom_call" | custom-call | flops 268435456 | bytes 1572864 | tf_op jit(solution)/shard_map/pallas_call | solution.py:342
  11.8 4.4 %all-to-all-done.1 = bf16[16,32,256]{2,1,0:T(8,128)(2,1)S(1)} async-done(((bf16[16,32,256]{2,1,0:T(8,128)(2,1)}), bf16[16,32,256]{2,1,0:T(8,128)(2,1)S(1)}, u32[]{:S(2)}, u32[]{:S(2)}) %all-to-all-start.1) | async-done | bytes 262176 | tf_op jit(solution)/shard_map/all_to_all | solution.py:361
  16.2 0.0 copy-start
  16.2 5.5 %all-to-all-start = ((bf16[16,32,1024]{2,1,0:T(8,128)(2,1)}), bf16[16,32,1024]{2,1,0:T(8,128)(2,1)S(1)}, u32[]{:S(2)}, u32[]{:S(2)}) async-start(bf16[16,32,1024]{2,1,0:T(8,128)(2,1)} %bitcast.9), calls=%async_computation | async-start | bytes 2097152 | tf_op jit(solution)/shard_map/all_to_all | solution.py:361
  21.7 0.0 copy-done
  21.7 0.3 shard_map.55.picks_ref.refs_1_
  22.0 0.2 shard_map.58.own_ref
  22.2 0.1 collective-permute-start
  22.3 1.3 %collective-permute-done.other_ref = bf16[256,256]{1,0:T(8,128)(2,1)S(1)} collective-permute-done((bf16[256,256]{1,0:T(8,128)(2,1)S(1)}, bf16[256,256]{1,0:T(8,128)(2,1)S(1)}, u32[]{:S(2)}, u32[]{:S(2)}) %collective-permute-start) | collective-permute-done | bytes 131104 | tf_op jit(solution)/shard_map/ppermute | solution.py:402
  23.7 0.0 copy-start.1
  23.7 1.1 %collective-permute-start.1 = (bf16[512,256]{1,0:T(8,128)(2,1)S(1)}, bf16[512,256]{1,0:T(8,128)(2,1)S(1)}, u32[]{:S(2)}, u32[]{:S(2)}) collective-permute-start(bf16[512,256]{1,0:T(8,128)(2,1)S(1)} %shard_map.59.refs_3_.refs_11_), channel_id=1, source_target_pairs={{0,2},{1,13},{2,4},{3,15},{4,6},{5,1},{6,8},{7,3},{8,10},{9,5},{10... | collective-permute-start | bytes 786440 | tf_op jit(solution)/shard_map/ppermute | solution.py:395
  24.8 5.4 %collective-permute-done.1.refs_4_.refs_10_ = bf16[512,256]{1,0:T(8,128)(2,1)S(1)} collective-permute-done((bf16[512,256]{1,0:T(8,128)(2,1)S(1)}, bf16[512,256]{1,0:T(8,128)(2,1)S(1)}, u32[]{:S(2)}, u32[]{:S(2)}) %collective-permute-start.1) | collective-permute-done | bytes 262176 | tf_op jit(solution)/shard_map/ppermute | solution.py:395
  30.1 1.0 %collective-permute-start.3 = (bf16[512,256]{1,0:T(8,128)(2,1)S(1)}, bf16[512,256]{1,0:T(8,128)(2,1)S(1)}, u32[]{:S(2)}, u32[]{:S(2)}) collective-permute-start(bf16[512,256]{1,0:T(8,128)(2,1)S(1)} %collective-permute-done.1.refs_4_.refs_10_), channel_id=1, source_target_pairs={{0,2},{1,15},{2,4},{3,1},{4,6},{5,3},{6,8},{7,5},{8,10},{9,7},{10,... | collective-permute-start | bytes 786440 | tf_op jit(solution)/shard_map/ppermute | solution.py:395
  31.1 0.7 %collective-permute-start.5 = (bf16[512,256]{1,0:T(8,128)(2,1)S(1)}, bf16[512,256]{1,0:T(8,128)(2,1)S(1)}, u32[]{:S(2)}, u32[]{:S(2)}) collective-permute-start(bf16[512,256]{1,0:T(8,128)(2,1)S(1)} %collective-permute-done.1.refs_4_.refs_10_), channel_id=1, source_target_pairs={{0,4},{1,13},{2,6},{3,15},{4,8},{5,1},{6,10},{7,3},{8,12},{9,5},{1... | collective-permute-start | bytes 786440 | tf_op jit(solution)/shard_map/ppermute | solution.py:395
  31.8 2.6 %collective-permute-start.2 = (bf16[512,256]{1,0:T(8,128)(2,1)S(1)}, bf16[512,256]{1,0:T(8,128)(2,1)S(1)}, u32[]{:S(2)}, u32[]{:S(2)}) collective-permute-start(bf16[512,256]{1,0:T(8,128)(2,1)S(1)} %collective-permute-done.1.refs_4_.refs_10_), channel_id=1, source_target_pairs={{0,1},{1,0},{2,3},{3,2},{4,5},{5,4},{6,7},{7,6},{8,9},{9,8},{10,11... | collective-permute-start | bytes 786440 | tf_op jit(solution)/shard_map/ppermute | solution.py:402
  34.4 2.2 %collective-permute-done.3.refs_5_.refs_7_ = bf16[512,256]{1,0:T(8,128)(2,1)S(1)} collective-permute-done((bf16[512,256]{1,0:T(8,128)(2,1)S(1)}, bf16[512,256]{1,0:T(8,128)(2,1)S(1)}, u32[]{:S(2)}, u32[]{:S(2)}) %collective-permute-start.3) | collective-permute-done | bytes 262176 | tf_op jit(solution)/shard_map/ppermute | solution.py:395
  36.5 3.4 %collective-permute-start.4 = (bf16[512,256]{1,0:T(8,128)(2,1)S(1)}, bf16[512,256]{1,0:T(8,128)(2,1)S(1)}, u32[]{:S(2)}, u32[]{:S(2)}) collective-permute-start(bf16[512,256]{1,0:T(8,128)(2,1)S(1)} %collective-permute-done.3.refs_5_.refs_7_), channel_id=1, source_target_pairs={{0,1},{1,0},{2,3},{3,2},{4,5},{5,4},{6,7},{7,6},{8,9},{9,8},{10,11... | collective-permute-start | bytes 786440 | tf_op jit(solution)/shard_map/ppermute | solution.py:402
  39.9 0.2 collective-permute-done.5.refs_5_
  40.1 5.3 %collective-permute-start.6 = (bf16[512,256]{1,0:T(8,128)(2,1)S(1)}, bf16[512,256]{1,0:T(8,128)(2,1)S(1)}, u32[]{:S(2)}, u32[]{:S(2)}) collective-permute-start(bf16[512,256]{1,0:T(8,128)(2,1)S(1)} %collective-permute-done.5.refs_5_), channel_id=1, source_target_pairs={{0,1},{1,0},{2,3},{3,2},{4,5},{5,4},{6,7},{7,6},{8,9},{9,8},{10,11... | collective-permute-start | bytes 786440 | tf_op jit(solution)/shard_map/ppermute | solution.py:402
  45.4 0.0 collective-permute-done.2.refs_5_.refs_9_
  45.4 0.0 all-to-all-done
  45.4 0.0 copy-done.1
  45.4 4.9 %shard_map.60 = (bf16[256,2048]{1,0:T(8,128)(2,1)S(1)}, f32[8,128,256]{2,1,0:T(8,128)S(1)}, f32[8,1,256]{2,1,0:T(1,128)S(1)}, f32[8,8,256]{2,1,0:T(8,128)S(1)}) custom-call(s32[1,4]{1,0:T(1,128)S(1)} %copy-done.1, bf16[256,512]{1,0:T(8,128)(2,1)S(1)} %shard_map.55.picks_ref.refs_1_, bf16[512,1024]{1,0:T(8,128)(2,1)S(1)} %bitcast.7, ...), custom_call_target="tpu_custom_call" | custom-call | flops 1610612736 | bytes 2097152 | tf_op jit(solution)/shard_map/pallas_call | solution.py:424
  50.3 0.0 collective-permute-done.4.refs_6_.refs_8_
  50.3 3.6 %shard_map.61 = (f32[8,128,256]{2,1,0:T(8,128)S(1)}, f32[8,8,256]{2,1,0:T(8,128)S(1)}) custom-call(s32[1,4]{1,0:T(1,128)S(1)} %copy-done.1, bf16[256,2048]{1,0:T(8,128)(2,1)S(1)} %get-tuple-element.11.refs_1_, f32[8,128,256]{2,1,0:T(8,128)S(1)} %get-tuple-element.12.refs_2_, f32[8,1,256]{2,1,0:T(1,128)S(1)} %get-tuple-element.13.refs_3_, ...), custom_call_target="tpu_custom_call" | custom-call | flops 1073741824 | bytes 2097152 | tf_op jit(solution)/shard_map/pallas_call | solution.py:424
  53.9 0.0 collective-permute-done.6.refs_6_
  53.9 4.5 %shard_map.62 = bf16[256,1024]{1,0:T(8,128)(2,1)} custom-call(s32[1,4]{1,0:T(1,128)S(1)} %copy-done.1, bf16[256,2048]{1,0:T(8,128)(2,1)S(1)} %get-tuple-element.11.refs_1_, f32[8,128,256]{2,1,0:T(8,128)S(1)} %get-tuple-element.15.refs_2_, f32[8,1,256]{2,1,0:T(1,128)S(1)} %get-tuple-element.13.refs_3_, f32[8,8,256]{2,1,0:T(8,128)S(1)} %get-tuple-element.16.refs_4_, ...), custom_call_target="tpu_custom_call" | custom-call | flops 1073741824 | bytes 2097152 | tf_op jit(solution)/shard_map/pallas_call | solution.py:424
  (1 shorter events, 0.0 us)
Async XLA Ops:
  1.9 14.3 %all-to-all-start.1 = ((bf16[16,32,256]{2,1,0:T(8,128)(2,1)}), bf16[16,32,256]{2,1,0:T(8,128)(2,1)S(1)}, u32[]{:S(2)}, u32[]{:S(2)}) async-start(bf16[16,32,256]{2,1,0:T(8,128)(2,1)} %bitcast.10), calls=%async_computation.1 | async-start | bytes 524288 | tf_op jit(solution)/shard_map/all_to_all | solution.py:361
  16.2 5.5 %copy-start = (s32[1,256]{1,0:T(1,128)S(1)}, s32[1,256]{1,0:T(1,128)}, u32[]{:S(2)}) copy-start(s32[1,256]{1,0:T(1,128)} %source_ref.1) | copy-start | bytes 3076
  16.2 29.2 %all-to-all-start = ((bf16[16,32,1024]{2,1,0:T(8,128)(2,1)}), bf16[16,32,1024]{2,1,0:T(8,128)(2,1)S(1)}, u32[]{:S(2)}, u32[]{:S(2)}) async-start(bf16[16,32,1024]{2,1,0:T(8,128)(2,1)} %bitcast.9), calls=%async_computation | async-start | bytes 2097152 | tf_op jit(solution)/shard_map/all_to_all | solution.py:361
  22.2 1.4 %collective-permute-start = (bf16[256,256]{1,0:T(8,128)(2,1)S(1)}, bf16[256,256]{1,0:T(8,128)(2,1)S(1)}, u32[]{:S(2)}, u32[]{:S(2)}) collective-permute-start(bf16[256,256]{1,0:T(8,128)(2,1)S(1)} %shard_map.58.own_ref), channel_id=1, source_target_pairs={{0,1},{1,0},{2,3},{3,2},{4,5},{5,4},{6,7},{7,6},{8,9},{9,8},{10,11... | collective-permute-start | bytes 393224 | tf_op jit(solution)/shard_map/ppermute | solution.py:402
  23.7 21.7 %copy-start.1 = (s32[1,4]{1,0:T(1,128)S(1)}, s32[1,4]{1,0:T(1,128)}, u32[]{:S(2)}) copy-start(s32[1,4]{1,0:T(1,128)} %refs_0_.5) | copy-start | bytes 52
  23.7 6.4 %collective-permute-start.1 = (bf16[512,256]{1,0:T(8,128)(2,1)S(1)}, bf16[512,256]{1,0:T(8,128)(2,1)S(1)}, u32[]{:S(2)}, u32[]{:S(2)}) collective-permute-start(bf16[512,256]{1,0:T(8,128)(2,1)S(1)} %shard_map.59.refs_3_.refs_11_), channel_id=1, source_target_pairs={{0,2},{1,13},{2,4},{3,15},{4,6},{5,1},{6,8},{7,3},{8,10},{9,5},{10... | collective-permute-start | bytes 786440 | tf_op jit(solution)/shard_map/ppermute | solution.py:395
  30.1 6.4 %collective-permute-start.3 = (bf16[512,256]{1,0:T(8,128)(2,1)S(1)}, bf16[512,256]{1,0:T(8,128)(2,1)S(1)}, u32[]{:S(2)}, u32[]{:S(2)}) collective-permute-start(bf16[512,256]{1,0:T(8,128)(2,1)S(1)} %collective-permute-done.1.refs_4_.refs_10_), channel_id=1, source_target_pairs={{0,2},{1,15},{2,4},{3,1},{4,6},{5,3},{6,8},{7,5},{8,10},{9,7},{10,... | collective-permute-start | bytes 786440 | tf_op jit(solution)/shard_map/ppermute | solution.py:395
  31.1 8.9 %collective-permute-start.5 = (bf16[512,256]{1,0:T(8,128)(2,1)S(1)}, bf16[512,256]{1,0:T(8,128)(2,1)S(1)}, u32[]{:S(2)}, u32[]{:S(2)}) collective-permute-start(bf16[512,256]{1,0:T(8,128)(2,1)S(1)} %collective-permute-done.1.refs_4_.refs_10_), channel_id=1, source_target_pairs={{0,4},{1,13},{2,6},{3,15},{4,8},{5,1},{6,10},{7,3},{8,12},{9,5},{1... | collective-permute-start | bytes 786440 | tf_op jit(solution)/shard_map/ppermute | solution.py:395
  31.8 13.6 %collective-permute-start.2 = (bf16[512,256]{1,0:T(8,128)(2,1)S(1)}, bf16[512,256]{1,0:T(8,128)(2,1)S(1)}, u32[]{:S(2)}, u32[]{:S(2)}) collective-permute-start(bf16[512,256]{1,0:T(8,128)(2,1)S(1)} %collective-permute-done.1.refs_4_.refs_10_), channel_id=1, source_target_pairs={{0,1},{1,0},{2,3},{3,2},{4,5},{5,4},{6,7},{7,6},{8,9},{9,8},{10,11... | collective-permute-start | bytes 786440 | tf_op jit(solution)/shard_map/ppermute | solution.py:402
  36.5 13.8 %collective-permute-start.4 = (bf16[512,256]{1,0:T(8,128)(2,1)S(1)}, bf16[512,256]{1,0:T(8,128)(2,1)S(1)}, u32[]{:S(2)}, u32[]{:S(2)}) collective-permute-start(bf16[512,256]{1,0:T(8,128)(2,1)S(1)} %collective-permute-done.3.refs_5_.refs_7_), channel_id=1, source_target_pairs={{0,1},{1,0},{2,3},{3,2},{4,5},{5,4},{6,7},{7,6},{8,9},{9,8},{10,11... | collective-permute-start | bytes 786440 | tf_op jit(solution)/shard_map/ppermute | solution.py:402
  40.1 13.8 %collective-permute-start.6 = (bf16[512,256]{1,0:T(8,128)(2,1)S(1)}, bf16[512,256]{1,0:T(8,128)(2,1)S(1)}, u32[]{:S(2)}, u32[]{:S(2)}) collective-permute-start(bf16[512,256]{1,0:T(8,128)(2,1)S(1)} %collective-permute-done.5.refs_5_), channel_id=1, source_target_pairs={{0,1},{1,0},{2,3},{3,2},{4,5},{5,4},{6,7},{7,6},{8,9},{9,8},{10,11... | collective-permute-start | bytes 786440 | tf_op jit(solution)/shard_map/ppermute | solution.py:402

commit v5 on v4

--- a/solution.py
+++ b/solution.py
@@ -401,6 +401,7 @@
     def swap(x):
         return lax.ppermute(x, "ctx", [(c, c ^ 1) for c in range(n_ctx)])
 
+    other = swap(own)
     pair = pl.pallas_call(
         join_kernel,
         out_shape=jax.ShapeDtypeStruct((2 * n, kv_width), keyvals.dtype),
@@ -410,7 +411,7 @@
         cost_estimate=pl.CostEstimate(
             flops=0, bytes_accessed=8 * n * kv_width, transcendentals=0
         ),
-    )(own, swap(own))
+    )(own, other)
     hop1 = hop(pair, 1, 2)
     hop2 = hop(hop1, 1, 1)
     hop3 = hop(hop1, 2, 2)
@@ -437,8 +438,10 @@
 
     swapped1 = swap(hop1)
     early = [((0, 0), pair), ((1, 6), hop1), ((6, 1), swapped1)]
-    middle = [((2, 5), hop2), ((5, 2), swap(hop2))]
-    late = [((3, 4), hop3), ((4, 3), swap(hop3))]
+    swapped2 = swap(hop2)
+    swapped3 = swap(hop3)
+    middle = [((2, 5), hop2), ((5, 2), swapped2)]
+    late = [((3, 4), hop3), ((4, 3), swapped3)]
     q_all, acc, top, total = attend(
         early, 3, (picks, got_q), (query, sums, tops, totals), [], first=True
     )

time: 58.8 us -> 58.8 us (level)
  no operation moved by 1% of the time
where the time goes in v5:
time: 58.8 us; the launch traced here: 58.5 us
  starting transfers between devices  27.1 us (46%)
  Pallas kernels  17.7 us (30%)
  waiting for transfers between devices  13.5 us (23%)
    all_to_all x2, starting transfers between devices, exchange(): lax.all_to_all(rows.reshape(owners, capacity, rows.shape[1]), 'dp', split...  13 us
    pallas_call x3, Pallas kernels, attend(): pl.pallas_call(functools.partial(part_kernel, head, [f for f, _ in pieces...  12.9 us
    ppermute x4, starting transfers between devices, swap(): return lax.ppermute(x, 'ctx', [(c, c ^ 1) for c in range(n_ctx)])  11.3 us
    ppermute x3, waiting for transfers between devices, hop(): lax.ppermute(x, 'ctx', [(c, (c + (2 * up if c % 2 == 0 else -2 * down)) %...  7.71 us
    all_to_all x2, waiting for transfers between devices, exchange(): lax.all_to_all(rows.reshape(owners, capacity, rows.shape[1]), 'dp', split...  4.42 us
    pallas_call x2, Pallas kernels, pack(): pl.pallas_call(functools.partial(pack_kernel, owners, capacity), out_shap...  4.26 us
    ppermute x3, starting transfers between devices, hop(): lax.ppermute(x, 'ctx', [(c, (c + (2 * up if c % 2 == 0 else -2 * down)) %...  2.75 us
    ppermute x4, waiting for transfers between devices, swap(): return lax.ppermute(x, 'ctx', [(c, c ^ 1) for c in range(n_ctx)])  1.34 us
  transfers between devices with their start and end apart: 9, of which 5 were waited for; matrix products, arithmetic and copies ran while one was open for 0% of the time, Pallas kernels for 19%

profile of v5, /device:TPU:194, one launch (start us, length us, event | category | flops | bytes accessed | tf_op | source)
XLA Modules:
  0.0 58.5 jit_solution(6858451986916664410)
XLA Ops:
  0.0 1.9 %shard_map.57 = bf16[512,256]{1,0:T(8,128)(2,1)} custom-call(s32[1,256]{1,0:T(1,128)} %dest_hbm.3, bf16[256,256]{1,0:T(8,128)(2,1)} %bitcast.12), custom_call_target="tpu_custom_call" | custom-call | flops 67108864 | bytes 393216 | tf_op jit(solution)/shard_map/pallas_call | solution.py:342
  1.9 7.5 %all-to-all-start.1 = ((bf16[16,32,256]{2,1,0:T(8,128)(2,1)}), bf16[16,32,256]{2,1,0:T(8,128)(2,1)S(1)}, u32[]{:S(2)}, u32[]{:S(2)}) async-start(bf16[16,32,256]{2,1,0:T(8,128)(2,1)} %bitcast.10), calls=%async_computation.1 | async-start | bytes 524288 | tf_op jit(solution)/shard_map/all_to_all | solution.py:361
  9.4 2.4 %shard_map.56 = bf16[512,1024]{1,0:T(8,128)(2,1)} custom-call(s32[1,256]{1,0:T(1,128)} %dest_hbm.3, bf16[256,1024]{1,0:T(8,128)(2,1)} %bitcast.11), custom_call_target="tpu_custom_call" | custom-call | flops 268435456 | bytes 1572864 | tf_op jit(solution)/shard_map/pallas_call | solution.py:342
  11.8 4.4 %all-to-all-done.1 = bf16[16,32,256]{2,1,0:T(8,128)(2,1)S(1)} async-done(((bf16[16,32,256]{2,1,0:T(8,128)(2,1)}), bf16[16,32,256]{2,1,0:T(8,128)(2,1)S(1)}, u32[]{:S(2)}, u32[]{:S(2)}) %all-to-all-start.1) | async-done | bytes 262176 | tf_op jit(solution)/shard_map/all_to_all | solution.py:361
  16.2 0.0 copy-start
  16.2 5.5 %all-to-all-start = ((bf16[16,32,1024]{2,1,0:T(8,128)(2,1)}), bf16[16,32,1024]{2,1,0:T(8,128)(2,1)S(1)}, u32[]{:S(2)}, u32[]{:S(2)}) async-start(bf16[16,32,1024]{2,1,0:T(8,128)(2,1)} %bitcast.9), calls=%async_computation | async-start | bytes 2097152 | tf_op jit(solution)/shard_map/all_to_all | solution.py:361
  21.7 0.0 copy-done
  21.7 0.3 shard_map.55.picks_ref.refs_1_
  22.0 0.2 shard_map.58.own_ref
  22.2 0.1 collective-permute-start
  22.3 1.3 %collective-permute-done.other_ref = bf16[256,256]{1,0:T(8,128)(2,1)S(1)} collective-permute-done((bf16[256,256]{1,0:T(8,128)(2,1)S(1)}, bf16[256,256]{1,0:T(8,128)(2,1)S(1)}, u32[]{:S(2)}, u32[]{:S(2)}) %collective-permute-start) | collective-permute-done | bytes 131104 | tf_op jit(solution)/shard_map/ppermute | solution.py:402
  23.7 0.0 copy-start.1
  23.7 1.1 %collective-permute-start.1 = (bf16[512,256]{1,0:T(8,128)(2,1)S(1)}, bf16[512,256]{1,0:T(8,128)(2,1)S(1)}, u32[]{:S(2)}, u32[]{:S(2)}) collective-permute-start(bf16[512,256]{1,0:T(8,128)(2,1)S(1)} %shard_map.59.refs_3_.refs_11_), channel_id=1, source_target_pairs={{0,2},{1,13},{2,4},{3,15},{4,6},{5,1},{6,8},{7,3},{8,10},{9,5},{10... | collective-permute-start | bytes 786440 | tf_op jit(solution)/shard_map/ppermute | solution.py:395
  24.8 5.4 %collective-permute-done.1.refs_4_.refs_10_ = bf16[512,256]{1,0:T(8,128)(2,1)S(1)} collective-permute-done((bf16[512,256]{1,0:T(8,128)(2,1)S(1)}, bf16[512,256]{1,0:T(8,128)(2,1)S(1)}, u32[]{:S(2)}, u32[]{:S(2)}) %collective-permute-start.1) | collective-permute-done | bytes 262176 | tf_op jit(solution)/shard_map/ppermute | solution.py:395
  30.1 1.0 %collective-permute-start.3 = (bf16[512,256]{1,0:T(8,128)(2,1)S(1)}, bf16[512,256]{1,0:T(8,128)(2,1)S(1)}, u32[]{:S(2)}, u32[]{:S(2)}) collective-permute-start(bf16[512,256]{1,0:T(8,128)(2,1)S(1)} %collective-permute-done.1.refs_4_.refs_10_), channel_id=1, source_target_pairs={{0,2},{1,15},{2,4},{3,1},{4,6},{5,3},{6,8},{7,5},{8,10},{9,7},{10,... | collective-permute-start | bytes 786440 | tf_op jit(solution)/shard_map/ppermute | solution.py:395
  31.1 0.7 %collective-permute-start.5 = (bf16[512,256]{1,0:T(8,128)(2,1)S(1)}, bf16[512,256]{1,0:T(8,128)(2,1)S(1)}, u32[]{:S(2)}, u32[]{:S(2)}) collective-permute-start(bf16[512,256]{1,0:T(8,128)(2,1)S(1)} %collective-permute-done.1.refs_4_.refs_10_), channel_id=1, source_target_pairs={{0,4},{1,13},{2,6},{3,15},{4,8},{5,1},{6,10},{7,3},{8,12},{9,5},{1... | collective-permute-start | bytes 786440 | tf_op jit(solution)/shard_map/ppermute | solution.py:395
  31.8 2.6 %collective-permute-start.2 = (bf16[512,256]{1,0:T(8,128)(2,1)S(1)}, bf16[512,256]{1,0:T(8,128)(2,1)S(1)}, u32[]{:S(2)}, u32[]{:S(2)}) collective-permute-start(bf16[512,256]{1,0:T(8,128)(2,1)S(1)} %collective-permute-done.1.refs_4_.refs_10_), channel_id=1, source_target_pairs={{0,1},{1,0},{2,3},{3,2},{4,5},{5,4},{6,7},{7,6},{8,9},{9,8},{10,11... | collective-permute-start | bytes 786440 | tf_op jit(solution)/shard_map/ppermute | solution.py:402
  34.4 2.2 %collective-permute-done.3.refs_5_.refs_7_ = bf16[512,256]{1,0:T(8,128)(2,1)S(1)} collective-permute-done((bf16[512,256]{1,0:T(8,128)(2,1)S(1)}, bf16[512,256]{1,0:T(8,128)(2,1)S(1)}, u32[]{:S(2)}, u32[]{:S(2)}) %collective-permute-start.3) | collective-permute-done | bytes 262176 | tf_op jit(solution)/shard_map/ppermute | solution.py:395
  36.5 3.4 %collective-permute-start.4 = (bf16[512,256]{1,0:T(8,128)(2,1)S(1)}, bf16[512,256]{1,0:T(8,128)(2,1)S(1)}, u32[]{:S(2)}, u32[]{:S(2)}) collective-permute-start(bf16[512,256]{1,0:T(8,128)(2,1)S(1)} %collective-permute-done.3.refs_5_.refs_7_), channel_id=1, source_target_pairs={{0,1},{1,0},{2,3},{3,2},{4,5},{5,4},{6,7},{7,6},{8,9},{9,8},{10,11... | collective-permute-start | bytes 786440 | tf_op jit(solution)/shard_map/ppermute | solution.py:402
  39.9 0.2 collective-permute-done.5.refs_5_
  40.1 5.3 %collective-permute-start.6 = (bf16[512,256]{1,0:T(8,128)(2,1)S(1)}, bf16[512,256]{1,0:T(8,128)(2,1)S(1)}, u32[]{:S(2)}, u32[]{:S(2)}) collective-permute-start(bf16[512,256]{1,0:T(8,128)(2,1)S(1)} %collective-permute-done.5.refs_5_), channel_id=1, source_target_pairs={{0,1},{1,0},{2,3},{3,2},{4,5},{5,4},{6,7},{7,6},{8,9},{9,8},{10,11... | collective-permute-start | bytes 786440 | tf_op jit(solution)/shard_map/ppermute | solution.py:402
  45.4 0.0 collective-permute-done.2.refs_5_.refs_9_
  45.4 0.0 all-to-all-done
  45.4 0.0 copy-done.1
  45.4 4.9 %shard_map.60 = (bf16[256,2048]{1,0:T(8,128)(2,1)S(1)}, f32[8,128,256]{2,1,0:T(8,128)S(1)}, f32[8,1,256]{2,1,0:T(1,128)S(1)}, f32[8,8,256]{2,1,0:T(8,128)S(1)}) custom-call(s32[1,4]{1,0:T(1,128)S(1)} %copy-done.1, bf16[256,512]{1,0:T(8,128)(2,1)S(1)} %shard_map.55.picks_ref.refs_1_, bf16[512,1024]{1,0:T(8,128)(2,1)S(1)} %bitcast.7, ...), custom_call_target="tpu_custom_call" | custom-call | flops 1610612736 | bytes 2097152 | tf_op jit(solution)/shard_map/pallas_call | solution.py:425
  50.3 0.0 collective-permute-done.4.refs_6_.refs_8_
  50.3 3.6 %shard_map.61 = (f32[8,128,256]{2,1,0:T(8,128)S(1)}, f32[8,8,256]{2,1,0:T(8,128)S(1)}) custom-call(s32[1,4]{1,0:T(1,128)S(1)} %copy-done.1, bf16[256,2048]{1,0:T(8,128)(2,1)S(1)} %get-tuple-element.11.refs_1_, f32[8,128,256]{2,1,0:T(8,128)S(1)} %get-tuple-element.12.refs_2_, f32[8,1,256]{2,1,0:T(1,128)S(1)} %get-tuple-element.13.refs_3_, ...), custom_call_target="tpu_custom_call" | custom-call | flops 1073741824 | bytes 2097152 | tf_op jit(solution)/shard_map/pallas_call | solution.py:425
  53.9 0.0 collective-permute-done.6.refs_6_
  53.9 4.5 %shard_map.62 = bf16[256,1024]{1,0:T(8,128)(2,1)} custom-call(s32[1,4]{1,0:T(1,128)S(1)} %copy-done.1, bf16[256,2048]{1,0:T(8,128)(2,1)S(1)} %get-tuple-element.11.refs_1_, f32[8,128,256]{2,1,0:T(8,128)S(1)} %get-tuple-element.15.refs_2_, f32[8,1,256]{2,1,0:T(1,128)S(1)} %get-tuple-element.13.refs_3_, f32[8,8,256]{2,1,0:T(8,128)S(1)} %get-tuple-element.16.refs_4_, ...), custom_call_target="tpu_custom_call" | custom-call | flops 1073741824 | bytes 2097152 | tf_op jit(solution)/shard_map/pallas_call | solution.py:425
  (1 shorter events, 0.0 us)
Async XLA Ops:
  1.9 14.3 %all-to-all-start.1 = ((bf16[16,32,256]{2,1,0:T(8,128)(2,1)}), bf16[16,32,256]{2,1,0:T(8,128)(2,1)S(1)}, u32[]{:S(2)}, u32[]{:S(2)}) async-start(bf16[16,32,256]{2,1,0:T(8,128)(2,1)} %bitcast.10), calls=%async_computation.1 | async-start | bytes 524288 | tf_op jit(solution)/shard_map/all_to_all | solution.py:361
  16.2 5.5 %copy-start = (s32[1,256]{1,0:T(1,128)S(1)}, s32[1,256]{1,0:T(1,128)}, u32[]{:S(2)}) copy-start(s32[1,256]{1,0:T(1,128)} %source_ref.1) | copy-start | bytes 3076
  16.2 29.2 %all-to-all-start = ((bf16[16,32,1024]{2,1,0:T(8,128)(2,1)}), bf16[16,32,1024]{2,1,0:T(8,128)(2,1)S(1)}, u32[]{:S(2)}, u32[]{:S(2)}) async-start(bf16[16,32,1024]{2,1,0:T(8,128)(2,1)} %bitcast.9), calls=%async_computation | async-start | bytes 2097152 | tf_op jit(solution)/shard_map/all_to_all | solution.py:361
  22.2 1.4 %collective-permute-start = (bf16[256,256]{1,0:T(8,128)(2,1)S(1)}, bf16[256,256]{1,0:T(8,128)(2,1)S(1)}, u32[]{:S(2)}, u32[]{:S(2)}) collective-permute-start(bf16[256,256]{1,0:T(8,128)(2,1)S(1)} %shard_map.58.own_ref), channel_id=1, source_target_pairs={{0,1},{1,0},{2,3},{3,2},{4,5},{5,4},{6,7},{7,6},{8,9},{9,8},{10,11... | collective-permute-start | bytes 393224 | tf_op jit(solution)/shard_map/ppermute | solution.py:402
  23.7 21.7 %copy-start.1 = (s32[1,4]{1,0:T(1,128)S(1)}, s32[1,4]{1,0:T(1,128)}, u32[]{:S(2)}) copy-start(s32[1,4]{1,0:T(1,128)} %refs_0_.5) | copy-start | bytes 52
  23.7 6.4 %collective-permute-start.1 = (bf16[512,256]{1,0:T(8,128)(2,1)S(1)}, bf16[512,256]{1,0:T(8,128)(2,1)S(1)}, u32[]{:S(2)}, u32[]{:S(2)}) collective-permute-start(bf16[512,256]{1,0:T(8,128)(2,1)S(1)} %shard_map.59.refs_3_.refs_11_), channel_id=1, source_target_pairs={{0,2},{1,13},{2,4},{3,15},{4,6},{5,1},{6,8},{7,3},{8,10},{9,5},{10... | collective-permute-start | bytes 786440 | tf_op jit(solution)/shard_map/ppermute | solution.py:395
  30.1 6.4 %collective-permute-start.3 = (bf16[512,256]{1,0:T(8,128)(2,1)S(1)}, bf16[512,256]{1,0:T(8,128)(2,1)S(1)}, u32[]{:S(2)}, u32[]{:S(2)}) collective-permute-start(bf16[512,256]{1,0:T(8,128)(2,1)S(1)} %collective-permute-done.1.refs_4_.refs_10_), channel_id=1, source_target_pairs={{0,2},{1,15},{2,4},{3,1},{4,6},{5,3},{6,8},{7,5},{8,10},{9,7},{10,... | collective-permute-start | bytes 786440 | tf_op jit(solution)/shard_map/ppermute | solution.py:395
  31.1 8.9 %collective-permute-start.5 = (bf16[512,256]{1,0:T(8,128)(2,1)S(1)}, bf16[512,256]{1,0:T(8,128)(2,1)S(1)}, u32[]{:S(2)}, u32[]{:S(2)}) collective-permute-start(bf16[512,256]{1,0:T(8,128)(2,1)S(1)} %collective-permute-done.1.refs_4_.refs_10_), channel_id=1, source_target_pairs={{0,4},{1,13},{2,6},{3,15},{4,8},{5,1},{6,10},{7,3},{8,12},{9,5},{1... | collective-permute-start | bytes 786440 | tf_op jit(solution)/shard_map/ppermute | solution.py:395
  31.8 13.6 %collective-permute-start.2 = (bf16[512,256]{1,0:T(8,128)(2,1)S(1)}, bf16[512,256]{1,0:T(8,128)(2,1)S(1)}, u32[]{:S(2)}, u32[]{:S(2)}) collective-permute-start(bf16[512,256]{1,0:T(8,128)(2,1)S(1)} %collective-permute-done.1.refs_4_.refs_10_), channel_id=1, source_target_pairs={{0,1},{1,0},{2,3},{3,2},{4,5},{5,4},{6,7},{7,6},{8,9},{9,8},{10,11... | collective-permute-start | bytes 786440 | tf_op jit(solution)/shard_map/ppermute | solution.py:402
  36.5 13.8 %collective-permute-start.4 = (bf16[512,256]{1,0:T(8,128)(2,1)S(1)}, bf16[512,256]{1,0:T(8,128)(2,1)S(1)}, u32[]{:S(2)}, u32[]{:S(2)}) collective-permute-start(bf16[512,256]{1,0:T(8,128)(2,1)S(1)} %collective-permute-done.3.refs_5_.refs_7_), channel_id=1, source_target_pairs={{0,1},{1,0},{2,3},{3,2},{4,5},{5,4},{6,7},{7,6},{8,9},{9,8},{10,11... | collective-permute-start | bytes 786440 | tf_op jit(solution)/shard_map/ppermute | solution.py:402
  40.1 13.8 %collective-permute-start.6 = (bf16[512,256]{1,0:T(8,128)(2,1)S(1)}, bf16[512,256]{1,0:T(8,128)(2,1)S(1)}, u32[]{:S(2)}, u32[]{:S(2)}) collective-permute-start(bf16[512,256]{1,0:T(8,128)(2,1)S(1)} %collective-permute-done.5.refs_5_), channel_id=1, source_target_pairs={{0,1},{1,0},{2,3},{3,2},{4,5},{5,4},{6,7},{7,6},{8,9},{9,8},{10,11... | collective-permute-start | bytes 786440 | tf_op jit(solution)/shard_map/ppermute | solution.py:402

commit v6 on v5

--- a/solution.py
+++ b/solution.py
@@ -440,15 +440,17 @@
     early = [((0, 0), pair), ((1, 6), hop1), ((6, 1), swapped1)]
     swapped2 = swap(hop2)
     swapped3 = swap(hop3)
-    middle = [((2, 5), hop2), ((5, 2), swapped2)]
-    late = [((3, 4), hop3), ((4, 3), swapped3)]
+    middle = [((2, 5), hop2)]
+    later = [((5, 2), swapped2), ((3, 4), hop3)]
+    last = [((4, 3), swapped3)]
     q_all, acc, top, total = attend(
         early, 3, (picks, got_q), (query, sums, tops, totals), [], first=True
     )
-    acc, total = attend(middle, 2, (q_all, acc, top, total), (sums, totals), [])
+    acc, total = attend(middle, 1, (q_all, acc, top, total), (sums, totals), [])
+    acc, total = attend(later, 2, (q_all, acc, top, total), (sums, totals), [])
     attended = attend(
-        late + middle + early[::-1],
-        2,
+        last + later + middle + early[::-1],
+        1,
         (q_all, acc, top, total),
         jax.ShapeDtypeStruct((n, width), queries.dtype),
         [

time: 58.8 us -> 59.6 us (1.014)
  Pallas kernels: 17.7 us -> 18.5 us
    pallas_call x3 -> x4, Pallas kernels: 12.9 us -> 13.7 us  [attend(): pl.pallas_call(functools.partial(part_kernel, head, [f for f, _ in pieces...]
  transfers between devices with their start and end apart: 9 -> 9, of which waited for: 5 -> 5; matrix products, arithmetic and copies ran while one was open for 0% -> 0% of each run, Pallas kernels for 19% -> 23%
where the time goes in v6:
time: 59.6 us; the launch traced here: 59.3 us
  starting transfers between devices  27.1 us (45%)
  Pallas kernels  18.5 us (31%)
  waiting for transfers between devices  13.5 us (23%)
    pallas_call x4, Pallas kernels, attend(): pl.pallas_call(functools.partial(part_kernel, head, [f for f, _ in pieces...  13.7 us
    all_to_all x2, starting transfers between devices, exchange(): lax.all_to_all(rows.reshape(owners, capacity, rows.shape[1]), 'dp', split...  13 us
    ppermute x4, starting transfers between devices, swap(): return lax.ppermute(x, 'ctx', [(c, c ^ 1) for c in range(n_ctx)])  11.3 us
    ppermute x3, waiting for transfers between devices, hop(): lax.ppermute(x, 'ctx', [(c, (c + (2 * up if c % 2 == 0 else -2 * down)) %...  7.71 us
    all_to_all x2, waiting for transfers between devices, exchange(): lax.all_to_all(rows.reshape(owners, capacity, rows.shape[1]), 'dp', split...  4.42 us
    pallas_call x2, Pallas kernels, pack(): pl.pallas_call(functools.partial(pack_kernel, owners, capacity), out_shap...  4.26 us
    ppermute x3, starting transfers between devices, hop(): lax.ppermute(x, 'ctx', [(c, (c + (2 * up if c % 2 == 0 else -2 * down)) %...  2.75 us
    ppermute x4, waiting for transfers between devices, swap(): return lax.ppermute(x, 'ctx', [(c, c ^ 1) for c in range(n_ctx)])  1.34 us
  transfers between devices with their start and end apart: 9, of which 5 were waited for; matrix products, arithmetic and copies ran while one was open for 0% of the time, Pallas kernels for 23%

profile of v6, /device:TPU:194, one launch (start us, length us, event | category | flops | bytes accessed | tf_op | source)
XLA Modules:
  0.0 59.3 jit_solution(6122169647607964413)
XLA Ops:
  0.0 1.9 %shard_map.57 = bf16[512,256]{1,0:T(8,128)(2,1)} custom-call(s32[1,256]{1,0:T(1,128)} %dest_hbm.3, bf16[256,256]{1,0:T(8,128)(2,1)} %bitcast.12), custom_call_target="tpu_custom_call" | custom-call | flops 67108864 | bytes 393216 | tf_op jit(solution)/shard_map/pallas_call | solution.py:342
  1.9 7.5 %all-to-all-start.1 = ((bf16[16,32,256]{2,1,0:T(8,128)(2,1)}), bf16[16,32,256]{2,1,0:T(8,128)(2,1)S(1)}, u32[]{:S(2)}, u32[]{:S(2)}) async-start(bf16[16,32,256]{2,1,0:T(8,128)(2,1)} %bitcast.10), calls=%async_computation.1 | async-start | bytes 524288 | tf_op jit(solution)/shard_map/all_to_all | solution.py:361
  9.4 2.4 %shard_map.56 = bf16[512,1024]{1,0:T(8,128)(2,1)} custom-call(s32[1,256]{1,0:T(1,128)} %dest_hbm.3, bf16[256,1024]{1,0:T(8,128)(2,1)} %bitcast.11), custom_call_target="tpu_custom_call" | custom-call | flops 268435456 | bytes 1572864 | tf_op jit(solution)/shard_map/pallas_call | solution.py:342
  11.8 4.4 %all-to-all-done.1 = bf16[16,32,256]{2,1,0:T(8,128)(2,1)S(1)} async-done(((bf16[16,32,256]{2,1,0:T(8,128)(2,1)}), bf16[16,32,256]{2,1,0:T(8,128)(2,1)S(1)}, u32[]{:S(2)}, u32[]{:S(2)}) %all-to-all-start.1) | async-done | bytes 262176 | tf_op jit(solution)/shard_map/all_to_all | solution.py:361
  16.2 0.0 copy-start.1
  16.2 5.5 %all-to-all-start = ((bf16[16,32,1024]{2,1,0:T(8,128)(2,1)}), bf16[16,32,1024]{2,1,0:T(8,128)(2,1)S(1)}, u32[]{:S(2)}, u32[]{:S(2)}) async-start(bf16[16,32,1024]{2,1,0:T(8,128)(2,1)} %bitcast.9), calls=%async_computation | async-start | bytes 2097152 | tf_op jit(solution)/shard_map/all_to_all | solution.py:361
  21.7 0.0 copy-done.1
  21.7 0.3 shard_map.55.picks_ref.refs_1_
  22.0 0.2 shard_map.58.own_ref
  22.2 0.1 collective-permute-start
  22.3 1.3 %collective-permute-done.other_ref = bf16[256,256]{1,0:T(8,128)(2,1)S(1)} collective-permute-done((bf16[256,256]{1,0:T(8,128)(2,1)S(1)}, bf16[256,256]{1,0:T(8,128)(2,1)S(1)}, u32[]{:S(2)}, u32[]{:S(2)}) %collective-permute-start) | collective-permute-done | bytes 131104 | tf_op jit(solution)/shard_map/ppermute | solution.py:402
  23.7 0.0 copy-start
  23.7 1.1 %collective-permute-start.1 = (bf16[512,256]{1,0:T(8,128)(2,1)S(1)}, bf16[512,256]{1,0:T(8,128)(2,1)S(1)}, u32[]{:S(2)}, u32[]{:S(2)}) collective-permute-start(bf16[512,256]{1,0:T(8,128)(2,1)S(1)} %shard_map.59.refs_3_.refs_11_), channel_id=1, source_target_pairs={{0,2},{1,13},{2,4},{3,15},{4,6},{5,1},{6,8},{7,3},{8,10},{9,5},{10... | collective-permute-start | bytes 786440 | tf_op jit(solution)/shard_map/ppermute | solution.py:395
  24.8 5.4 %collective-permute-done.1.refs_4_.refs_10_ = bf16[512,256]{1,0:T(8,128)(2,1)S(1)} collective-permute-done((bf16[512,256]{1,0:T(8,128)(2,1)S(1)}, bf16[512,256]{1,0:T(8,128)(2,1)S(1)}, u32[]{:S(2)}, u32[]{:S(2)}) %collective-permute-start.1) | collective-permute-done | bytes 262176 | tf_op jit(solution)/shard_map/ppermute | solution.py:395
  30.1 1.0 %collective-permute-start.3 = (bf16[512,256]{1,0:T(8,128)(2,1)S(1)}, bf16[512,256]{1,0:T(8,128)(2,1)S(1)}, u32[]{:S(2)}, u32[]{:S(2)}) collective-permute-start(bf16[512,256]{1,0:T(8,128)(2,1)S(1)} %collective-permute-done.1.refs_4_.refs_10_), channel_id=1, source_target_pairs={{0,2},{1,15},{2,4},{3,1},{4,6},{5,3},{6,8},{7,5},{8,10},{9,7},{10,... | collective-permute-start | bytes 786440 | tf_op jit(solution)/shard_map/ppermute | solution.py:395
  31.1 0.7 %collective-permute-start.5 = (bf16[512,256]{1,0:T(8,128)(2,1)S(1)}, bf16[512,256]{1,0:T(8,128)(2,1)S(1)}, u32[]{:S(2)}, u32[]{:S(2)}) collective-permute-start(bf16[512,256]{1,0:T(8,128)(2,1)S(1)} %collective-permute-done.1.refs_4_.refs_10_), channel_id=1, source_target_pairs={{0,4},{1,13},{2,6},{3,15},{4,8},{5,1},{6,10},{7,3},{8,12},{9,5},{1... | collective-permute-start | bytes 786440 | tf_op jit(solution)/shard_map/ppermute | solution.py:395
  31.8 2.6 %collective-permute-start.2 = (bf16[512,256]{1,0:T(8,128)(2,1)S(1)}, bf16[512,256]{1,0:T(8,128)(2,1)S(1)}, u32[]{:S(2)}, u32[]{:S(2)}) collective-permute-start(bf16[512,256]{1,0:T(8,128)(2,1)S(1)} %collective-permute-done.1.refs_4_.refs_10_), channel_id=1, source_target_pairs={{0,1},{1,0},{2,3},{3,2},{4,5},{5,4},{6,7},{7,6},{8,9},{9,8},{10,11... | collective-permute-start | bytes 786440 | tf_op jit(solution)/shard_map/ppermute | solution.py:402
  34.4 2.2 %collective-permute-done.3.refs_5_.refs_8_ = bf16[512,256]{1,0:T(8,128)(2,1)S(1)} collective-permute-done((bf16[512,256]{1,0:T(8,128)(2,1)S(1)}, bf16[512,256]{1,0:T(8,128)(2,1)S(1)}, u32[]{:S(2)}, u32[]{:S(2)}) %collective-permute-start.3) | collective-permute-done | bytes 262176 | tf_op jit(solution)/shard_map/ppermute | solution.py:395
  36.5 3.4 %collective-permute-start.4 = (bf16[512,256]{1,0:T(8,128)(2,1)S(1)}, bf16[512,256]{1,0:T(8,128)(2,1)S(1)}, u32[]{:S(2)}, u32[]{:S(2)}) collective-permute-start(bf16[512,256]{1,0:T(8,128)(2,1)S(1)} %collective-permute-done.3.refs_5_.refs_8_), channel_id=1, source_target_pairs={{0,1},{1,0},{2,3},{3,2},{4,5},{5,4},{6,7},{7,6},{8,9},{9,8},{10,11... | collective-permute-start | bytes 786440 | tf_op jit(solution)/shard_map/ppermute | solution.py:402
  39.9 0.2 collective-permute-done.5.refs_6_.refs_7_
  40.1 5.3 %collective-permute-start.6 = (bf16[512,256]{1,0:T(8,128)(2,1)S(1)}, bf16[512,256]{1,0:T(8,128)(2,1)S(1)}, u32[]{:S(2)}, u32[]{:S(2)}) collective-permute-start(bf16[512,256]{1,0:T(8,128)(2,1)S(1)} %collective-permute-done.5.refs_6_.refs_7_), channel_id=1, source_target_pairs={{0,1},{1,0},{2,3},{3,2},{4,5},{5,4},{6,7},{7,6},{8,9},{9,8},{10,11... | collective-permute-start | bytes 786440 | tf_op jit(solution)/shard_map/ppermute | solution.py:402
  45.4 0.0 collective-permute-done.2.refs_5_.refs_9_
  45.4 0.0 all-to-all-done
  45.4 0.0 copy-done
  45.4 5.0 %shard_map.60 = (bf16[256,2048]{1,0:T(8,128)(2,1)S(1)}, f32[8,128,256]{2,1,0:T(8,128)S(1)}, f32[8,1,256]{2,1,0:T(1,128)S(1)}, f32[8,8,256]{2,1,0:T(8,128)S(1)}) custom-call(s32[1,4]{1,0:T(1,128)S(1)} %copy-done, bf16[256,512]{1,0:T(8,128)(2,1)S(1)} %shard_map.55.picks_ref.refs_1_, bf16[512,1024]{1,0:T(8,128)(2,1)S(1)} %bitcast.7, ...), custom_call_target="tpu_custom_call" | custom-call | flops 1610612736 | bytes 2097152 | tf_op jit(solution)/shard_map/pallas_call | solution.py:425
  50.4 2.2 %shard_map.61 = (f32[8,128,256]{2,1,0:T(8,128)S(1)}, f32[8,8,256]{2,1,0:T(8,128)S(1)}) custom-call(s32[1,4]{1,0:T(1,128)S(1)} %copy-done, bf16[256,2048]{1,0:T(8,128)(2,1)S(1)} %get-tuple-element.13.refs_1_, f32[8,128,256]{2,1,0:T(8,128)S(1)} %get-tuple-element.14.refs_2_, f32[8,1,256]{2,1,0:T(1,128)S(1)} %get-tuple-element.15.refs_3_, ...), custom_call_target="tpu_custom_call" | custom-call | flops 536870912 | bytes 2097152 | tf_op jit(solution)/shard_map/pallas_call | solution.py:425
  52.6 0.0 collective-permute-done.4.refs_5_.refs_6_
  52.6 3.4 %shard_map.62 = (f32[8,128,256]{2,1,0:T(8,128)S(1)}, f32[8,8,256]{2,1,0:T(8,128)S(1)}) custom-call(s32[1,4]{1,0:T(1,128)S(1)} %copy-done, bf16[256,2048]{1,0:T(8,128)(2,1)S(1)} %get-tuple-element.13.refs_1_, f32[8,128,256]{2,1,0:T(8,128)S(1)} %get-tuple-element.17.refs_2_, f32[8,1,256]{2,1,0:T(1,128)S(1)} %get-tuple-element.15.refs_3_, ...), custom_call_target="tpu_custom_call" | custom-call | flops 1073741824 | bytes 2097152 | tf_op jit(solution)/shard_map/pallas_call | solution.py:425
  56.0 0.0 collective-permute-done.6.refs_5_
  56.0 3.1 %shard_map.63 = bf16[256,1024]{1,0:T(8,128)(2,1)} custom-call(s32[1,4]{1,0:T(1,128)S(1)} %copy-done, bf16[256,2048]{1,0:T(8,128)(2,1)S(1)} %get-tuple-element.13.refs_1_, f32[8,128,256]{2,1,0:T(8,128)S(1)} %get-tuple-element.19.refs_2_, f32[8,1,256]{2,1,0:T(1,128)S(1)} %get-tuple-element.15.refs_3_, f32[8,8,256]{2,1,0:T(8,128)S(1)} %get-tuple-element.20.refs_4_, ...), custom_call_target="tpu_custom_call" | custom-call | flops 536870912 | bytes 2097152 | tf_op jit(solution)/shard_map/pallas_call | solution.py:425
  (1 shorter events, 0.0 us)
Async XLA Ops:
  1.9 14.3 %all-to-all-start.1 = ((bf16[16,32,256]{2,1,0:T(8,128)(2,1)}), bf16[16,32,256]{2,1,0:T(8,128)(2,1)S(1)}, u32[]{:S(2)}, u32[]{:S(2)}) async-start(bf16[16,32,256]{2,1,0:T(8,128)(2,1)} %bitcast.10), calls=%async_computation.1 | async-start | bytes 524288 | tf_op jit(solution)/shard_map/all_to_all | solution.py:361
  16.2 5.5 %copy-start.1 = (s32[1,256]{1,0:T(1,128)S(1)}, s32[1,256]{1,0:T(1,128)}, u32[]{:S(2)}) copy-start(s32[1,256]{1,0:T(1,128)} %source_ref.1) | copy-start | bytes 3076
  16.2 29.2 %all-to-all-start = ((bf16[16,32,1024]{2,1,0:T(8,128)(2,1)}), bf16[16,32,1024]{2,1,0:T(8,128)(2,1)S(1)}, u32[]{:S(2)}, u32[]{:S(2)}) async-start(bf16[16,32,1024]{2,1,0:T(8,128)(2,1)} %bitcast.9), calls=%async_computation | async-start | bytes 2097152 | tf_op jit(solution)/shard_map/all_to_all | solution.py:361
  22.2 1.4 %collective-permute-start = (bf16[256,256]{1,0:T(8,128)(2,1)S(1)}, bf16[256,256]{1,0:T(8,128)(2,1)S(1)}, u32[]{:S(2)}, u32[]{:S(2)}) collective-permute-start(bf16[256,256]{1,0:T(8,128)(2,1)S(1)} %shard_map.58.own_ref), channel_id=1, source_target_pairs={{0,1},{1,0},{2,3},{3,2},{4,5},{5,4},{6,7},{7,6},{8,9},{9,8},{10,11... | collective-permute-start | bytes 393224 | tf_op jit(solution)/shard_map/ppermute | solution.py:402
  23.7 21.7 %copy-start = (s32[1,4]{1,0:T(1,128)S(1)}, s32[1,4]{1,0:T(1,128)}, u32[]{:S(2)}) copy-start(s32[1,4]{1,0:T(1,128)} %refs_0_.7) | copy-start | bytes 52
  23.7 6.4 %collective-permute-start.1 = (bf16[512,256]{1,0:T(8,128)(2,1)S(1)}, bf16[512,256]{1,0:T(8,128)(2,1)S(1)}, u32[]{:S(2)}, u32[]{:S(2)}) collective-permute-start(bf16[512,256]{1,0:T(8,128)(2,1)S(1)} %shard_map.59.refs_3_.refs_11_), channel_id=1, source_target_pairs={{0,2},{1,13},{2,4},{3,15},{4,6},{5,1},{6,8},{7,3},{8,10},{9,5},{10... | collective-permute-start | bytes 786440 | tf_op jit(solution)/shard_map/ppermute | solution.py:395
  30.1 6.4 %collective-permute-start.3 = (bf16[512,256]{1,0:T(8,128)(2,1)S(1)}, bf16[512,256]{1,0:T(8,128)(2,1)S(1)}, u32[]{:S(2)}, u32[]{:S(2)}) collective-permute-start(bf16[512,256]{1,0:T(8,128)(2,1)S(1)} %collective-permute-done.1.refs_4_.refs_10_), channel_id=1, source_target_pairs={{0,2},{1,15},{2,4},{3,1},{4,6},{5,3},{6,8},{7,5},{8,10},{9,7},{10,... | collective-permute-start | bytes 786440 | tf_op jit(solution)/shard_map/ppermute | solution.py:395
  31.1 8.9 %collective-permute-start.5 = (bf16[512,256]{1,0:T(8,128)(2,1)S(1)}, bf16[512,256]{1,0:T(8,128)(2,1)S(1)}, u32[]{:S(2)}, u32[]{:S(2)}) collective-permute-start(bf16[512,256]{1,0:T(8,128)(2,1)S(1)} %collective-permute-done.1.refs_4_.refs_10_), channel_id=1, source_target_pairs={{0,4},{1,13},{2,6},{3,15},{4,8},{5,1},{6,10},{7,3},{8,12},{9,5},{1... | collective-permute-start | bytes 786440 | tf_op jit(solution)/shard_map/ppermute | solution.py:395
  31.8 13.6 %collective-permute-start.2 = (bf16[512,256]{1,0:T(8,128)(2,1)S(1)}, bf16[512,256]{1,0:T(8,128)(2,1)S(1)}, u32[]{:S(2)}, u32[]{:S(2)}) collective-permute-start(bf16[512,256]{1,0:T(8,128)(2,1)S(1)} %collective-permute-done.1.refs_4_.refs_10_), channel_id=1, source_target_pairs={{0,1},{1,0},{2,3},{3,2},{4,5},{5,4},{6,7},{7,6},{8,9},{9,8},{10,11... | collective-permute-start | bytes 786440 | tf_op jit(solution)/shard_map/ppermute | solution.py:402
  36.5 16.1 %collective-permute-start.4 = (bf16[512,256]{1,0:T(8,128)(2,1)S(1)}, bf16[512,256]{1,0:T(8,128)(2,1)S(1)}, u32[]{:S(2)}, u32[]{:S(2)}) collective-permute-start(bf16[512,256]{1,0:T(8,128)(2,1)S(1)} %collective-permute-done.3.refs_5_.refs_8_), channel_id=1, source_target_pairs={{0,1},{1,0},{2,3},{3,2},{4,5},{5,4},{6,7},{7,6},{8,9},{9,8},{10,11... | collective-permute-start | bytes 786440 | tf_op jit(solution)/shard_map/ppermute | solution.py:402
  40.1 16.0 %collective-permute-start.6 = (bf16[512,256]{1,0:T(8,128)(2,1)S(1)}, bf16[512,256]{1,0:T(8,128)(2,1)S(1)}, u32[]{:S(2)}, u32[]{:S(2)}) collective-permute-start(bf16[512,256]{1,0:T(8,128)(2,1)S(1)} %collective-permute-done.5.refs_6_.refs_7_), channel_id=1, source_target_pairs={{0,1},{1,0},{2,3},{3,2},{4,5},{5,4},{6,7},{7,6},{8,9},{9,8},{10,11... | collective-permute-start | bytes 786440 | tf_op jit(solution)/shard_map/ppermute | solution.py:402

commit v7 on v5

--- a/solution.py
+++ b/solution.py
@@ -264,10 +264,22 @@
         def _():
             block.step(0, chunk, block.own, True, "first")
 
+    def usable(i):
+        at = block.place(i)
+        return block.here(at) & block.clear(at)
+
+    pair = jnp.bool_(False)
+    if not first and len(names) == 2:
+        pair = usable(0) & usable(1)
+
+        @pl.when(pair)
+        def _():
+            block.step(0, 2 * chunk, 0, False, "fixed")
+
     @pl.loop(skip, len(names))
     def _(i):
         at = place(i, len(names))
-        is_here = block.here(at)
+        is_here = block.here(at) & jnp.logical_not(pair)
         is_clear = block.clear(at)
         is_late = block.late(at)
 

time: 58.8 us -> 58.8 us (level)
  no operation moved by 1% of the time
where the time goes in v7:
time: 58.8 us; the launch traced here: 58.5 us
  starting transfers between devices  27.1 us (46%)
  Pallas kernels  17.8 us (30%)
  waiting for transfers between devices  13.5 us (23%)
    all_to_all x2, starting transfers between devices, exchange(): lax.all_to_all(rows.reshape(owners, capacity, rows.shape[1]), 'dp', split...  13 us
    pallas_call x3, Pallas kernels, attend(): pl.pallas_call(functools.partial(part_kernel, head, [f for f, _ in pieces...  13 us
    ppermute x4, starting transfers between devices, swap(): return lax.ppermute(x, 'ctx', [(c, c ^ 1) for c in range(n_ctx)])  11.3 us
    ppermute x3, waiting for transfers between devices, hop(): lax.ppermute(x, 'ctx', [(c, (c + (2 * up if c % 2 == 0 else -2 * down)) %...  7.71 us
    all_to_all x2, waiting for transfers between devices, exchange(): lax.all_to_all(rows.reshape(owners, capacity, rows.shape[1]), 'dp', split...  4.42 us
    pallas_call x2, Pallas kernels, pack(): pl.pallas_call(functools.partial(pack_kernel, owners, capacity), out_shap...  4.26 us
    ppermute x3, starting transfers between devices, hop(): lax.ppermute(x, 'ctx', [(c, (c + (2 * up if c % 2 == 0 else -2 * down)) %...  2.75 us
    ppermute x4, waiting for transfers between devices, swap(): return lax.ppermute(x, 'ctx', [(c, c ^ 1) for c in range(n_ctx)])  1.34 us
  transfers between devices with their start and end apart: 9, of which 5 were waited for; matrix products, arithmetic and copies ran while one was open for 0% of the time, Pallas kernels for 19%

profile of v7, /device:TPU:194, one launch (start us, length us, event | category | flops | bytes accessed | tf_op | source)
XLA Modules:
  0.0 58.5 jit_solution(17819281730274142574)
XLA Ops:
  0.0 1.9 %shard_map.57 = bf16[512,256]{1,0:T(8,128)(2,1)} custom-call(s32[1,256]{1,0:T(1,128)} %dest_hbm.3, bf16[256,256]{1,0:T(8,128)(2,1)} %bitcast.12), custom_call_target="tpu_custom_call" | custom-call | flops 67108864 | bytes 393216 | tf_op jit(solution)/shard_map/pallas_call | solution.py:354
  1.9 7.5 %all-to-all-start.1 = ((bf16[16,32,256]{2,1,0:T(8,128)(2,1)}), bf16[16,32,256]{2,1,0:T(8,128)(2,1)S(1)}, u32[]{:S(2)}, u32[]{:S(2)}) async-start(bf16[16,32,256]{2,1,0:T(8,128)(2,1)} %bitcast.10), calls=%async_computation.1 | async-start | bytes 524288 | tf_op jit(solution)/shard_map/all_to_all | solution.py:373
  9.4 2.4 %shard_map.56 = bf16[512,1024]{1,0:T(8,128)(2,1)} custom-call(s32[1,256]{1,0:T(1,128)} %dest_hbm.3, bf16[256,1024]{1,0:T(8,128)(2,1)} %bitcast.11), custom_call_target="tpu_custom_call" | custom-call | flops 268435456 | bytes 1572864 | tf_op jit(solution)/shard_map/pallas_call | solution.py:354
  11.8 4.4 %all-to-all-done.1 = bf16[16,32,256]{2,1,0:T(8,128)(2,1)S(1)} async-done(((bf16[16,32,256]{2,1,0:T(8,128)(2,1)}), bf16[16,32,256]{2,1,0:T(8,128)(2,1)S(1)}, u32[]{:S(2)}, u32[]{:S(2)}) %all-to-all-start.1) | async-done | bytes 262176 | tf_op jit(solution)/shard_map/all_to_all | solution.py:373
  16.2 0.0 copy-start
  16.2 5.5 %all-to-all-start = ((bf16[16,32,1024]{2,1,0:T(8,128)(2,1)}), bf16[16,32,1024]{2,1,0:T(8,128)(2,1)S(1)}, u32[]{:S(2)}, u32[]{:S(2)}) async-start(bf16[16,32,1024]{2,1,0:T(8,128)(2,1)} %bitcast.9), calls=%async_computation | async-start | bytes 2097152 | tf_op jit(solution)/shard_map/all_to_all | solution.py:373
  21.7 0.0 copy-done
  21.7 0.3 shard_map.55.picks_ref.refs_1_
  22.0 0.2 shard_map.58.own_ref
  22.2 0.1 collective-permute-start
  22.3 1.3 %collective-permute-done.other_ref = bf16[256,256]{1,0:T(8,128)(2,1)S(1)} collective-permute-done((bf16[256,256]{1,0:T(8,128)(2,1)S(1)}, bf16[256,256]{1,0:T(8,128)(2,1)S(1)}, u32[]{:S(2)}, u32[]{:S(2)}) %collective-permute-start) | collective-permute-done | bytes 131104 | tf_op jit(solution)/shard_map/ppermute | solution.py:414
  23.7 0.0 copy-start.1
  23.7 1.1 %collective-permute-start.1 = (bf16[512,256]{1,0:T(8,128)(2,1)S(1)}, bf16[512,256]{1,0:T(8,128)(2,1)S(1)}, u32[]{:S(2)}, u32[]{:S(2)}) collective-permute-start(bf16[512,256]{1,0:T(8,128)(2,1)S(1)} %shard_map.59.refs_3_.refs_11_), channel_id=1, source_target_pairs={{0,2},{1,13},{2,4},{3,15},{4,6},{5,1},{6,8},{7,3},{8,10},{9,5},{10... | collective-permute-start | bytes 786440 | tf_op jit(solution)/shard_map/ppermute | solution.py:407
  24.8 5.4 %collective-permute-done.1.refs_4_.refs_10_ = bf16[512,256]{1,0:T(8,128)(2,1)S(1)} collective-permute-done((bf16[512,256]{1,0:T(8,128)(2,1)S(1)}, bf16[512,256]{1,0:T(8,128)(2,1)S(1)}, u32[]{:S(2)}, u32[]{:S(2)}) %collective-permute-start.1) | collective-permute-done | bytes 262176 | tf_op jit(solution)/shard_map/ppermute | solution.py:407
  30.1 1.0 %collective-permute-start.3 = (bf16[512,256]{1,0:T(8,128)(2,1)S(1)}, bf16[512,256]{1,0:T(8,128)(2,1)S(1)}, u32[]{:S(2)}, u32[]{:S(2)}) collective-permute-start(bf16[512,256]{1,0:T(8,128)(2,1)S(1)} %collective-permute-done.1.refs_4_.refs_10_), channel_id=1, source_target_pairs={{0,2},{1,15},{2,4},{3,1},{4,6},{5,3},{6,8},{7,5},{8,10},{9,7},{10,... | collective-permute-start | bytes 786440 | tf_op jit(solution)/shard_map/ppermute | solution.py:407
  31.1 0.7 %collective-permute-start.5 = (bf16[512,256]{1,0:T(8,128)(2,1)S(1)}, bf16[512,256]{1,0:T(8,128)(2,1)S(1)}, u32[]{:S(2)}, u32[]{:S(2)}) collective-permute-start(bf16[512,256]{1,0:T(8,128)(2,1)S(1)} %collective-permute-done.1.refs_4_.refs_10_), channel_id=1, source_target_pairs={{0,4},{1,13},{2,6},{3,15},{4,8},{5,1},{6,10},{7,3},{8,12},{9,5},{1... | collective-permute-start | bytes 786440 | tf_op jit(solution)/shard_map/ppermute | solution.py:407
  31.8 2.6 %collective-permute-start.2 = (bf16[512,256]{1,0:T(8,128)(2,1)S(1)}, bf16[512,256]{1,0:T(8,128)(2,1)S(1)}, u32[]{:S(2)}, u32[]{:S(2)}) collective-permute-start(bf16[512,256]{1,0:T(8,128)(2,1)S(1)} %collective-permute-done.1.refs_4_.refs_10_), channel_id=1, source_target_pairs={{0,1},{1,0},{2,3},{3,2},{4,5},{5,4},{6,7},{7,6},{8,9},{9,8},{10,11... | collective-permute-start | bytes 786440 | tf_op jit(solution)/shard_map/ppermute | solution.py:414
  34.4 2.2 %collective-permute-done.3.refs_5_.refs_7_ = bf16[512,256]{1,0:T(8,128)(2,1)S(1)} collective-permute-done((bf16[512,256]{1,0:T(8,128)(2,1)S(1)}, bf16[512,256]{1,0:T(8,128)(2,1)S(1)}, u32[]{:S(2)}, u32[]{:S(2)}) %collective-permute-start.3) | collective-permute-done | bytes 262176 | tf_op jit(solution)/shard_map/ppermute | solution.py:407
  36.5 3.4 %collective-permute-start.4 = (bf16[512,256]{1,0:T(8,128)(2,1)S(1)}, bf16[512,256]{1,0:T(8,128)(2,1)S(1)}, u32[]{:S(2)}, u32[]{:S(2)}) collective-permute-start(bf16[512,256]{1,0:T(8,128)(2,1)S(1)} %collective-permute-done.3.refs_5_.refs_7_), channel_id=1, source_target_pairs={{0,1},{1,0},{2,3},{3,2},{4,5},{5,4},{6,7},{7,6},{8,9},{9,8},{10,11... | collective-permute-start | bytes 786440 | tf_op jit(solution)/shard_map/ppermute | solution.py:414
  39.9 0.2 collective-permute-done.5.refs_5_
  40.1 5.3 %collective-permute-start.6 = (bf16[512,256]{1,0:T(8,128)(2,1)S(1)}, bf16[512,256]{1,0:T(8,128)(2,1)S(1)}, u32[]{:S(2)}, u32[]{:S(2)}) collective-permute-start(bf16[512,256]{1,0:T(8,128)(2,1)S(1)} %collective-permute-done.5.refs_5_), channel_id=1, source_target_pairs={{0,1},{1,0},{2,3},{3,2},{4,5},{5,4},{6,7},{7,6},{8,9},{9,8},{10,11... | collective-permute-start | bytes 786440 | tf_op jit(solution)/shard_map/ppermute | solution.py:414
  45.4 0.0 collective-permute-done.2.refs_5_.refs_9_
  45.4 0.0 all-to-all-done
  45.4 0.0 copy-done.1
  45.4 4.9 %shard_map.60 = (bf16[256,2048]{1,0:T(8,128)(2,1)S(1)}, f32[8,128,256]{2,1,0:T(8,128)S(1)}, f32[8,1,256]{2,1,0:T(1,128)S(1)}, f32[8,8,256]{2,1,0:T(8,128)S(1)}) custom-call(s32[1,4]{1,0:T(1,128)S(1)} %copy-done.1, bf16[256,512]{1,0:T(8,128)(2,1)S(1)} %shard_map.55.picks_ref.refs_1_, bf16[512,1024]{1,0:T(8,128)(2,1)S(1)} %bitcast.7, ...), custom_call_target="tpu_custom_call" | custom-call | flops 1610612736 | bytes 2097152 | tf_op jit(solution)/shard_map/pallas_call | solution.py:437
  50.3 0.0 collective-permute-done.4.refs_6_.refs_8_
  50.3 3.6 %shard_map.61 = (f32[8,128,256]{2,1,0:T(8,128)S(1)}, f32[8,8,256]{2,1,0:T(8,128)S(1)}) custom-call(s32[1,4]{1,0:T(1,128)S(1)} %copy-done.1, bf16[256,2048]{1,0:T(8,128)(2,1)S(1)} %get-tuple-element.11.refs_1_, f32[8,128,256]{2,1,0:T(8,128)S(1)} %get-tuple-element.12.refs_2_, f32[8,1,256]{2,1,0:T(1,128)S(1)} %get-tuple-element.13.refs_3_, ...), custom_call_target="tpu_custom_call" | custom-call | flops 1073741824 | bytes 2097152 | tf_op jit(solution)/shard_map/pallas_call | solution.py:437
  53.9 0.0 collective-permute-done.6.refs_6_
  53.9 4.5 %shard_map.62 = bf16[256,1024]{1,0:T(8,128)(2,1)} custom-call(s32[1,4]{1,0:T(1,128)S(1)} %copy-done.1, bf16[256,2048]{1,0:T(8,128)(2,1)S(1)} %get-tuple-element.11.refs_1_, f32[8,128,256]{2,1,0:T(8,128)S(1)} %get-tuple-element.15.refs_2_, f32[8,1,256]{2,1,0:T(1,128)S(1)} %get-tuple-element.13.refs_3_, f32[8,8,256]{2,1,0:T(8,128)S(1)} %get-tuple-element.16.refs_4_, ...), custom_call_target="tpu_custom_call" | custom-call | flops 1073741824 | bytes 2097152 | tf_op jit(solution)/shard_map/pallas_call | solution.py:437
  (1 shorter events, 0.0 us)
Async XLA Ops:
  1.9 14.3 %all-to-all-start.1 = ((bf16[16,32,256]{2,1,0:T(8,128)(2,1)}), bf16[16,32,256]{2,1,0:T(8,128)(2,1)S(1)}, u32[]{:S(2)}, u32[]{:S(2)}) async-start(bf16[16,32,256]{2,1,0:T(8,128)(2,1)} %bitcast.10), calls=%async_computation.1 | async-start | bytes 524288 | tf_op jit(solution)/shard_map/all_to_all | solution.py:373
  16.2 5.5 %copy-start = (s32[1,256]{1,0:T(1,128)S(1)}, s32[1,256]{1,0:T(1,128)}, u32[]{:S(2)}) copy-start(s32[1,256]{1,0:T(1,128)} %source_ref.1) | copy-start | bytes 3076
  16.2 29.2 %all-to-all-start = ((bf16[16,32,1024]{2,1,0:T(8,128)(2,1)}), bf16[16,32,1024]{2,1,0:T(8,128)(2,1)S(1)}, u32[]{:S(2)}, u32[]{:S(2)}) async-start(bf16[16,32,1024]{2,1,0:T(8,128)(2,1)} %bitcast.9), calls=%async_computation | async-start | bytes 2097152 | tf_op jit(solution)/shard_map/all_to_all | solution.py:373
  22.2 1.4 %collective-permute-start = (bf16[256,256]{1,0:T(8,128)(2,1)S(1)}, bf16[256,256]{1,0:T(8,128)(2,1)S(1)}, u32[]{:S(2)}, u32[]{:S(2)}) collective-permute-start(bf16[256,256]{1,0:T(8,128)(2,1)S(1)} %shard_map.58.own_ref), channel_id=1, source_target_pairs={{0,1},{1,0},{2,3},{3,2},{4,5},{5,4},{6,7},{7,6},{8,9},{9,8},{10,11... | collective-permute-start | bytes 393224 | tf_op jit(solution)/shard_map/ppermute | solution.py:414
  23.7 21.7 %copy-start.1 = (s32[1,4]{1,0:T(1,128)S(1)}, s32[1,4]{1,0:T(1,128)}, u32[]{:S(2)}) copy-start(s32[1,4]{1,0:T(1,128)} %refs_0_.5) | copy-start | bytes 52
  23.7 6.4 %collective-permute-start.1 = (bf16[512,256]{1,0:T(8,128)(2,1)S(1)}, bf16[512,256]{1,0:T(8,128)(2,1)S(1)}, u32[]{:S(2)}, u32[]{:S(2)}) collective-permute-start(bf16[512,256]{1,0:T(8,128)(2,1)S(1)} %shard_map.59.refs_3_.refs_11_), channel_id=1, source_target_pairs={{0,2},{1,13},{2,4},{3,15},{4,6},{5,1},{6,8},{7,3},{8,10},{9,5},{10... | collective-permute-start | bytes 786440 | tf_op jit(solution)/shard_map/ppermute | solution.py:407
  30.1 6.4 %collective-permute-start.3 = (bf16[512,256]{1,0:T(8,128)(2,1)S(1)}, bf16[512,256]{1,0:T(8,128)(2,1)S(1)}, u32[]{:S(2)}, u32[]{:S(2)}) collective-permute-start(bf16[512,256]{1,0:T(8,128)(2,1)S(1)} %collective-permute-done.1.refs_4_.refs_10_), channel_id=1, source_target_pairs={{0,2},{1,15},{2,4},{3,1},{4,6},{5,3},{6,8},{7,5},{8,10},{9,7},{10,... | collective-permute-start | bytes 786440 | tf_op jit(solution)/shard_map/ppermute | solution.py:407
  31.1 8.9 %collective-permute-start.5 = (bf16[512,256]{1,0:T(8,128)(2,1)S(1)}, bf16[512,256]{1,0:T(8,128)(2,1)S(1)}, u32[]{:S(2)}, u32[]{:S(2)}) collective-permute-start(bf16[512,256]{1,0:T(8,128)(2,1)S(1)} %collective-permute-done.1.refs_4_.refs_10_), channel_id=1, source_target_pairs={{0,4},{1,13},{2,6},{3,15},{4,8},{5,1},{6,10},{7,3},{8,12},{9,5},{1... | collective-permute-start | bytes 786440 | tf_op jit(solution)/shard_map/ppermute | solution.py:407
  31.8 13.6 %collective-permute-start.2 = (bf16[512,256]{1,0:T(8,128)(2,1)S(1)}, bf16[512,256]{1,0:T(8,128)(2,1)S(1)}, u32[]{:S(2)}, u32[]{:S(2)}) collective-permute-start(bf16[512,256]{1,0:T(8,128)(2,1)S(1)} %collective-permute-done.1.refs_4_.refs_10_), channel_id=1, source_target_pairs={{0,1},{1,0},{2,3},{3,2},{4,5},{5,4},{6,7},{7,6},{8,9},{9,8},{10,11... | collective-permute-start | bytes 786440 | tf_op jit(solution)/shard_map/ppermute | solution.py:414
  36.5 13.8 %collective-permute-start.4 = (bf16[512,256]{1,0:T(8,128)(2,1)S(1)}, bf16[512,256]{1,0:T(8,128)(2,1)S(1)}, u32[]{:S(2)}, u32[]{:S(2)}) collective-permute-start(bf16[512,256]{1,0:T(8,128)(2,1)S(1)} %collective-permute-done.3.refs_5_.refs_7_), channel_id=1, source_target_pairs={{0,1},{1,0},{2,3},{3,2},{4,5},{5,4},{6,7},{7,6},{8,9},{9,8},{10,11... | collective-permute-start | bytes 786440 | tf_op jit(solution)/shard_map/ppermute | solution.py:414
  40.1 13.8 %collective-permute-start.6 = (bf16[512,256]{1,0:T(8,128)(2,1)S(1)}, bf16[512,256]{1,0:T(8,128)(2,1)S(1)}, u32[]{:S(2)}, u32[]{:S(2)}) collective-permute-start(bf16[512,256]{1,0:T(8,128)(2,1)S(1)} %collective-permute-done.5.refs_5_), channel_id=1, source_target_pairs={{0,1},{1,0},{2,3},{3,2},{4,5},{5,4},{6,7},{7,6},{8,9},{9,8},{10,11... | collective-permute-start | bytes 786440 | tf_op jit(solution)/shard_map/ppermute | solution.py:414

commit v8 on v5

--- a/solution.py
+++ b/solution.py
@@ -13,15 +13,18 @@
 LOW = -1e30
 
 
-def slots_of(labels, owners, capacity):
+def earlier_of(n):
+    earlier = lax.broadcasted_iota(jnp.int32, (n, n), 0) < lax.broadcasted_iota(
+        jnp.int32, (n, n), 1
+    )
+    return jnp.where(earlier, 1.0, 0.0).astype(jnp.bfloat16)
+
+
+def slots_of(labels, earlier, owners, capacity):
     n = labels.shape[1]
     hot = lax.broadcasted_iota(jnp.int32, (owners, n), 0) == labels
     hot16 = jnp.where(hot, 1.0, 0.0).astype(jnp.bfloat16)
-    earlier = lax.broadcasted_iota(jnp.int32, (n, n), 0) < lax.broadcasted_iota(
-        jnp.int32, (n, n), 1
-    )
-    earlier16 = jnp.where(earlier, 1.0, 0.0).astype(jnp.bfloat16)
-    before = jnp.dot(hot16, earlier16, preferred_element_type=jnp.float32)
+    before = jnp.dot(hot16, earlier, preferred_element_type=jnp.float32)
     rank = jnp.sum(jnp.where(hot, before, 0.0), axis=0, keepdims=True)
     return labels * capacity + rank.astype(jnp.int32)
 
@@ -33,8 +36,9 @@
     fetch_rows = pltpu.make_async_copy(rows_hbm, rows, sems.at[1])
     fetch_dest.start()
     fetch_rows.start()
+    earlier = earlier_of(n)
     fetch_dest.wait()
-    slot = slots_of(dest[...], owners, capacity)
+    slot = slots_of(dest[...], earlier, owners, capacity)
     half = slots // 2
     hot = [
         half * i + lax.broadcasted_iota(jnp.int32, (half, n), 0) == slot for i in range(2)
@@ -56,8 +60,8 @@
 
 
 def picks_of(source_ref, owners, capacity):
-    slots = slots_of(source_ref[...], owners, capacity)
-    n = slots.shape[1]
+    n = source_ref.shape[1]
+    slots = slots_of(source_ref[...], earlier_of(n), owners, capacity)
     wide = jnp.broadcast_to(slots.astype(jnp.float32), (128, n))
     tall = jnp.transpose(wide).astype(jnp.int32)
     lane = lax.broadcasted_iota(jnp.int32, (n, 128), 1)
@@ -85,22 +89,6 @@
     out_ref[pl.ds(pl.multiple_of((1 - core) * n, n), n), :] = other_ref[...]
 
 
-def split_query(head, picks, got_ref, q_all):
-    groups = got_ref.shape[1] // head
-    for h in range(0, groups, 2):
-        both = jnp.dot(
-            picks, got_ref[:, h * head : (h + 2) * head], preferred_element_type=jnp.float32
-        ) * (LOG2E * head ** (-0.5))
-        for i in range(2):
-            exact = both[:, i * head : (i + 1) * head]
-            high = exact.astype(q_all.dtype)
-            at = 2 * (h + i) * head
-            q_all[:, at : at + head] = high
-            q_all[:, at + head : at + 2 * head] = (exact - high.astype(jnp.float32)).astype(
-                q_all.dtype
-            )
-
-
 class Block(typing.NamedTuple):
     core: jax.Array
     own: jax.Array
@@ -158,7 +146,7 @@
 
     def step(row, rows, position, masked, mode):
         row = pl.multiple_of(row, n)
-        keys = jnp.concatenate([kv[pl.ds(row, rows), :head]] * 2, axis=1)
+        keys = kv[pl.ds(row, rows), :head]
         values = jnp.transpose(kv[pl.ds(row, rows), head:])
         if masked:
             k_pos = position + lax.broadcasted_iota(jnp.int32, (rows, n), 0)
@@ -167,10 +155,10 @@
         def scores(h):
             s = lax.dot_general(
                 keys,
-                q_all[:, 2 * h * head : 2 * (h + 1) * head],
+                q_all[:, h * head : (h + 1) * head],
                 (((1,), (1,)), ((), ())),
                 preferred_element_type=jnp.float32,
-            )
+            ) * (LOG2E * head ** (-0.5))
             return jnp.where(visible, s, LOW) if masked else s
 
         def weigh(h, s):
@@ -222,7 +210,9 @@
         picks_ref, got_ref = refs[1:3]
         near = refs[3 : 3 + len(far)]
         q_all, acc, top, total, kv = refs[3 + len(far) :]
-        split_query(head, picks_ref[...], got_ref, q_all)
+        q_all[...] = jnp.dot(
+            picks_ref[...], got_ref[...], preferred_element_type=jnp.float32
+        ).astype(q_all.dtype)
     else:
         q_all, acc_ref, top_ref, total_ref = refs[1:5]
         near = refs[5 : 5 + len(far)]
@@ -416,7 +406,7 @@
     hop2 = hop(hop1, 1, 1)
     hop3 = hop(hop1, 2, 2)
     groups = width // head
-    query = jax.ShapeDtypeStruct((n, 2 * width), queries.dtype)
+    query = jax.ShapeDtypeStruct((n, width), queries.dtype)
     sums = jax.ShapeDtypeStruct((groups, head, n), jnp.float32)
     tops = jax.ShapeDtypeStruct((groups, 1, n), jnp.float32)
     totals = jax.ShapeDtypeStruct((groups, 8, n), jnp.float32)
@@ -440,8 +430,8 @@
     early = [((0, 0), pair), ((1, 6), hop1), ((6, 1), swapped1)]
     swapped2 = swap(hop2)
     swapped3 = swap(hop3)
-    middle = [((2, 5), hop2), ((5, 2), swapped2)]
-    late = [((3, 4), hop3), ((4, 3), swapped3)]
+    middle = [((3, 4), hop3), ((4, 3), swapped3)]
+    late = [((2, 5), hop2), ((5, 2), swapped2)]
     q_all, acc, top, total = attend(
         early, 3, (picks, got_q), (query, sums, tops, totals), [], first=True
     )

time: 58.8 us -> 59.9 us (1.019)
  the two profiles are of different devices: /device:TPU:194 before, /device:TPU:231 now
where the time goes in v8:
time: 59.9 us; the launch traced here: 59.6 us
  waiting for transfers between devices  23.1 us (39%)
  Pallas kernels  18.2 us (30%)
  starting transfers between devices  18.1 us (30%)
    ppermute x3, waiting for transfers between devices, hop(): lax.ppermute(x, 'ctx', [(c, (c + (2 * up if c % 2 == 0 else -2 * down)) %...  18.6 us
    pallas_call x3, Pallas kernels, attend(): pl.pallas_call(functools.partial(part_kernel, head, [f for f, _ in pieces...  13.4 us
    all_to_all x2, starting transfers between devices, exchange(): lax.all_to_all(rows.reshape(owners, capacity, rows.shape[1]), 'dp', split...  12.2 us
    pallas_call x2, Pallas kernels, pack(): pl.pallas_call(functools.partial(pack_kernel, owners, capacity), out_shap...  4.26 us
    all_to_all x2, waiting for transfers between devices, exchange(): lax.all_to_all(rows.reshape(owners, capacity, rows.shape[1]), 'dp', split...  3.45 us
    ppermute x3, starting transfers between devices, hop(): lax.ppermute(x, 'ctx', [(c, (c + (2 * up if c % 2 == 0 else -2 * down)) %...  3.4 us
    ppermute x4, starting transfers between devices, swap(): return lax.ppermute(x, 'ctx', [(c, c ^ 1) for c in range(n_ctx)])  2.42 us
  transfers between devices with their start and end apart: 9, of which 5 were waited for; matrix products, arithmetic and copies ran while one was open for 0% of the time, Pallas kernels for 20%

profile of v8, /device:TPU:231, one launch (start us, length us, event | category | flops | bytes accessed | tf_op | source)
XLA Modules:
  0.0 59.6 jit_solution(6777475854270234387)
XLA Ops:
  0.0 1.9 %shard_map.57 = bf16[512,256]{1,0:T(8,128)(2,1)} custom-call(s32[1,256]{1,0:T(1,128)} %dest_hbm.3, bf16[256,256]{1,0:T(8,128)(2,1)} %bitcast.12), custom_call_target="tpu_custom_call" | custom-call | flops 67108864 | bytes 393216 | tf_op jit(solution)/shard_map/pallas_call | solution.py:332
  1.9 6.9 %all-to-all-start.1 = ((bf16[16,32,256]{2,1,0:T(8,128)(2,1)}), bf16[16,32,256]{2,1,0:T(8,128)(2,1)S(1)}, u32[]{:S(2)}, u32[]{:S(2)}) async-start(bf16[16,32,256]{2,1,0:T(8,128)(2,1)} %bitcast.10), calls=%async_computation.1 | async-start | bytes 524288 | tf_op jit(solution)/shard_map/all_to_all | solution.py:351
  8.8 2.4 %shard_map.56 = bf16[512,1024]{1,0:T(8,128)(2,1)} custom-call(s32[1,256]{1,0:T(1,128)} %dest_hbm.3, bf16[256,1024]{1,0:T(8,128)(2,1)} %bitcast.11), custom_call_target="tpu_custom_call" | custom-call | flops 268435456 | bytes 1572864 | tf_op jit(solution)/shard_map/pallas_call | solution.py:332
  11.2 3.4 %all-to-all-done.1 = bf16[16,32,256]{2,1,0:T(8,128)(2,1)S(1)} async-done(((bf16[16,32,256]{2,1,0:T(8,128)(2,1)}), bf16[16,32,256]{2,1,0:T(8,128)(2,1)S(1)}, u32[]{:S(2)}, u32[]{:S(2)}) %all-to-all-start.1) | async-done | bytes 262176 | tf_op jit(solution)/shard_map/all_to_all | solution.py:351
  14.6 0.0 copy-start
  14.6 5.4 %all-to-all-start = ((bf16[16,32,1024]{2,1,0:T(8,128)(2,1)}), bf16[16,32,1024]{2,1,0:T(8,128)(2,1)S(1)}, u32[]{:S(2)}, u32[]{:S(2)}) async-start(bf16[16,32,1024]{2,1,0:T(8,128)(2,1)} %bitcast.9), calls=%async_computation | async-start | bytes 2097152 | tf_op jit(solution)/shard_map/all_to_all | solution.py:351
  20.0 0.0 copy-done
  20.0 0.3 shard_map.55.picks_ref.refs_1_
  20.3 0.2 shard_map.58.own_ref
  20.5 2.4 %collective-permute-start = (bf16[256,256]{1,0:T(8,128)(2,1)S(1)}, bf16[256,256]{1,0:T(8,128)(2,1)S(1)}, u32[]{:S(2)}, u32[]{:S(2)}) collective-permute-start(bf16[256,256]{1,0:T(8,128)(2,1)S(1)} %shard_map.58.own_ref), channel_id=1, source_target_pairs={{0,1},{1,0},{2,3},{3,2},{4,5},{5,4},{6,7},{7,6},{8,9},{9,8},{10,11... | collective-permute-start | bytes 393224 | tf_op jit(solution)/shard_map/ppermute | solution.py:392
  22.9 1.0 %collective-permute-done.other_ref = bf16[256,256]{1,0:T(8,128)(2,1)S(1)} collective-permute-done((bf16[256,256]{1,0:T(8,128)(2,1)S(1)}, bf16[256,256]{1,0:T(8,128)(2,1)S(1)}, u32[]{:S(2)}, u32[]{:S(2)}) %collective-permute-start) | collective-permute-done | bytes 131104 | tf_op jit(solution)/shard_map/ppermute | solution.py:392
  23.9 0.0 copy-start.1
  23.9 1.3 %collective-permute-start.1 = (bf16[512,256]{1,0:T(8,128)(2,1)S(1)}, bf16[512,256]{1,0:T(8,128)(2,1)S(1)}, u32[]{:S(2)}, u32[]{:S(2)}) collective-permute-start(bf16[512,256]{1,0:T(8,128)(2,1)S(1)} %shard_map.59.refs_3_.refs_11_), channel_id=1, source_target_pairs={{0,2},{1,13},{2,4},{3,15},{4,6},{5,1},{6,8},{7,3},{8,10},{9,5},{10... | collective-permute-start | bytes 786440 | tf_op jit(solution)/shard_map/ppermute | solution.py:385
  25.2 7.8 %collective-permute-done.1.refs_4_.refs_10_ = bf16[512,256]{1,0:T(8,128)(2,1)S(1)} collective-permute-done((bf16[512,256]{1,0:T(8,128)(2,1)S(1)}, bf16[512,256]{1,0:T(8,128)(2,1)S(1)}, u32[]{:S(2)}, u32[]{:S(2)}) %collective-permute-start.1) | collective-permute-done | bytes 262176 | tf_op jit(solution)/shard_map/ppermute | solution.py:385
  33.0 0.5 collective-permute-start.3
  33.5 1.7 %collective-permute-start.5 = (bf16[512,256]{1,0:T(8,128)(2,1)S(1)}, bf16[512,256]{1,0:T(8,128)(2,1)S(1)}, u32[]{:S(2)}, u32[]{:S(2)}) collective-permute-start(bf16[512,256]{1,0:T(8,128)(2,1)S(1)} %collective-permute-done.1.refs_4_.refs_10_), channel_id=1, source_target_pairs={{0,2},{1,15},{2,4},{3,1},{4,6},{5,3},{6,8},{7,5},{8,10},{9,7},{10,... | collective-permute-start | bytes 786440 | tf_op jit(solution)/shard_map/ppermute | solution.py:385
  35.1 0.0 collective-permute-start.2
  35.2 8.0 %collective-permute-done.3.refs_5_.refs_7_ = bf16[512,256]{1,0:T(8,128)(2,1)S(1)} collective-permute-done((bf16[512,256]{1,0:T(8,128)(2,1)S(1)}, bf16[512,256]{1,0:T(8,128)(2,1)S(1)}, u32[]{:S(2)}, u32[]{:S(2)}) %collective-permute-start.3) | collective-permute-done | bytes 262176 | tf_op jit(solution)/shard_map/ppermute | solution.py:385
  43.1 0.0 collective-permute-start.4
  43.1 2.9 %collective-permute-done.5.refs_5_ = bf16[512,256]{1,0:T(8,128)(2,1)S(1)} collective-permute-done((bf16[512,256]{1,0:T(8,128)(2,1)S(1)}, bf16[512,256]{1,0:T(8,128)(2,1)S(1)}, u32[]{:S(2)}, u32[]{:S(2)}) %collective-permute-start.5) | collective-permute-done | bytes 262176 | tf_op jit(solution)/shard_map/ppermute | solution.py:385
  46.0 0.0 collective-permute-start.6
  46.0 0.0 collective-permute-done.2.refs_5_.refs_9_
  46.0 0.0 all-to-all-done
  46.0 0.0 copy-done.1
  46.0 5.0 %shard_map.60 = (bf16[256,1024]{1,0:T(8,128)(2,1)S(1)}, f32[8,128,256]{2,1,0:T(8,128)S(1)}, f32[8,1,256]{2,1,0:T(1,128)S(1)}, f32[8,8,256]{2,1,0:T(8,128)S(1)}) custom-call(s32[1,4]{1,0:T(1,128)S(1)} %copy-done.1, bf16[256,512]{1,0:T(8,128)(2,1)S(1)} %shard_map.55.picks_ref.refs_1_, bf16[512,1024]{1,0:T(8,128)(2,1)S(1)} %bitcast.7, ...), custom_call_target="tpu_custom_call" | custom-call | flops 1610612736 | bytes 2097152 | tf_op jit(solution)/shard_map/pallas_call | solution.py:415
  51.1 0.0 collective-permute-done.4.refs_6_.refs_8_
  51.1 3.7 %shard_map.61 = (f32[8,128,256]{2,1,0:T(8,128)S(1)}, f32[8,8,256]{2,1,0:T(8,128)S(1)}) custom-call(s32[1,4]{1,0:T(1,128)S(1)} %copy-done.1, bf16[256,1024]{1,0:T(8,128)(2,1)S(1)} %get-tuple-element.11.refs_1_, f32[8,128,256]{2,1,0:T(8,128)S(1)} %get-tuple-element.12.refs_2_, f32[8,1,256]{2,1,0:T(1,128)S(1)} %get-tuple-element.13.refs_3_, ...), custom_call_target="tpu_custom_call" | custom-call | flops 1073741824 | bytes 2097152 | tf_op jit(solution)/shard_map/pallas_call | solution.py:415
  54.8 0.0 collective-permute-done.6.refs_6_
  54.8 4.7 %shard_map.62 = bf16[256,1024]{1,0:T(8,128)(2,1)} custom-call(s32[1,4]{1,0:T(1,128)S(1)} %copy-done.1, bf16[256,1024]{1,0:T(8,128)(2,1)S(1)} %get-tuple-element.11.refs_1_, f32[8,128,256]{2,1,0:T(8,128)S(1)} %get-tuple-element.15.refs_2_, f32[8,1,256]{2,1,0:T(1,128)S(1)} %get-tuple-element.13.refs_3_, f32[8,8,256]{2,1,0:T(8,128)S(1)} %get-tuple-element.16.refs_4_, ...), custom_call_target="tpu_custom_call" | custom-call | flops 1073741824 | bytes 2097152 | tf_op jit(solution)/shard_map/pallas_call | solution.py:415
  (1 shorter events, 0.0 us)
Async XLA Ops:
  1.9 12.7 %all-to-all-start.1 = ((bf16[16,32,256]{2,1,0:T(8,128)(2,1)}), bf16[16,32,256]{2,1,0:T(8,128)(2,1)S(1)}, u32[]{:S(2)}, u32[]{:S(2)}) async-start(bf16[16,32,256]{2,1,0:T(8,128)(2,1)} %bitcast.10), calls=%async_computation.1 | async-start | bytes 524288 | tf_op jit(solution)/shard_map/all_to_all | solution.py:351
  14.6 5.4 %copy-start = (s32[1,256]{1,0:T(1,128)S(1)}, s32[1,256]{1,0:T(1,128)}, u32[]{:S(2)}) copy-start(s32[1,256]{1,0:T(1,128)} %source_ref.1) | copy-start | bytes 3076
  14.6 31.4 %all-to-all-start = ((bf16[16,32,1024]{2,1,0:T(8,128)(2,1)}), bf16[16,32,1024]{2,1,0:T(8,128)(2,1)S(1)}, u32[]{:S(2)}, u32[]{:S(2)}) async-start(bf16[16,32,1024]{2,1,0:T(8,128)(2,1)} %bitcast.9), calls=%async_computation | async-start | bytes 2097152 | tf_op jit(solution)/shard_map/all_to_all | solution.py:351
  20.5 3.4 %collective-permute-start = (bf16[256,256]{1,0:T(8,128)(2,1)S(1)}, bf16[256,256]{1,0:T(8,128)(2,1)S(1)}, u32[]{:S(2)}, u32[]{:S(2)}) collective-permute-start(bf16[256,256]{1,0:T(8,128)(2,1)S(1)} %shard_map.58.own_ref), channel_id=1, source_target_pairs={{0,1},{1,0},{2,3},{3,2},{4,5},{5,4},{6,7},{7,6},{8,9},{9,8},{10,11... | collective-permute-start | bytes 393224 | tf_op jit(solution)/shard_map/ppermute | solution.py:392
  23.9 22.1 %copy-start.1 = (s32[1,4]{1,0:T(1,128)S(1)}, s32[1,4]{1,0:T(1,128)}, u32[]{:S(2)}) copy-start(s32[1,4]{1,0:T(1,128)} %refs_0_.5) | copy-start | bytes 52
  23.9 9.1 %collective-permute-start.1 = (bf16[512,256]{1,0:T(8,128)(2,1)S(1)}, bf16[512,256]{1,0:T(8,128)(2,1)S(1)}, u32[]{:S(2)}, u32[]{:S(2)}) collective-permute-start(bf16[512,256]{1,0:T(8,128)(2,1)S(1)} %shard_map.59.refs_3_.refs_11_), channel_id=1, source_target_pairs={{0,2},{1,13},{2,4},{3,15},{4,6},{5,1},{6,8},{7,3},{8,10},{9,5},{10... | collective-permute-start | bytes 786440 | tf_op jit(solution)/shard_map/ppermute | solution.py:385
  33.0 10.1 %collective-permute-start.3 = (bf16[512,256]{1,0:T(8,128)(2,1)S(1)}, bf16[512,256]{1,0:T(8,128)(2,1)S(1)}, u32[]{:S(2)}, u32[]{:S(2)}) collective-permute-start(bf16[512,256]{1,0:T(8,128)(2,1)S(1)} %collective-permute-done.1.refs_4_.refs_10_), channel_id=1, source_target_pairs={{0,4},{1,13},{2,6},{3,15},{4,8},{5,1},{6,10},{7,3},{8,12},{9,5},{1... | collective-permute-start | bytes 786440 | tf_op jit(solution)/shard_map/ppermute | solution.py:385
  33.5 12.5 %collective-permute-start.5 = (bf16[512,256]{1,0:T(8,128)(2,1)S(1)}, bf16[512,256]{1,0:T(8,128)(2,1)S(1)}, u32[]{:S(2)}, u32[]{:S(2)}) collective-permute-start(bf16[512,256]{1,0:T(8,128)(2,1)S(1)} %collective-permute-done.1.refs_4_.refs_10_), channel_id=1, source_target_pairs={{0,2},{1,15},{2,4},{3,1},{4,6},{5,3},{6,8},{7,5},{8,10},{9,7},{10,... | collective-permute-start | bytes 786440 | tf_op jit(solution)/shard_map/ppermute | solution.py:385
  35.1 10.9 %collective-permute-start.2 = (bf16[512,256]{1,0:T(8,128)(2,1)S(1)}, bf16[512,256]{1,0:T(8,128)(2,1)S(1)}, u32[]{:S(2)}, u32[]{:S(2)}) collective-permute-start(bf16[512,256]{1,0:T(8,128)(2,1)S(1)} %collective-permute-done.1.refs_4_.refs_10_), channel_id=1, source_target_pairs={{0,1},{1,0},{2,3},{3,2},{4,5},{5,4},{6,7},{7,6},{8,9},{9,8},{10,11... | collective-permute-start | bytes 786440 | tf_op jit(solution)/shard_map/ppermute | solution.py:392
  43.1 7.9 %collective-permute-start.4 = (bf16[512,256]{1,0:T(8,128)(2,1)S(1)}, bf16[512,256]{1,0:T(8,128)(2,1)S(1)}, u32[]{:S(2)}, u32[]{:S(2)}) collective-permute-start(bf16[512,256]{1,0:T(8,128)(2,1)S(1)} %collective-permute-done.3.refs_5_.refs_7_), channel_id=1, source_target_pairs={{0,1},{1,0},{2,3},{3,2},{4,5},{5,4},{6,7},{7,6},{8,9},{9,8},{10,11... | collective-permute-start | bytes 786440 | tf_op jit(solution)/shard_map/ppermute | solution.py:392
  46.0 8.8 %collective-permute-start.6 = (bf16[512,256]{1,0:T(8,128)(2,1)S(1)}, bf16[512,256]{1,0:T(8,128)(2,1)S(1)}, u32[]{:S(2)}, u32[]{:S(2)}) collective-permute-start(bf16[512,256]{1,0:T(8,128)(2,1)S(1)} %collective-permute-done.5.refs_5_), channel_id=1, source_target_pairs={{0,1},{1,0},{2,3},{3,2},{4,5},{5,4},{6,7},{7,6},{8,9},{9,8},{10,11... | collective-permute-start | bytes 786440 | tf_op jit(solution)/shard_map/ppermute | solution.py:392
